TPU v7x, 1024 devices: a whole 4x4x32 slice. The times are simulated.
1024 devices in a mesh: seq: 4 (over x), row: 8 (over y, core), col: 32 (over z).
Axes of the slice: x: 4, y: 4, z: 32, core: 2. Of those that a mesh axis runs over, the one named last changes fastest.
Arguments:
- inputs: bfloat16 [8, 32, 64, 4096], P('row', 'seq', None, 'col'), may hold values from -8 to 8
- query_proj: bfloat16 [8, 32, 64, 4096], P('row', 'seq', None, 'col'), may hold values from -5 to 5
- key_proj: bfloat16 [8, 32, 64, 4096], P('row', 'seq', None, 'col'), may hold values from -5 to 5
- value_proj: bfloat16 [8, 32, 64, 4096], P('row', 'seq', None, 'col'), may hold values from -6 to 6
- depth_weight: bfloat16 [7, 7, 4096], P(None, None, 'col'), may hold values from -1.25 to 1.25
- depth_bias: bfloat16 [4096], P('col'), may hold values from -3 to 3
- norm_gain: bfloat16 [4096], replicated, may hold values from 0.099609375 to 1.8984375
- norm_bias: bfloat16 [4096], replicated, may hold values from -3 to 3
- expand_weight: bfloat16 [4096, 16384], P(('seq', 'row'), 'col'), may hold values from -0.09375 to 0.09375
- expand_bias: bfloat16 [16384], P('col'), may hold values from -3 to 3
Outputs:
- residual_out: bfloat16 [8, 32, 64, 4096], P('row', 'seq', None, 'col')
- hidden: bfloat16 [8, 32, 64, 16384], P('row', 'seq', None, 'col')
All inputs are finite; a program needn't handle non-finite values.
Results may differ from a plain program's by a relative error of at most 0.0075.
Values may be sent and summed in bfloat16 or wider, within the bound.
No kernel may reach another device: no remote copies, remote signals or barrier semaphores. Data moves between devices by JAX's collectives and lax.ppermute only.
A program may use at most 32 MiB of HBM per device.

v0:
```python
import math

import jax
import jax.numpy as jnp
from jax import lax
from jax.sharding import PartitionSpec as P

HEAD_DIM = 128
KERNEL = 7


def padded_2(array, sides, width):
    for axis, dim in sides:
        peers, length = (lax.axis_size(axis), array.shape[dim])
        up = [(i, (i + 1) % peers) for i in range(peers - 1)]
        down = [(j, i) for i, j in up]
        last = lax.slice_in_dim(array, length - width, length, axis=dim)
        leading = lax.slice_in_dim(array, 0, width, axis=dim)
        before = lax.ppermute(last, axis, up)
        after = lax.ppermute(leading, axis, down)
        array = jnp.concatenate([before, array, after], axis=dim)
    return array


def on_device(
    inputs,
    query_proj,
    key_proj,
    value_proj,
    depth_weight,
    depth_bias,
    norm_gain,
    norm_bias,
    expand_weight,
    expand_bias,
):
    samples, rows_here, col_count, channels = inputs.shape
    heads_here = channels // HEAD_DIM
    positions = rows_here * col_count
    score_scale = 1.0 / math.sqrt(HEAD_DIM)
    queries = query_proj.reshape(samples, positions, heads_here, HEAD_DIM)
    start_max = jnp.full((samples, heads_here, positions), -1e30, jnp.float32)
    keys_in = lax.all_gather(key_proj, "seq", axis=1, tiled=True)
    values_in = lax.all_gather(value_proj, "seq", axis=1, tiled=True)
    count = keys_in.shape[1] * keys_in.shape[2]
    keys_in = keys_in.reshape(samples, count, heads_here, HEAD_DIM)
    values_in = values_in.reshape(samples, count, heads_here, HEAD_DIM)
    scores = (
        jnp.einsum("bqhd,bkhd->bhqk", queries, keys_in, preferred_element_type=jnp.float32)
        * score_scale
    )
    new_max = jnp.maximum(start_max, jnp.max(scores, axis=-1))
    weights = jnp.exp(scores - new_max[..., None])
    new_total = jnp.sum(weights, axis=-1)
    update = jnp.einsum(
        "bhqk,bkhd->bhqd",
        weights.astype(jnp.bfloat16),
        values_in,
        preferred_element_type=jnp.float32,
    )
    attended = update / new_total[..., None]
    attended = jnp.transpose(attended, (0, 2, 1, 3)).reshape(
        samples, rows_here, col_count, channels
    )
    residual_out = (inputs.astype(jnp.float32) + attended).astype(jnp.bfloat16)
    margin = KERNEL // 2
    padded = padded_2(residual_out, (("seq", 1),), margin)
    padded = jnp.pad(padded, ((0, 0), (0, 0), (margin, margin), (0, 0))).astype(jnp.float32)
    kernel_taps = depth_weight.astype(jnp.float32)
    convolved = jnp.zeros((samples, rows_here, col_count, channels), jnp.float32)
    for row_tap in range(KERNEL):
        for col_tap in range(KERNEL):
            convolved = (
                convolved
                + padded[:, row_tap : row_tap + rows_here, col_tap : col_tap + col_count, :]
                * kernel_taps[row_tap, col_tap]
            )
    convolved = (convolved + depth_bias.astype(jnp.float32)).astype(jnp.bfloat16)
    flat_rows = convolved.reshape(samples * positions, channels)
    gathered = lax.all_gather(flat_rows, "col", axis=1, tiled=True)
    widened = gathered.astype(jnp.float32)
    center = jnp.mean(widened, axis=1, keepdims=True)
    spread = jnp.mean((widened - center) * (widened - center), axis=1, keepdims=True)
    normed = (
        (widened - center) * lax.rsqrt(spread + 1e-06) * norm_gain.astype(jnp.float32)
        + norm_bias.astype(jnp.float32)
    ).astype(jnp.bfloat16)
    project = jnp.dot(
        normed,
        lax.all_gather(expand_weight, ("seq", "row"), axis=0, tiled=True),
        preferred_element_type=jnp.float32,
    )
    hidden = jax.nn.gelu(project + expand_bias.astype(jnp.float32), approximate=False).astype(
        jnp.bfloat16
    )
    return (residual_out, hidden.reshape(samples, rows_here, col_count, expand_weight.shape[1]))


def solution(mesh):
    return jax.shard_map(
        on_device,
        mesh=mesh,
        in_specs=(
            P("row", "seq", None, "col"),
            P("row", "seq", None, "col"),
            P("row", "seq", None, "col"),
            P("row", "seq", None, "col"),
            P(None, None, "col"),
            P("col"),
            P(),
            P(),
            P(("seq", "row"), "col"),
            P("col"),
        ),
        out_specs=(P("row", "seq", None, "col"), P("row", "seq", None, "col")),
        check_vma=False,
    )
```

profile of v0, /device:TPU:6, one launch (start us, length us, event | category | flops | bytes accessed | tf_op | source)
XLA Modules:
  0.0 304.7 jit_solution(933490023741050744)
XLA Ops:
  7.2 0.0 copy-start
  7.2 0.0 all-gather.3.cloned.1.call-start
  7.2 23.9 %all_gather.12 = bf16[1,32,64,128]{3,2,0,1:T(8,128)(2,1)S(1)} all-gather(bf16[1,8,64,128]{3,2,0,1:T(8,128)(2,1)} %bitcast.115), channel_id=1, replica_groups=mesh['seq'=4,'row'=8,'col'=32] {'seq'}, dimensions={1}, use_global_device_ids=true | all-gather | bytes 655360 | tf_op jit(solution)/shard_map/all_gather | solution.py:43
  31.1 0.8 multiply_reduce_fusion
  31.9 12.8 %all_gather.13 = bf16[1,32,64,128]{3,2,0,1:T(8,128)(2,1)S(1)} all-gather(bf16[1,8,64,128]{3,2,0,1:T(8,128)(2,1)S(1)} %bitcast.116), channel_id=1, replica_groups=mesh['seq'=4,'row'=8,'col'=32] {'seq'}, dimensions={1}, use_global_device_ids=true | all-gather | bytes 655360 | tf_op jit(solution)/shard_map/all_gather | solution.py:44
  44.7 0.8 fusion.12
  45.5 0.9 fusion.21
  46.4 0.0 copy-start.2
  46.5 1.3 collective-permute-start
  47.8 4.5 %collective-permute-start.1 = (bf16[1,3,64,128]{3,2,1,0:T(8,128)(2,1)S(1)}, bf16[1,3,64,128]{3,2,1,0:T(8,128)(2,1)S(1)}, u32[]{:S(2)}, u32[]{:S(2)}) collective-permute-start(bf16[1,3,64,128]{3,2,1,0:T(8,128)(2,1)S(1)} %get-tuple-element.3), channel_id=1, source_target_pairs={{256,0},{512,256},{768,512},{257,1},{513,257},{769,513},{258,2},{5... | collective-permute-start | bytes 147464 | tf_op jit(solution)/shard_map/ppermute | solution.py:20
  52.4 0.0 collective-permute-done
  52.5 1.6 collective-permute-done.1
  54.1 0.1 fusion.92
  54.1 0.0 copy-start.6
  54.2 2.1 fusion.42
  56.3 0.0 all-gather.3.cloned.1.call-update
  56.3 0.0 all-gather.5.cloned.1.call-start
  56.4 0.7 all-gather.5.cloned.1.call-update
  57.1 155.0 %all-gather.3.cloned.1.call-done = bf16[512,4096]{1,0:T(8,128)(2,1)} async-done(((bf16[512,128]{1,0:T(8,128)(2,1)}), bf16[512,4096]{1,0:T(8,128)(2,1)}) %all-gather.3.cloned.1.call-update) | async-done | bytes 4194320 | tf_op jit(solution)/shard_map/all_gather | solution.py:80
  212.2 3.0 convert_reduce_fusion
  215.1 0.5 copy-done.1
  215.6 1.2 fusion.2
  216.9 72.2 %all-gather.5.cloned.1.call-done = bf16[4096,512]{1,0:T(8,128)(2,1)} async-done(((bf16[128,512]{1,0:T(8,128)(2,1)}), bf16[4096,512]{1,0:T(8,128)(2,1)}) %all-gather.5.cloned.1.call-update) | async-done | bytes 4194320 | tf_op jit(solution)/shard_map/all_gather | solution.py:90
  289.0 8.8 %fusion.26 = bf16[512,512]{1,0:T(8,128)(2,1)} fusion(bf16[4096,512]{1,0:T(8,128)(2,1)} %all-gather.5.cloned.1.call-done, bf16[512,4096]{1,0:T(8,128)(2,1)} %all-gather.3.cloned.1.call-done, f32[4096]{0:T(1024)S(1)} %convert_element_type.51, f32[4096]{0:T(1024)S(1)} %convert_element_type.50, f32[512]{0:T(512)S(1)} %add_rsqrt_fusion, ...), kind=kOutput, calls=%fused_computation.25 | convolution fusion | flops 2177368064 | bytes 8951808 | tf_op jit(solution)/shard_map/dot_general | solution.py:88
  (29 shorter events, 0.2 us)
Async XLA Ops:
  7.2 24.0 %copy-start = (bf16[1,8,64,128]{3,2,1,0:T(8,128)(2,1)S(1)}, bf16[1,8,64,128]{3,2,1,0:T(8,128)(2,1)}, u32[]{:S(2)}) copy-start(bf16[1,8,64,128]{3,2,1,0:T(8,128)(2,1)} %param.11) | copy-start | bytes 393220
  7.2 24.7 %copy-start.3 = (bf16[1,8,64,128]{3,2,1,0:T(8,128)(2,1)S(1)}, bf16[1,8,64,128]{3,2,1,0:T(8,128)(2,1)}, u32[]{:S(2)}) copy-start(bf16[1,8,64,128]{3,2,1,0:T(8,128)(2,1)} %param.13) | copy-start | bytes 393220
  7.2 205.0 %all-gather.3.cloned.1.call-start = ((), (), s32[]{:S(2)}) async-start(), calls=%async_computation | async-start | bytes 4325376 | tf_op jit(solution)/shard_map/all_gather | solution.py:80
  44.7 1.7 copy-start.4
  44.7 7.6 %copy-start.5 = (bf16[7,7,128]{2,1,0:T(8,128)(2,1)S(1)}, bf16[7,7,128]{2,1,0:T(8,128)(2,1)}, u32[]{:S(2)}) copy-start(bf16[7,7,128]{2,1,0:T(8,128)(2,1)} %param.14) | copy-start | bytes 37636
  45.5 6.9 %copy-start.9 = (bf16[128]{0:T(256)(128)(2,1)S(1)}, bf16[128]{0:T(256)(128)(2,1)}, u32[]{:S(2)}) copy-start(bf16[128]{0:T(256)(128)(2,1)} %param.15) | copy-start | bytes 772
  46.4 9.8 %copy-start.2 = (bf16[1,8,64,128]{3,2,1,0:T(8,128)(2,1)}, bf16[1,8,64,128]{3,2,1,0:T(8,128)(2,1)S(1)}, u32[]{:S(2)}) copy-start(bf16[1,8,64,128]{3,2,1,0:T(8,128)(2,1)S(1)} %add_convert_fusion) | copy-start | bytes 393220
  46.5 6.0 %collective-permute-start = (bf16[1,3,64,128]{3,2,1,0:T(8,128)(2,1)S(1)}, bf16[1,3,64,128]{3,2,1,0:T(8,128)(2,1)S(1)}, u32[]{:S(2)}, u32[]{:S(2)}) collective-permute-start(bf16[1,3,64,128]{3,2,1,0:T(8,128)(2,1)S(1)} %get-tuple-element.2), channel_id=1, source_target_pairs={{0,256},{256,512},{512,768},{1,257},{257,513},{513,769},{2,258},{2... | collective-permute-start | bytes 147464 | tf_op jit(solution)/shard_map/ppermute | solution.py:19
  47.8 6.3 %collective-permute-start.1 = (bf16[1,3,64,128]{3,2,1,0:T(8,128)(2,1)S(1)}, bf16[1,3,64,128]{3,2,1,0:T(8,128)(2,1)S(1)}, u32[]{:S(2)}, u32[]{:S(2)}) collective-permute-start(bf16[1,3,64,128]{3,2,1,0:T(8,128)(2,1)S(1)} %get-tuple-element.3), channel_id=1, source_target_pairs={{256,0},{512,256},{768,512},{257,1},{513,257},{769,513},{258,2},{5... | collective-permute-start | bytes 147464 | tf_op jit(solution)/shard_map/ppermute | solution.py:20
  54.1 2.9 copy-start.6
  54.1 2.9 copy-start.7
  54.2 3.0 copy-start.8
  56.3 232.7 %all-gather.5.cloned.1.call-start = ((), (), s32[]{:S(2)}) async-start(), calls=%async_computation.1 | async-start | bytes 4325376 | tf_op jit(solution)/shard_map/all_gather | solution.py:90
  212.2 3.4 %copy-start.1 = (bf16[512,4096]{1,0:T(8,128)(2,1)S(1)}, bf16[512,4096]{1,0:T(8,128)(2,1)}, u32[]{:S(2)}) copy-start(bf16[512,4096]{1,0:T(8,128)(2,1)} %all-gather.3.cloned.1.call-done) | copy-start | bytes 12582916
Sparse Core Ops, SparseCore 0:
  56.4 155.6 all-gather.2
  216.5 72.5 all-gather.4
where the time goes:
time: 307 us; the launch traced here: 305 us
  waiting for transfers between devices  230 us (75%)
  blocking collectives  36.7 us (12%)
  between operations  14.3 us (5%)
  matrix products  10.4 us (3%)
  other arithmetic  7.26 us (2%)
  starting transfers between devices  5.92 us (2%)
    all_gather x1, waiting for transfers between devices, on_device(): gathered = lax.all_gather(flat_rows, 'col', axis=1, tiled=True)  155 us
    all_gather x1, waiting for transfers between devices, on_device(): lax.all_gather(expand_weight, ('seq', 'row'), axis=0, tiled=True)  72.2 us
    all_gather x1, blocking collectives, on_device(): keys_in = lax.all_gather(key_proj, 'seq', axis=1, tiled=True)  23.9 us
    all_gather x1, blocking collectives, on_device(): values_in = lax.all_gather(value_proj, 'seq', axis=1, tiled=True)  12.8 us
    dot_general x1, matrix products, on_device(): jnp.dot(normed, lax.all_gather(expand_weight, ('seq', 'row'), axis=0, til...  8.78 us
  transfers between devices with their start and end apart: 4, of which 3 were waited for; matrix products, arithmetic and copies ran while one was open for 1% of the time, Pallas kernels for 0%

commit v1 on v0

v1 whole, which is shorter than its diff:
```python
import functools
import math

import jax
import jax.numpy as jnp
from jax import lax
from jax.experimental import pallas as pl
from jax.experimental.pallas import tpu as pltpu
from jax.sharding import PartitionSpec as P

HEAD_DIM = 128
KERNEL = 7
MARGIN = KERNEL // 2
IMG_W = 64
ROWS = 8
POS = ROWS * IMG_W
EDGE = MARGIN * IMG_W
C = 4096
SEQ = 4
CLASSES = 8
LEFT = 8
F32 = jnp.float32
BF16 = jnp.bfloat16


def shift(array, axis, by):
    peers = lax.axis_size(axis)
    return lax.ppermute(array, axis, [(i, (i + by) % peers) for i in range(peers)])


def attend_kernel(place, q, k, v, x, above, below, far, taps, bias, res, conv, qs, xs, image):
    qs[0:EDGE] = above[2 * POS : 2 * POS + EDGE]
    qs[EDGE : EDGE + POS] = q[...]
    qs[EDGE + POS :] = below[2 * POS : 2 * POS + EDGE]
    xs[0:EDGE] = above[2 * POS + EDGE :]
    xs[EDGE : EDGE + POS] = x[...]
    xs[EDGE + POS :] = below[2 * POS + EDGE :]
    tall = ROWS + 2 * MARGIN
    blank = jnp.zeros((tall, 8, HEAD_DIM), F32)
    image[:, 0:LEFT, :] = blank
    image[:, LEFT + IMG_W : LEFT + IMG_W + 8, :] = blank
    keys = [k[...], above[0:POS], below[0:POS], far[0:POS]]
    values = [v[...], above[POS : 2 * POS], below[POS : 2 * POS], far[POS : 2 * POS]]
    to_log2 = math.log2(math.e) / math.sqrt(HEAD_DIM)
    tile = 2 * IMG_W
    for t in range(tall // 2):
        own = slice(t * tile, (t + 1) * tile)
        queries = qs[own]
        scores = [
            lax.dot_general(queries, key, (((1,), (1,)), ((), ())), preferred_element_type=F32)
            for key in keys
        ]
        peak = functools.reduce(jnp.maximum, scores)
        peak = jnp.max(peak, axis=1, keepdims=True)
        weights = [jnp.exp2((score - peak) * to_log2) for score in scores]
        total = jnp.sum(functools.reduce(jnp.add, weights), axis=1, keepdims=True)
        summed = functools.reduce(
            jnp.add,
            [
                jnp.dot(weight.astype(BF16), value, preferred_element_type=F32)
                for weight, value in zip(weights, values)
            ],
        )
        out = (xs[own].astype(F32) + summed / total).astype(BF16).astype(F32)
        image[2 * t : 2 * t + 2, LEFT : LEFT + IMG_W, :] = out.reshape(2, IMG_W, HEAD_DIM)

    @pl.when(place[0] == 0)
    def _():
        image[0:MARGIN] = jnp.zeros((MARGIN, IMG_W + 16, HEAD_DIM), F32)

    @pl.when(place[0] == SEQ - 1)
    def _():
        image[tall - MARGIN :] = jnp.zeros((MARGIN, IMG_W + 16, HEAD_DIM), F32)

    for i in range(ROWS):
        res[i * IMG_W : (i + 1) * IMG_W] = image[MARGIN + i, LEFT : LEFT + IMG_W, :].astype(BF16)
    wide = 16
    for c0 in range(0, IMG_W, wide):
        sums = [jnp.broadcast_to(bias[...], (wide, HEAD_DIM)) for _ in range(ROWS)]
        for b in range(KERNEL):
            start = LEFT - MARGIN + b + c0
            columns = [image[r, start : start + wide, :] for r in range(tall)]
            for a in range(KERNEL):
                tap = taps[a * KERNEL + b : a * KERNEL + b + 1, :]
                for i in range(ROWS):
                    sums[i] = sums[i] + columns[i + a] * tap
        for i in range(ROWS):
            conv[i * IMG_W + c0 : i * IMG_W + c0 + wide] = sums[i].astype(BF16)


def attend(place, q, k, v, x, above, below, far, taps, bias):
    out = jax.ShapeDtypeStruct((POS, HEAD_DIM), BF16)
    vmem = pl.BlockSpec(memory_space=pltpu.VMEM)
    flops = 4 * (POS + 2 * EDGE) * SEQ * POS * HEAD_DIM
    return pl.pallas_call(
        attend_kernel,
        out_shape=(out, out),
        in_specs=[pl.BlockSpec(memory_space=pltpu.SMEM)] + [vmem] * 9,
        out_specs=(vmem, vmem),
        scratch_shapes=[
            pltpu.VMEM((POS + 2 * EDGE, HEAD_DIM), BF16),
            pltpu.VMEM((POS + 2 * EDGE, HEAD_DIM), BF16),
            pltpu.VMEM((ROWS + 2 * MARGIN, IMG_W + 16, HEAD_DIM), F32),
        ],
        compiler_params=pltpu.CompilerParams(vmem_limit_bytes=32 << 20),
        cost_estimate=pl.CostEstimate(flops=flops, bytes_accessed=2 << 20, transcendentals=2 << 20),
        name="attend",
    )(place, q, k, v, x, above, below, far, taps, bias)


AUX = 16


def slab(weights, group):
    return jnp.concatenate([weights[j, group] for j in range(SEQ)], axis=0)


def add_stats(blocks, pivot, sum1, sum2, rows=64):
    for t in range(0, POS, rows):
        here = slice(t, t + rows)
        centre, one, two = pivot[here], sum1[here], sum2[here]
        for block in blocks:
            away = block[here].astype(F32) - centre
            one = one + away
            two = two + away * away
        sum1[here] = one
        sum2[here] = two


def first_kernel(place, *refs):
    parts, (weights, aux, acc, pivot, sum1, sum2) = refs[:7], refs[7:]
    lead = jnp.mean(parts[0][0].astype(F32), axis=1, keepdims=True)
    pivot[...] = jnp.broadcast_to(lead, (POS, HEAD_DIM))
    sum1[...] = jnp.zeros((POS, HEAD_DIM), F32)
    sum2[...] = jnp.zeros((POS, HEAD_DIM), F32)
    for n, (offset, part) in enumerate(zip((0, -1, 1, -2, 2, -3, 3), parts)):
        group = lax.rem(place[0] + offset + CLASSES, CLASSES)
        left = jnp.concatenate([part[j] for j in range(SEQ)], axis=1)
        left = jnp.concatenate([left, aux[group]], axis=0)
        product = jnp.dot(left, slab(weights, group), preferred_element_type=F32)
        if n == 0:
            acc[...] = product
        else:
            acc[...] += product
        add_stats([part.at[j] for j in range(SEQ)], pivot, sum1, sum2)


def first(place, parts, weights, aux):
    vmem = pl.BlockSpec(memory_space=pltpu.VMEM)
    hidden = weights.shape[-1]
    stat = jax.ShapeDtypeStruct((POS, HEAD_DIM), F32)
    return pl.pallas_call(
        first_kernel,
        out_shape=(jax.ShapeDtypeStruct((POS + AUX, hidden), F32), stat, stat, stat),
        in_specs=[pl.BlockSpec(memory_space=pltpu.SMEM)] + [vmem] * 9,
        out_specs=(vmem,) * 4,
        compiler_params=pltpu.CompilerParams(vmem_limit_bytes=40 << 20),
        cost_estimate=pl.CostEstimate(flops=2 << 30, bytes_accessed=9 << 20, transcendentals=0),
        name="first",
    )(place, *parts, weights, aux)


def last_kernel(place, acc, pivot, sum1, sum2, above, below, weights, aux, bias, out):
    group = lax.rem(place[0] + 4, CLASSES)
    blocks = [above.at[0], above.at[1], below.at[0], below.at[1]]
    left = jnp.concatenate([block[...] for block in blocks], axis=1)
    left = jnp.concatenate([left, aux[group]], axis=0)
    product = acc[...] + jnp.dot(left, slab(weights, group), preferred_element_type=F32)
    add_stats(blocks, pivot, sum1, sum2)
    mean1 = jnp.sum(sum1[...], axis=1, keepdims=True) * (1.0 / C)
    mean2 = jnp.sum(sum2[...], axis=1, keepdims=True) * (1.0 / C)
    centre = pivot[:, 0:1] + mean1
    spread = jnp.maximum(mean2 - mean1 * mean1, 0.0)
    scale = lax.rsqrt(spread + 1e-06)
    slope = product[POS : POS + 1]
    level = product[POS + 1 : POS + 2] + product[POS + 2 : POS + 3] + bias[...]
    project = scale * (product[0:POS] - centre * slope) + level
    out[...] = (0.5 * project * (1.0 + lax.erf(project * math.sqrt(0.5)))).astype(BF16)


def last(place, acc, stats, above, below, weights, aux, bias):
    vmem = pl.BlockSpec(memory_space=pltpu.VMEM)
    hidden = weights.shape[-1]
    return pl.pallas_call(
        last_kernel,
        out_shape=jax.ShapeDtypeStruct((POS, hidden), BF16),
        in_specs=[pl.BlockSpec(memory_space=pltpu.SMEM)] + [vmem] * 9,
        out_specs=vmem,
        compiler_params=pltpu.CompilerParams(vmem_limit_bytes=40 << 20),
        cost_estimate=pl.CostEstimate(flops=1 << 29, bytes_accessed=7 << 20, transcendentals=1 << 18),
        name="last",
    )(place, acc, *stats, above, below, weights, aux, bias)


def on_device(
    inputs,
    query_proj,
    key_proj,
    value_proj,
    depth_weight,
    depth_bias,
    norm_gain,
    norm_bias,
    expand_weight,
    expand_bias,
):
    seq, row, col = (lax.axis_index(axis) for axis in ("seq", "row", "col"))
    depth, hidden = expand_weight.shape
    gain, offset = norm_gain.astype(F32), norm_bias.astype(F32)
    my_gain = lax.dynamic_slice(gain, ((seq * CLASSES + row) * depth,), (depth,))
    scaled = (expand_weight.astype(F32) * my_gain[:, None]).astype(BF16)
    weights = lax.all_gather(scaled, ("seq", "row"), axis=0, tiled=True)
    weights = weights.reshape(SEQ, CLASSES, depth, hidden)
    ratio = offset / gain
    high = lax.reduce_precision(ratio, 8, 7)
    aux = jnp.stack([jnp.ones_like(ratio), high, ratio - high] + [jnp.zeros_like(ratio)] * (AUX - 3))
    aux = aux.astype(BF16).reshape(AUX, SEQ, CLASSES, depth)
    aux = jnp.transpose(aux, (2, 0, 1, 3)).reshape(CLASSES, AUX, SEQ * depth)

    x, q, k, v = (a.reshape(POS, HEAD_DIM) for a in (inputs, query_proj, key_proj, value_proj))
    both = jnp.concatenate([k, v])
    far = shift(both, "seq", 2)
    above = shift(jnp.concatenate([k, v, q[POS - EDGE :], x[POS - EDGE :]]), "seq", 1)
    below = shift(jnp.concatenate([k, v, q[:EDGE], x[:EDGE]]), "seq", -1)
    taps = depth_weight.astype(F32).reshape(KERNEL * KERNEL, HEAD_DIM)
    bias = depth_bias.astype(F32).reshape(1, HEAD_DIM)
    residual, convolved = attend(
        seq.astype(jnp.int32).reshape(1), q, k, v, x, above, below, far, taps, bias
    )

    strides = [[i + CLASSES * j for j in range(SEQ)] for i in range(CLASSES)]
    own = lax.all_gather(convolved, "col", axis=0, tiled=True, axis_index_groups=strides)
    own = own.reshape(SEQ, POS, HEAD_DIM)
    parts, up, down = [own], own, own
    for _ in range(3):
        up, down = shift(up, "col", 1), shift(down, "col", -1)
        parts += [up, down]
    up, down = shift(up[:2], "col", 1), shift(down[2:], "col", -1)
    place = col.astype(jnp.int32).reshape(1)
    acc, *stats = first(place, parts, weights, aux)
    out = last(
        place, acc, stats, up, down, weights, aux, expand_bias.astype(F32).reshape(1, hidden)
    )
    return (
        residual.reshape(inputs.shape),
        out.reshape(inputs.shape[:3] + (hidden,)),
    )


def solution(mesh):
    return jax.shard_map(
        on_device,
        mesh=mesh,
        in_specs=(
            P("row", "seq", None, "col"),
            P("row", "seq", None, "col"),
            P("row", "seq", None, "col"),
            P("row", "seq", None, "col"),
            P(None, None, "col"),
            P("col"),
            P(),
            P(),
            P(("seq", "row"), "col"),
            P("col"),
        ),
        out_specs=(P("row", "seq", None, "col"), P("row", "seq", None, "col")),
        check_vma=False,
    )
```

time: 307 us -> 176 us (0.57)
  waiting for transfers between devices: 230 us -> 29.6 us
  starting transfers between devices: 5.92 us -> 48.5 us
  blocking collectives: 36.7 us -> 53.3 us
  Pallas kernels: 0 us -> 11.7 us
  local copies, waits for them, and re-layouts: 0.57 us -> 12.1 us
  matrix products: 10.4 us -> 0 us
    all_gather x2 -> x1, waiting for transfers between devices: 227 us -> 0.02 us  [on_device(): weights = lax.all_gather(scaled, ('seq', 'row'), axis=0, tiled=True)]
    ppermute x2 -> x11, starting transfers between devices: 5.84 us -> 48.5 us  [shift(): lax.ppermute(array, axis, [(i, (i + by) % peers) for i in range(peers)])]
    ppermute x2 -> x11, waiting for transfers between devices: 1.63 us -> 29.6 us  [shift(): lax.ppermute(array, axis, [(i, (i + by) % peers) for i in range(peers)])]
    all_gather x2 -> x1, blocking collectives: 36.7 us -> 53.3 us  [on_device(): lax.all_gather(convolved, 'col', axis=0, tiled=True, axis_index_groups=st...]
    pallas_call x0 -> x3, Pallas kernels: none -> 11.7 us  [the longest x1 4.53 us: attend(): pl.pallas_call(attend_kernel, out_shape=(out, out), in_specs=[pl.BlockSpe...]
    dot_general x3 -> x0, matrix products: 10.4 us -> none  [the longest x1 8.78 us: on_device(): jnp.dot(normed, lax.all_gather(expand_weight, ('seq', 'row'), axis=0, til...]
    unnamed x20 -> x25, local copies, waits for them, and re-layouts: 0.53 us -> 6.52 us
    reduce_sum x3 -> x0, other arithmetic: 5 us -> none  [the longest x1 2.96 us: on_device(): center = jnp.mean(widened, axis=1, keepdims=True)]
  transfers between devices with their start and end apart: 4 -> 12, of which waited for: 3 -> 5; matrix products, arithmetic and copies ran while one was open for 1% -> 4% of each run, Pallas kernels for 0% -> 5%
where the time goes in v1:
time: 176 us; the launch traced here: 174 us
  blocking collectives  53.3 us (30%)
  starting transfers between devices  48.5 us (28%)
  waiting for transfers between devices  29.6 us (17%)
  between operations  14.3 us (8%)
  local copies, waits for them, and re-layouts  12.1 us (7%)
  Pallas kernels  11.7 us (7%)
  other arithmetic  4.35 us (2%)
    all_gather x1, blocking collectives, on_device(): lax.all_gather(convolved, 'col', axis=0, tiled=True, axis_index_groups=st...  53.3 us
    ppermute x11, starting transfers between devices, shift(): lax.ppermute(array, axis, [(i, (i + by) % peers) for i in range(peers)])  48.5 us
    ppermute x11, waiting for transfers between devices, shift(): lax.ppermute(array, axis, [(i, (i + by) % peers) for i in range(peers)])  29.6 us
    unnamed x25, local copies, waits for them, and re-layouts  6.52 us
    pallas_call x1, Pallas kernels, attend(): pl.pallas_call(attend_kernel, out_shape=(out, out), in_specs=[pl.BlockSpe...  4.53 us
    pallas_call x1, Pallas kernels, first(): pl.pallas_call(first_kernel, out_shape=(jax.ShapeDtypeStruct((POS + AUX,...  4.24 us
  transfers between devices with their start and end apart: 12, of which 5 were waited for; matrix products, arithmetic and copies ran while one was open for 4% of the time, Pallas kernels for 5%

profile of v1, /device:TPU:6, one launch (start us, length us, event | category | flops | bytes accessed | tf_op | source)
XLA Modules:
  0.0 173.9 jit_solution(512102085081387498)
XLA Ops:
  8.0 1.6 multiply_convert_fusion
  11.3 1.0 pad_maximum_fusion.2
  12.4 15.0 %collective-permute-start = (bf16[1408,128]{1,0:T(8,128)(2,1)S(1)}, bf16[1408,128]{1,0:T(8,128)(2,1)S(1)}, u32[]{:S(2)}, u32[]{:S(2)}) collective-permute-start(bf16[1408,128]{1,0:T(8,128)(2,1)S(1)} %get-tuple-element.15), channel_id=1, source_target_pairs={{0,256},{256,512},{512,768},{768,0},{1,257},{257,513},{513,769},{7... | collective-permute-start | bytes 1081352 | tf_op jit(solution)/shard_map/ppermute | solution.py:28
  27.4 1.9 %collective-permute-start.1 = (bf16[1408,128]{1,0:T(8,128)(2,1)S(1)}, bf16[1408,128]{1,0:T(8,128)(2,1)S(1)}, u32[]{:S(2)}, u32[]{:S(2)}) collective-permute-start(bf16[1408,128]{1,0:T(8,128)(2,1)S(1)} %get-tuple-element.14), channel_id=1, source_target_pairs={{0,768},{256,0},{512,256},{768,512},{1,769},{257,1},{513,257},{769... | collective-permute-start | bytes 1081352 | tf_op jit(solution)/shard_map/ppermute | solution.py:28
  29.4 1.0 pad_maximum_fusion.3
  30.3 3.4 %collective-permute-start.2 = (bf16[1024,128]{1,0:T(8,128)(2,1)S(1)}, bf16[1024,128]{1,0:T(8,128)(2,1)S(1)}, u32[]{:S(2)}, u32[]{:S(2)}) collective-permute-start(bf16[1024,128]{1,0:T(8,128)(2,1)S(1)} %pad_maximum_fusion.3), channel_id=1, source_target_pairs={{0,512},{256,768},{512,0},{768,256},{1,513},{257,769},{513,1},{769... | collective-permute-start | bytes 786440 | tf_op jit(solution)/shard_map/ppermute | solution.py:28
  35.1 5.1 %collective-permute-done.2.far = bf16[1024,128]{1,0:T(8,128)(2,1)S(1)} collective-permute-done((bf16[1024,128]{1,0:T(8,128)(2,1)S(1)}, bf16[1024,128]{1,0:T(8,128)(2,1)S(1)}, u32[]{:S(2)}, u32[]{:S(2)}) %collective-permute-start.2) | collective-permute-done | bytes 262176 | tf_op jit(solution)/shard_map/ppermute | solution.py:28
  44.4 4.5 %attend.1 = (bf16[512,128]{1,0:T(8,128)(2,1)}, bf16[512,128]{1,0:T(8,128)(2,1)S(1)}) custom-call(s32[1]{0:T(128)} %bitcast.place, bf16[512,128]{1,0:T(8,128)(2,1)S(1)} %bitcast.34, bf16[512,128]{1,0:T(8,128)(2,1)S(1)} %bitcast.30, bf16[512,128]{1,0:T(8,128)(2,1)S(1)} %bitcast.33, bf16[512,128]{1,0:T(8,128)(2,1)S(1)} %bitcast.35, ...), custom_call_target="tpu_custom_call" | custom-call | flops 939524096 | bytes 2097152 | tf_op jit(solution)/shard_map/attend/pallas_call | solution.py:95
  48.9 53.3 %all_gather.6 = bf16[2048,128]{1,0:T(8,128)(2,1)S(1)} all-gather(bf16[512,128]{1,0:T(8,128)(2,1)S(1)} %get-tuple-element.9), channel_id=1, replica_groups={{0,8,16,24},{1,9,17,25},{2,10,18,26},{3,11,19,27},{4,12,20,28},{5,13,21..., dimensions={0}, use_global_device_ids=true | all-gather | bytes 655360 | tf_op jit(solution)/shard_map/all_gather | solution.py:232
  102.2 4.0 %collective-permute-start.3 = (bf16[4,512,128]{2,1,0:T(8,128)(2,1)S(1)}, bf16[4,512,128]{2,1,0:T(8,128)(2,1)S(1)}, u32[]{:S(2)}, u32[]{:S(2)}) collective-permute-start(bf16[4,512,128]{2,1,0:T(8,128)(2,1)S(1)} %bitcast.25), channel_id=1, source_target_pairs={{0,1},{1,2},{2,3},{3,4},{4,5},{5,6},{6,7},{7,8},{8,9},{9,10},{10,1... | collective-permute-start | bytes 1572872 | tf_op jit(solution)/shard_map/ppermute | solution.py:28
  106.2 3.0 %collective-permute-start.4 = (bf16[4,512,128]{2,1,0:T(8,128)(2,1)S(1)}, bf16[4,512,128]{2,1,0:T(8,128)(2,1)S(1)}, u32[]{:S(2)}, u32[]{:S(2)}) collective-permute-start(bf16[4,512,128]{2,1,0:T(8,128)(2,1)S(1)} %bitcast.26), channel_id=1, source_target_pairs={{0,31},{1,0},{2,1},{3,2},{4,3},{5,4},{6,5},{7,6},{8,7},{9,8},{10,9... | collective-permute-start | bytes 1572872 | tf_op jit(solution)/shard_map/ppermute | solution.py:28
  109.3 8.7 %collective-permute-done.3.refs_1_ = bf16[4,512,128]{2,1,0:T(8,128)(2,1)S(1)} collective-permute-done((bf16[4,512,128]{2,1,0:T(8,128)(2,1)S(1)}, bf16[4,512,128]{2,1,0:T(8,128)(2,1)S(1)}, u32[]{:S(2)}, u32[]{:S(2)}) %collective-permute-start.3) | collective-permute-done | bytes 524320 | tf_op jit(solution)/shard_map/ppermute | solution.py:28
  118.0 3.7 %collective-permute-start.5 = (bf16[4,512,128]{2,1,0:T(8,128)(2,1)S(1)}, bf16[4,512,128]{2,1,0:T(8,128)(2,1)S(1)}, u32[]{:S(2)}, u32[]{:S(2)}) collective-permute-start(bf16[4,512,128]{2,1,0:T(8,128)(2,1)S(1)} %collective-permute-done.3.refs_1_), channel_id=1, source_target_pairs={{0,1},{1,2},{2,3},{3,4},{4,5},{5,6},{6,7},{7,8},{8,9},{9,10},{10,1... | collective-permute-start | bytes 1572872 | tf_op jit(solution)/shard_map/ppermute | solution.py:28
  121.7 3.3 %collective-permute-start.6 = (bf16[4,512,128]{2,1,0:T(8,128)(2,1)S(1)}, bf16[4,512,128]{2,1,0:T(8,128)(2,1)}, u32[]{:S(2)}, u32[]{:S(2)}) collective-permute-start(bf16[4,512,128]{2,1,0:T(8,128)(2,1)S(1)} %collective-permute-done.4.refs_2_), channel_id=1, source_target_pairs={{0,31},{1,0},{2,1},{3,2},{4,3},{5,4},{6,5},{7,6},{8,7},{9,8},{10,9... | collective-permute-start | bytes 1572872 | tf_op jit(solution)/shard_map/ppermute | solution.py:28
  125.1 8.1 %collective-permute-done.5.refs_3_ = bf16[4,512,128]{2,1,0:T(8,128)(2,1)S(1)} collective-permute-done((bf16[4,512,128]{2,1,0:T(8,128)(2,1)S(1)}, bf16[4,512,128]{2,1,0:T(8,128)(2,1)S(1)}, u32[]{:S(2)}, u32[]{:S(2)}) %collective-permute-start.5) | collective-permute-done | bytes 524320 | tf_op jit(solution)/shard_map/ppermute | solution.py:28
  133.2 3.2 %collective-permute-start.7 = (bf16[4,512,128]{2,1,0:T(8,128)(2,1)S(1)}, bf16[4,512,128]{2,1,0:T(8,128)(2,1)S(1)}, u32[]{:S(2)}, u32[]{:S(2)}) collective-permute-start(bf16[4,512,128]{2,1,0:T(8,128)(2,1)S(1)} %collective-permute-done.5.refs_3_), channel_id=1, source_target_pairs={{0,1},{1,2},{2,3},{3,4},{4,5},{5,6},{6,7},{7,8},{8,9},{9,10},{10,1... | collective-permute-start | bytes 1572872 | tf_op jit(solution)/shard_map/ppermute | solution.py:28
  136.4 3.9 %collective-permute-start.8 = (bf16[4,512,128]{2,1,0:T(8,128)(2,1)}, bf16[4,512,128]{2,1,0:T(8,128)(2,1)S(1)}, u32[]{:S(2)}, u32[]{:S(2)}) collective-permute-start(bf16[4,512,128]{2,1,0:T(8,128)(2,1)} %collective-permute-done.6.refs_4_), channel_id=1, source_target_pairs={{0,31},{1,0},{2,1},{3,2},{4,3},{5,4},{6,5},{7,6},{8,7},{9,8},{10,9... | collective-permute-start | bytes 1572872 | tf_op jit(solution)/shard_map/ppermute | solution.py:28
  140.3 7.1 %collective-permute-done.7.refs_5_ = bf16[4,512,128]{2,1,0:T(8,128)(2,1)S(1)} collective-permute-done((bf16[4,512,128]{2,1,0:T(8,128)(2,1)S(1)}, bf16[4,512,128]{2,1,0:T(8,128)(2,1)S(1)}, u32[]{:S(2)}, u32[]{:S(2)}) %collective-permute-start.7) | collective-permute-done | bytes 524320 | tf_op jit(solution)/shard_map/ppermute | solution.py:28
  148.2 2.7 %collective-permute-start.9 = (bf16[2,512,128]{2,1,0:T(8,128)(2,1)}, bf16[2,512,128]{2,1,0:T(8,128)(2,1)S(1)}, u32[]{:S(2)}, u32[]{:S(2)}) collective-permute-start(bf16[2,512,128]{2,1,0:T(8,128)(2,1)} %slice.40), channel_id=1, source_target_pairs={{0,1},{1,2},{2,3},{3,4},{4,5},{5,6},{6,7},{7,8},{8,9},{9,10},{10,1... | collective-permute-start | bytes 786440 | tf_op jit(solution)/shard_map/ppermute | solution.py:28
  151.6 4.3 %collective-permute-start.10 = (bf16[2,512,128]{2,1,0:T(8,128)(2,1)}, bf16[2,512,128]{2,1,0:T(8,128)(2,1)}, u32[]{:S(2)}, u32[]{:S(2)}) collective-permute-start(bf16[2,512,128]{2,1,0:T(8,128)(2,1)} %slice.41), channel_id=1, source_target_pairs={{0,31},{1,0},{2,1},{3,2},{4,3},{5,4},{6,5},{7,6},{8,7},{9,8},{10,9... | collective-permute-start | bytes 786440 | tf_op jit(solution)/shard_map/ppermute | solution.py:28
  156.6 1.0 reshape.81.refs_8_.aux
  157.7 2.2 %copy-done = bf16[4096,512]{1,0:T(8,128)(2,1)S(1)} copy-done((bf16[4096,512]{1,0:T(8,128)(2,1)S(1)}, bf16[4096,512]{1,0:T(8,128)(2,1)}, u32[]{:S(2)}) %copy-start) | copy-done | bytes 4194328
  159.8 4.2 %first.1 = (f32[528,512]{1,0:T(8,128)S(1)}, f32[512,128]{1,0:T(8,128)S(1)}, f32[512,128]{1,0:T(8,128)S(1)}, f32[512,128]{1,0:T(8,128)S(1)}) custom-call(s32[1]{0:T(128)} %bitcast.11.place, bf16[4,512,128]{2,1,0:T(8,128)(2,1)S(1)} %bitcast.27, bf16[4,512,128]{2,1,0:T(8,128)(2,1)S(1)} %collective-permute-done.3.refs_1_, ...), custom_call_target="tpu_custom_call" | custom-call | flops 2147483648 | bytes 9437184 | tf_op jit(solution)/shard_map/first/pallas_call | solution.py:152
  164.1 3.0 %last.1 = bf16[512,512]{1,0:T(8,128)(2,1)} custom-call(s32[1]{0:T(128)} %bitcast.11.place, f32[528,512]{1,0:T(8,128)S(1)} %get-tuple-element.10.acc, f32[512,128]{1,0:T(8,128)S(1)} %get-tuple-element.11.pivot, f32[512,128]{1,0:T(8,128)S(1)} %get-tuple-element.12.sum1, f32[512,128]{1,0:T(8,128)S(1)} %get-tuple-element.13.sum2, ...), custom_call_target="tpu_custom_call" | custom-call | flops 536870912 | bytes 7340032 | tf_op jit(solution)/shard_map/last/pallas_call | solution.py:184
  (44 shorter events, 10.3 us)
Async XLA Ops:
  7.2 117.9 %copy-start.7 = (bf16[4096]{0:T(1024)(128)(2,1)S(1)}, bf16[4096]{0:T(1024)(128)(2,1)}, u32[]{:S(2)}) copy-start(bf16[4096]{0:T(1024)(128)(2,1)} %param.16) | copy-start | bytes 24580
  7.2 117.9 %copy-start.8 = (bf16[4096]{0:T(1024)(128)(2,1)S(1)}, bf16[4096]{0:T(1024)(128)(2,1)}, u32[]{:S(2)}) copy-start(bf16[4096]{0:T(1024)(128)(2,1)} %param.17) | copy-start | bytes 24580
  7.2 150.5 %all-gather.2.cloned.1.call-start = ((), (), s32[]{:S(2)}) async-start(), calls=%async_computation | async-start | bytes 4325376 | tf_op jit(solution)/shard_map/all_gather | solution.py:212
  9.6 148.0 %copy-start.9 = (bf16[512]{0:T(512)(128)(2,1)S(1)}, bf16[512]{0:T(512)(128)(2,1)}, u32[]{:S(2)}) copy-start(bf16[512]{0:T(512)(128)(2,1)} %param.19) | copy-start | bytes 3076
  12.4 27.8 %collective-permute-start = (bf16[1408,128]{1,0:T(8,128)(2,1)S(1)}, bf16[1408,128]{1,0:T(8,128)(2,1)S(1)}, u32[]{:S(2)}, u32[]{:S(2)}) collective-permute-start(bf16[1408,128]{1,0:T(8,128)(2,1)S(1)} %get-tuple-element.15), channel_id=1, source_target_pairs={{0,256},{256,512},{512,768},{768,0},{1,257},{257,513},{513,769},{7... | collective-permute-start | bytes 1081352 | tf_op jit(solution)/shard_map/ppermute | solution.py:28
  27.4 13.3 %collective-permute-start.1 = (bf16[1408,128]{1,0:T(8,128)(2,1)S(1)}, bf16[1408,128]{1,0:T(8,128)(2,1)S(1)}, u32[]{:S(2)}, u32[]{:S(2)}) collective-permute-start(bf16[1408,128]{1,0:T(8,128)(2,1)S(1)} %get-tuple-element.14), channel_id=1, source_target_pairs={{0,768},{256,0},{512,256},{768,512},{1,769},{257,1},{513,257},{769... | collective-permute-start | bytes 1081352 | tf_op jit(solution)/shard_map/ppermute | solution.py:28
  30.3 9.9 %collective-permute-start.2 = (bf16[1024,128]{1,0:T(8,128)(2,1)S(1)}, bf16[1024,128]{1,0:T(8,128)(2,1)S(1)}, u32[]{:S(2)}, u32[]{:S(2)}) collective-permute-start(bf16[1024,128]{1,0:T(8,128)(2,1)S(1)} %pad_maximum_fusion.3), channel_id=1, source_target_pairs={{0,512},{256,768},{512,0},{768,256},{1,513},{257,769},{513,1},{769... | collective-permute-start | bytes 786440 | tf_op jit(solution)/shard_map/ppermute | solution.py:28
  40.8 0.9 copy-start.2
  41.7 0.9 copy-start.3
  42.6 0.9 copy-start.4
  43.5 0.9 copy-start.5
  102.2 15.8 %collective-permute-start.3 = (bf16[4,512,128]{2,1,0:T(8,128)(2,1)S(1)}, bf16[4,512,128]{2,1,0:T(8,128)(2,1)S(1)}, u32[]{:S(2)}, u32[]{:S(2)}) collective-permute-start(bf16[4,512,128]{2,1,0:T(8,128)(2,1)S(1)} %bitcast.25), channel_id=1, source_target_pairs={{0,1},{1,2},{2,3},{3,4},{4,5},{5,6},{6,7},{7,8},{8,9},{9,10},{10,1... | collective-permute-start | bytes 1572872 | tf_op jit(solution)/shard_map/ppermute | solution.py:28
  106.2 15.5 %collective-permute-start.4 = (bf16[4,512,128]{2,1,0:T(8,128)(2,1)S(1)}, bf16[4,512,128]{2,1,0:T(8,128)(2,1)S(1)}, u32[]{:S(2)}, u32[]{:S(2)}) collective-permute-start(bf16[4,512,128]{2,1,0:T(8,128)(2,1)S(1)} %bitcast.26), channel_id=1, source_target_pairs={{0,31},{1,0},{2,1},{3,2},{4,3},{5,4},{6,5},{7,6},{8,7},{9,8},{10,9... | collective-permute-start | bytes 1572872 | tf_op jit(solution)/shard_map/ppermute | solution.py:28
  118.0 15.2 %collective-permute-start.5 = (bf16[4,512,128]{2,1,0:T(8,128)(2,1)S(1)}, bf16[4,512,128]{2,1,0:T(8,128)(2,1)S(1)}, u32[]{:S(2)}, u32[]{:S(2)}) collective-permute-start(bf16[4,512,128]{2,1,0:T(8,128)(2,1)S(1)} %collective-permute-done.3.refs_1_), channel_id=1, source_target_pairs={{0,1},{1,2},{2,3},{3,4},{4,5},{5,6},{6,7},{7,8},{8,9},{9,10},{10,1... | collective-permute-start | bytes 1572872 | tf_op jit(solution)/shard_map/ppermute | solution.py:28
  121.7 14.6 %collective-permute-start.6 = (bf16[4,512,128]{2,1,0:T(8,128)(2,1)S(1)}, bf16[4,512,128]{2,1,0:T(8,128)(2,1)}, u32[]{:S(2)}, u32[]{:S(2)}) collective-permute-start(bf16[4,512,128]{2,1,0:T(8,128)(2,1)S(1)} %collective-permute-done.4.refs_2_), channel_id=1, source_target_pairs={{0,31},{1,0},{2,1},{3,2},{4,3},{5,4},{6,5},{7,6},{8,7},{9,8},{10,9... | collective-permute-start | bytes 1572872 | tf_op jit(solution)/shard_map/ppermute | solution.py:28
  133.2 14.3 %collective-permute-start.7 = (bf16[4,512,128]{2,1,0:T(8,128)(2,1)S(1)}, bf16[4,512,128]{2,1,0:T(8,128)(2,1)S(1)}, u32[]{:S(2)}, u32[]{:S(2)}) collective-permute-start(bf16[4,512,128]{2,1,0:T(8,128)(2,1)S(1)} %collective-permute-done.5.refs_3_), channel_id=1, source_target_pairs={{0,1},{1,2},{2,3},{3,4},{4,5},{5,6},{6,7},{7,8},{8,9},{9,10},{10,1... | collective-permute-start | bytes 1572872 | tf_op jit(solution)/shard_map/ppermute | solution.py:28
  136.4 14.5 %collective-permute-start.8 = (bf16[4,512,128]{2,1,0:T(8,128)(2,1)}, bf16[4,512,128]{2,1,0:T(8,128)(2,1)S(1)}, u32[]{:S(2)}, u32[]{:S(2)}) collective-permute-start(bf16[4,512,128]{2,1,0:T(8,128)(2,1)} %collective-permute-done.6.refs_4_), channel_id=1, source_target_pairs={{0,31},{1,0},{2,1},{3,2},{4,3},{5,4},{6,5},{7,6},{8,7},{9,8},{10,9... | collective-permute-start | bytes 1572872 | tf_op jit(solution)/shard_map/ppermute | solution.py:28
  148.2 15.9 %collective-permute-start.9 = (bf16[2,512,128]{2,1,0:T(8,128)(2,1)}, bf16[2,512,128]{2,1,0:T(8,128)(2,1)S(1)}, u32[]{:S(2)}, u32[]{:S(2)}) collective-permute-start(bf16[2,512,128]{2,1,0:T(8,128)(2,1)} %slice.40), channel_id=1, source_target_pairs={{0,1},{1,2},{2,3},{3,4},{4,5},{5,6},{6,7},{7,8},{8,9},{9,10},{10,1... | collective-permute-start | bytes 786440 | tf_op jit(solution)/shard_map/ppermute | solution.py:28
  151.6 12.5 %collective-permute-start.10 = (bf16[2,512,128]{2,1,0:T(8,128)(2,1)}, bf16[2,512,128]{2,1,0:T(8,128)(2,1)}, u32[]{:S(2)}, u32[]{:S(2)}) collective-permute-start(bf16[2,512,128]{2,1,0:T(8,128)(2,1)} %slice.41), channel_id=1, source_target_pairs={{0,31},{1,0},{2,1},{3,2},{4,3},{5,4},{6,5},{7,6},{8,7},{9,8},{10,9... | collective-permute-start | bytes 786440 | tf_op jit(solution)/shard_map/ppermute | solution.py:28
  156.0 0.7 copy-start.6
  157.7 2.2 %copy-start = (bf16[4096,512]{1,0:T(8,128)(2,1)S(1)}, bf16[4096,512]{1,0:T(8,128)(2,1)}, u32[]{:S(2)}) copy-start(bf16[4096,512]{1,0:T(8,128)(2,1)} %all-gather.2.cloned.1.call-done) | copy-start | bytes 12582916
  159.8 4.3 %copy-start.1 = (bf16[4096,512]{1,0:T(8,128)(2,1)S(1)}, bf16[4096,512]{1,0:T(8,128)(2,1)}, u32[]{:S(2)}) copy-start(bf16[4096,512]{1,0:T(8,128)(2,1)} %all-gather.2.cloned.1.call-done) | copy-start | bytes 12582916
Sparse Core Ops, SparseCore 0:
  12.3 89.0 all-gather.1

commit v2 on v1

v2 whole, which is shorter than its diff:
```python
import functools
import math

import jax
import jax.numpy as jnp
from jax import lax
from jax.experimental import pallas as pl
from jax.experimental.pallas import tpu as pltpu
from jax.sharding import PartitionSpec as P

HEAD_DIM = 128
KERNEL = 7
MARGIN = KERNEL // 2
IMG_W = 64
ROWS = 8
POS = ROWS * IMG_W
EDGE = MARGIN * IMG_W
C = 4096
SEQ = 4
CLASSES = 8
LEFT = 8
F32 = jnp.float32
BF16 = jnp.bfloat16


def shift(array, axis, by):
    peers = lax.axis_size(axis)
    return lax.ppermute(array, axis, [(i, (i + by) % peers) for i in range(peers)])


def pack_kernel(place, k, v, q, x, weight_in, gain_in, kv, lower, upper, scaled, weight, gain, sems):
    first, end = slice(0, EDGE), slice(POS - EDGE, POS)
    moves = [(weight_in, weight), (gain_in, gain), (k, kv.at[0:POS]), (v, kv.at[POS:])]
    for message, edge in ((lower, end), (upper, first)):
        moves += [
            (k, message.at[0:POS]),
            (v, message.at[POS : 2 * POS]),
            (q.at[edge], message.at[2 * POS : 2 * POS + EDGE]),
            (x.at[edge], message.at[2 * POS + EDGE :]),
        ]
    copies = [pltpu.make_async_copy(a, b, sems.at[i]) for i, (a, b) in enumerate(moves)]
    for copy in copies:
        copy.start()
    for copy in copies[:2]:
        copy.wait()
    depth = weight.shape[0]
    gains = gain[...].astype(F32)
    line = lax.broadcasted_iota(jnp.int32, gains.shape, 0) == place[0]
    mine = jnp.sum(jnp.where(line, gains, 0.0), axis=0, keepdims=True)
    mine = jnp.transpose(jnp.broadcast_to(mine, (depth, depth)))
    for c in range(0, weight.shape[1], depth):
        scaled[:, c : c + depth] = (weight[:, c : c + depth].astype(F32) * mine).astype(BF16)
    for copy in copies[2:]:
        copy.wait()


def pack(place, k, v, q, x, weight, gain):
    vmem, here = pl.BlockSpec(memory_space=pltpu.VMEM), pl.BlockSpec(memory_space=pltpu.HBM)
    two = jax.ShapeDtypeStruct((2 * POS, HEAD_DIM), BF16)
    message = jax.ShapeDtypeStruct((2 * (POS + EDGE), HEAD_DIM), BF16)
    return pl.pallas_call(
        pack_kernel,
        out_shape=(two, message, message, jax.ShapeDtypeStruct(weight.shape, BF16)),
        in_specs=[pl.BlockSpec(memory_space=pltpu.SMEM)] + [here] * 6,
        out_specs=(vmem,) * 4,
        scratch_shapes=[
            pltpu.VMEM(weight.shape, BF16),
            pltpu.VMEM(gain.shape, BF16),
            pltpu.SemaphoreType.DMA((12,)),
        ],
        compiler_params=pltpu.CompilerParams(vmem_limit_bytes=8 << 20),
        name="pack",
    )(place, k, v, q, x, weight, gain)


def attend_kernel(place, k, v, q, x, above, below, far, taps, bias, res, conv, kv, qs, xs, image, sems):
    middle = slice(EDGE, EDGE + POS)
    moves = ((k, kv.at[0:POS]), (v, kv.at[POS:]), (q, qs.at[middle]), (x, xs.at[middle]))
    copies = [pltpu.make_async_copy(a, b, sems.at[i]) for i, (a, b) in enumerate(moves)]
    for copy in copies:
        copy.start()
    qs[0:EDGE] = above[2 * POS : 2 * POS + EDGE]
    qs[EDGE + POS :] = below[2 * POS : 2 * POS + EDGE]
    xs[0:EDGE] = above[2 * POS + EDGE :]
    xs[EDGE + POS :] = below[2 * POS + EDGE :]
    tall = ROWS + 2 * MARGIN
    blank = jnp.zeros((tall, 8, HEAD_DIM), F32)
    image[:, 0:LEFT, :] = blank
    image[:, LEFT + IMG_W : LEFT + IMG_W + 8, :] = blank
    for copy in copies:
        copy.wait()
    keys = [part[0:POS] for part in (kv, above, below, far)]
    values = [part[POS : 2 * POS] for part in (kv, above, below, far)]
    to_log2 = math.log2(math.e) / math.sqrt(HEAD_DIM)
    tile = 2 * IMG_W
    for t in range(tall // 2):
        own = slice(t * tile, (t + 1) * tile)
        queries = qs[own]
        scores = [
            lax.dot_general(queries, key, (((1,), (1,)), ((), ())), preferred_element_type=F32)
            for key in keys
        ]
        peak = functools.reduce(jnp.maximum, scores)
        peak = jnp.max(peak, axis=1, keepdims=True)
        weights = [jnp.exp2((score - peak) * to_log2) for score in scores]
        total = jnp.sum(functools.reduce(jnp.add, weights), axis=1, keepdims=True)
        summed = functools.reduce(
            jnp.add,
            [
                jnp.dot(weight.astype(BF16), value, preferred_element_type=F32)
                for weight, value in zip(weights, values)
            ],
        )
        out = (xs[own].astype(F32) + summed / total).astype(BF16).astype(F32)
        image[2 * t : 2 * t + 2, LEFT : LEFT + IMG_W, :] = out.reshape(2, IMG_W, HEAD_DIM)

    @pl.when(place[0] == 0)
    def _():
        image[0:MARGIN] = jnp.zeros((MARGIN, IMG_W + 16, HEAD_DIM), F32)

    @pl.when(place[0] == SEQ - 1)
    def _():
        image[tall - MARGIN :] = jnp.zeros((MARGIN, IMG_W + 16, HEAD_DIM), F32)

    for i in range(ROWS):
        res[i * IMG_W : (i + 1) * IMG_W] = image[MARGIN + i, LEFT : LEFT + IMG_W, :].astype(BF16)
    wide = 16
    for c0 in range(0, IMG_W, wide):
        sums = [jnp.broadcast_to(bias[...], (wide, HEAD_DIM)) for _ in range(ROWS)]
        for b in range(KERNEL):
            start = LEFT - MARGIN + b + c0
            columns = [image[r, start : start + wide, :] for r in range(tall)]
            for a in range(KERNEL):
                tap = taps[a * KERNEL + b : a * KERNEL + b + 1, :]
                for i in range(ROWS):
                    sums[i] = sums[i] + columns[i + a] * tap
        for i in range(ROWS):
            conv[i * IMG_W + c0 : i * IMG_W + c0 + wide] = sums[i].astype(BF16)


def attend(place, k, v, q, x, above, below, far, taps, bias):
    out = jax.ShapeDtypeStruct((POS, HEAD_DIM), BF16)
    vmem, here = pl.BlockSpec(memory_space=pltpu.VMEM), pl.BlockSpec(memory_space=pltpu.HBM)
    flops = 4 * (POS + 2 * EDGE) * SEQ * POS * HEAD_DIM
    return pl.pallas_call(
        attend_kernel,
        out_shape=(out, out),
        in_specs=[pl.BlockSpec(memory_space=pltpu.SMEM)] + [here] * 4 + [vmem] * 5,
        out_specs=(vmem, vmem),
        scratch_shapes=[
            pltpu.VMEM((2 * POS, HEAD_DIM), BF16),
            pltpu.VMEM((POS + 2 * EDGE, HEAD_DIM), BF16),
            pltpu.VMEM((POS + 2 * EDGE, HEAD_DIM), BF16),
            pltpu.VMEM((ROWS + 2 * MARGIN, IMG_W + 16, HEAD_DIM), F32),
            pltpu.SemaphoreType.DMA((4,)),
        ],
        compiler_params=pltpu.CompilerParams(vmem_limit_bytes=16 << 20),
        cost_estimate=pl.CostEstimate(flops=flops, bytes_accessed=2 << 20, transcendentals=2 << 20),
        name="attend",
    )(place, k, v, q, x, above, below, far, taps, bias)


AUX = 16


def fetch(weights, groups, slabs, sems):
    copies = []
    for n, group in enumerate(groups):
        rows = weights.shape[2]
        copies.append(
            [
                pltpu.make_async_copy(
                    weights.at[j, group], slabs.at[n, j * rows : (j + 1) * rows], sems.at[n, j]
                )
                for j in range(SEQ)
            ]
        )
        for copy in copies[-1]:
            copy.start()
    return copies


def slab_scratch(count, weights):
    _, _, rows, columns = weights.shape
    return [
        pltpu.VMEM((count, SEQ * rows, columns), BF16),
        pltpu.SemaphoreType.DMA((count, SEQ)),
    ]


def extra_rows(gain, offset, group):
    tiles = []
    for j in range(SEQ):
        here = pl.ds(j * CLASSES + group, 1)
        ratio = offset[here] / gain[here]
        high = ratio.astype(BF16).astype(F32)
        row = lax.broadcasted_iota(jnp.int32, (AUX, HEAD_DIM), 0)
        tile = jnp.where(row == 0, 1.0, 0.0)
        tile = jnp.where(row == 1, jnp.broadcast_to(high, tile.shape), tile)
        tile = jnp.where(row == 2, jnp.broadcast_to(ratio - high, tile.shape), tile)
        tiles.append(tile.astype(BF16))
    return jnp.concatenate(tiles, axis=1)


def product_of(blocks, copies, slab, gain, offset, group):
    left = jnp.concatenate([block[...] for block in blocks], axis=1)
    left = jnp.concatenate([left, extra_rows(gain, offset, group)], axis=0)
    for copy in copies:
        copy.wait()
    return jnp.dot(left, slab[...], preferred_element_type=F32)


def add_stats(blocks, pivot, before1, before2, sum1, sum2, rows=64):
    for t in range(0, POS, rows):
        here = slice(t, t + rows)
        centre, one, two = pivot[here], before1[here], before2[here]
        for block in blocks:
            away = block[here].astype(F32) - centre
            one = one + away
            two = two + away * away
        sum1[here] = one
        sum2[here] = two


def first_kernel(offsets, place, *refs):
    count = len(offsets)
    parts, refs = refs[:count], refs[count:]
    weights, gain, offset, acc, pivot, sum1, sum2, slabs, sems = refs
    groups = [lax.rem(place[0] + away + CLASSES, CLASSES) for away in offsets]
    copies = fetch(weights, groups, slabs, sems)
    lead = jnp.mean(parts[0][0].astype(F32), axis=1, keepdims=True)
    pivot[...] = jnp.broadcast_to(lead, (POS, HEAD_DIM))
    sum1[...] = jnp.zeros((POS, HEAD_DIM), F32)
    sum2[...] = jnp.zeros((POS, HEAD_DIM), F32)
    for n, part in enumerate(parts):
        blocks = [part.at[j] for j in range(SEQ)]
        product = product_of(blocks, copies[n], slabs.at[n], gain, offset, groups[n])
        if n == 0:
            acc[...] = product
        else:
            acc[...] += product
        add_stats(blocks, pivot, sum1, sum2, sum1, sum2)


def more_kernel(offsets, place, *refs):
    count = len(offsets)
    parts, refs = refs[:count], refs[count:]
    acc, pivot, sum1, sum2, weights, gain, offset, acc_out, sum1_out, sum2_out, slabs, sems = refs
    groups = [lax.rem(place[0] + away + CLASSES, CLASSES) for away in offsets]
    copies = fetch(weights, groups, slabs, sems)
    for n, part in enumerate(parts):
        blocks = [part.at[j] for j in range(SEQ)]
        before = (acc, sum1, sum2) if n == 0 else (acc_out, sum1_out, sum2_out)
        product = product_of(blocks, copies[n], slabs.at[n], gain, offset, groups[n])
        acc_out[...] = before[0][...] + product
        add_stats(blocks, pivot, before[1], before[2], sum1_out, sum2_out)


def stage(kernel, offsets, place, parts, before, weights, gain, offset):
    vmem, here = pl.BlockSpec(memory_space=pltpu.VMEM), pl.BlockSpec(memory_space=pltpu.HBM)
    hidden = weights.shape[-1]
    stat = jax.ShapeDtypeStruct((POS, HEAD_DIM), F32)
    total = jax.ShapeDtypeStruct((POS + AUX, hidden), F32)
    out_shape = (total, stat, stat) if before else (total, stat, stat, stat)
    return pl.pallas_call(
        functools.partial(kernel, offsets),
        out_shape=out_shape,
        in_specs=[pl.BlockSpec(memory_space=pltpu.SMEM)]
        + [vmem] * (len(parts) + len(before))
        + [here, vmem, vmem],
        out_specs=(vmem,) * len(out_shape),
        scratch_shapes=slab_scratch(len(parts), weights),
        compiler_params=pltpu.CompilerParams(vmem_limit_bytes=16 << 20),
        cost_estimate=pl.CostEstimate(
            flops=len(parts) << 28, bytes_accessed=len(parts) << 20, transcendentals=0
        ),
        name="stage",
    )(place, *parts, *before, weights, gain, offset)


def last_kernel(place, *refs):
    acc, pivot, sum1, sum2, above, below, weights, gain, offset, bias, out, one, two, slabs, sems = refs
    group = lax.rem(place[0] + 4, CLASSES)
    (copies,) = fetch(weights, [group], slabs, sems)
    blocks = [above.at[0], above.at[1], below.at[0], below.at[1]]
    add_stats(blocks, pivot, sum1, sum2, one, two)
    product = acc[...] + product_of(blocks, copies, slabs.at[0], gain, offset, group)
    mean1 = jnp.sum(one[...], axis=1, keepdims=True) * (1.0 / C)
    mean2 = jnp.sum(two[...], axis=1, keepdims=True) * (1.0 / C)
    centre = pivot[:, 0:1] + mean1
    spread = jnp.maximum(mean2 - mean1 * mean1, 0.0)
    scale = lax.rsqrt(spread + 1e-06)
    slope = product[POS : POS + 1]
    level = product[POS + 1 : POS + 2] + product[POS + 2 : POS + 3] + bias[...]
    project = scale * (product[0:POS] - centre * slope) + level
    out[...] = (0.5 * project * (1.0 + lax.erf(project * math.sqrt(0.5)))).astype(BF16)


def last(place, acc, stats, above, below, weights, gain, offset, bias):
    vmem, here = pl.BlockSpec(memory_space=pltpu.VMEM), pl.BlockSpec(memory_space=pltpu.HBM)
    hidden = weights.shape[-1]
    return pl.pallas_call(
        last_kernel,
        out_shape=jax.ShapeDtypeStruct((POS, hidden), BF16),
        in_specs=[pl.BlockSpec(memory_space=pltpu.SMEM)] + [vmem] * 6 + [here] + [vmem] * 3,
        out_specs=vmem,
        scratch_shapes=[pltpu.VMEM((POS, HEAD_DIM), F32)] * 2 + slab_scratch(1, weights),
        compiler_params=pltpu.CompilerParams(vmem_limit_bytes=16 << 20),
        cost_estimate=pl.CostEstimate(flops=1 << 28, bytes_accessed=7 << 20, transcendentals=1 << 18),
        name="last",
    )(place, acc, *stats, above, below, weights, gain, offset, bias)


def on_device(
    inputs,
    query_proj,
    key_proj,
    value_proj,
    depth_weight,
    depth_bias,
    norm_gain,
    norm_bias,
    expand_weight,
    expand_bias,
):
    seq, row, col = (lax.axis_index(axis) for axis in ("seq", "row", "col"))
    depth, hidden = expand_weight.shape
    gain, offset = (a.reshape(C // depth, depth) for a in (norm_gain, norm_bias))
    x, q, k, v = (a.reshape(POS, HEAD_DIM) for a in (inputs, query_proj, key_proj, value_proj))
    x, q, k, v = (pltpu.with_memory_space_constraint(a, pltpu.HBM) for a in (x, q, k, v))
    mine = (seq * CLASSES + row).astype(jnp.int32).reshape(1)
    held = (pltpu.with_memory_space_constraint(a, pltpu.HBM) for a in (expand_weight, gain))
    kv, lower, upper, scaled = pack(mine, k, v, q, x, *held)
    far = shift(kv, "seq", 2)
    above, below = shift(lower, "seq", 1), shift(upper, "seq", -1)
    weights = lax.all_gather(scaled, ("seq", "row"), axis=0, tiled=True)
    weights = weights.reshape(SEQ, CLASSES, depth, hidden)
    weights = pltpu.with_memory_space_constraint(weights, pltpu.HBM)
    gain, offset = gain.astype(F32), offset.astype(F32)
    taps = depth_weight.astype(F32).reshape(KERNEL * KERNEL, HEAD_DIM)
    bias = depth_bias.astype(F32).reshape(1, HEAD_DIM)
    residual, convolved = attend(
        seq.astype(jnp.int32).reshape(1), k, v, q, x, above, below, far, taps, bias
    )

    strides = [[i + CLASSES * j for j in range(SEQ)] for i in range(CLASSES)]
    own = lax.all_gather(convolved, "col", axis=0, tiled=True, axis_index_groups=strides)
    own = own.reshape(SEQ, POS, HEAD_DIM)
    pairs, up, down = [], own, own
    for _ in range(3):
        up, down = shift(up, "col", 1), shift(down, "col", -1)
        pairs.append((up, down))
    place = col.astype(jnp.int32).reshape(1)
    parts = (own, *pairs[0], *pairs[1])
    before = stage(first_kernel, (0, -1, 1, -2, 2), place, parts, (), weights, gain, offset)
    up, down, before = lax.optimization_barrier((up, down, before))
    pairs[2] = (up, down)
    up, down = shift(up[:2], "col", 1), shift(down[2:], "col", -1)
    acc, *sums = stage(more_kernel, (-3, 3), place, pairs[2], before, weights, gain, offset)
    pivot = before[1]
    bias = expand_bias.astype(F32).reshape(1, hidden)
    out = last(place, acc, (pivot, *sums), up, down, weights, gain, offset, bias)
    return (
        residual.reshape(inputs.shape),
        out.reshape(inputs.shape[:3] + (hidden,)),
    )


def solution(mesh):
    return jax.shard_map(
        on_device,
        mesh=mesh,
        in_specs=(
            P("row", "seq", None, "col"),
            P("row", "seq", None, "col"),
            P("row", "seq", None, "col"),
            P("row", "seq", None, "col"),
            P(None, None, "col"),
            P("col"),
            P(),
            P(),
            P(("seq", "row"), "col"),
            P("col"),
        ),
        out_specs=(P("row", "seq", None, "col"), P("row", "seq", None, "col")),
        check_vma=False,
    )
```

time: 176 us -> 172 us (0.977)
  local copies, waits for them, and re-layouts: 12.1 us -> 0.78 us
  Pallas kernels: 11.7 us -> 17.9 us
  waiting for transfers between devices: 29.6 us -> 33.8 us
  other arithmetic: 4.35 us -> 0.67 us
    unnamed x25 -> x6, local copies, waits for them, and re-layouts: 6.52 us -> 0.01 us
    pallas_call x1 -> x3, Pallas kernels: 4.24 us -> 9.1 us  [the longest x2 7.05 us: stage(): pl.pallas_call(functools.partial(kernel, offsets), out_shape=out_shape, i...]
    ppermute x11, waiting for transfers between devices: 29.6 us -> 33.7 us  [shift(): lax.ppermute(array, axis, [(i, (i + by) % peers) for i in range(peers)])]
    concatenate x2 -> x0, other arithmetic: 2.04 us -> none  [the longest x1 1.05 us: on_device(): below = shift(jnp.concatenate([k, v, q[:EDGE], x[:EDGE]]), 'seq', -1)]
  transfers between devices with their start and end apart: 12 -> 12, of which waited for: 5 -> 7; matrix products, arithmetic and copies ran while one was open for 4% -> 1% of each run, Pallas kernels for 5% -> 8%
where the time goes in v2:
time: 172 us; the launch traced here: 168 us
  blocking collectives  53.3 us (31%)
  starting transfers between devices  47.6 us (28%)
  waiting for transfers between devices  33.8 us (20%)
  Pallas kernels  17.9 us (10%)
  between operations  14.3 us (8%)
    all_gather x1, blocking collectives, on_device(): lax.all_gather(convolved, 'col', axis=0, tiled=True, axis_index_groups=st...  53.3 us
    ppermute x11, starting transfers between devices, shift(): lax.ppermute(array, axis, [(i, (i + by) % peers) for i in range(peers)])  47.6 us
    ppermute x11, waiting for transfers between devices, shift(): lax.ppermute(array, axis, [(i, (i + by) % peers) for i in range(peers)])  33.7 us
    pallas_call x2, Pallas kernels, stage(): pl.pallas_call(functools.partial(kernel, offsets), out_shape=out_shape, i...  7.05 us
    pallas_call x1, Pallas kernels, attend(): pl.pallas_call(attend_kernel, out_shape=(out, out), in_specs=[pl.BlockSpe...  5.73 us
  transfers between devices with their start and end apart: 12, of which 7 were waited for; matrix products, arithmetic and copies ran while one was open for 1% of the time, Pallas kernels for 8%

profile of v2, /device:TPU:6, one launch (start us, length us, event | category | flops | bytes accessed | tf_op | source)
XLA Modules:
  0.0 168.4 jit_solution(12872971031158467531)
XLA Ops:
  7.2 2.1 %pack.1 = (bf16[1024,128]{1,0:T(8,128)(2,1)S(1)}, bf16[1408,128]{1,0:T(8,128)(2,1)S(1)}, bf16[1408,128]{1,0:T(8,128)(2,1)S(1)}, bf16[128,512]{1,0:T(8,128)(2,1)}) custom-call(s32[1]{0:T(128)} %bitcast.5.place, bf16[512,128]{1,0:T(8,128)(2,1)} %bitcast.28, bf16[512,128]{1,0:T(8,128)(2,1)} %bitcast.30, bf16[512,128]{1,0:T(8,128)(2,1)} %bitcast.32, ...), custom_call_target="tpu_custom_call" | custom-call | tf_op jit(solution)/shard_map/pack/pallas_call | solution.py:61
  9.3 15.0 %collective-permute-start = (bf16[1408,128]{1,0:T(8,128)(2,1)S(1)}, bf16[1408,128]{1,0:T(8,128)(2,1)S(1)}, u32[]{:S(2)}, u32[]{:S(2)}) collective-permute-start(bf16[1408,128]{1,0:T(8,128)(2,1)S(1)} %get-tuple-element.21), channel_id=1, source_target_pairs={{0,256},{256,512},{512,768},{768,0},{1,257},{257,513},{513,769},{7... | collective-permute-start | bytes 1081352 | tf_op jit(solution)/shard_map/ppermute | solution.py:28
  24.3 1.9 %collective-permute-start.1 = (bf16[1408,128]{1,0:T(8,128)(2,1)S(1)}, bf16[1408,128]{1,0:T(8,128)(2,1)S(1)}, u32[]{:S(2)}, u32[]{:S(2)}) collective-permute-start(bf16[1408,128]{1,0:T(8,128)(2,1)S(1)} %get-tuple-element.22), channel_id=1, source_target_pairs={{0,768},{256,0},{512,256},{768,512},{1,769},{257,1},{513,257},{769... | collective-permute-start | bytes 1081352 | tf_op jit(solution)/shard_map/ppermute | solution.py:28
  26.3 3.4 %collective-permute-start.2 = (bf16[1024,128]{1,0:T(8,128)(2,1)S(1)}, bf16[1024,128]{1,0:T(8,128)(2,1)S(1)}, u32[]{:S(2)}, u32[]{:S(2)}) collective-permute-start(bf16[1024,128]{1,0:T(8,128)(2,1)S(1)} %get-tuple-element.23), channel_id=1, source_target_pairs={{0,512},{256,768},{512,0},{768,256},{1,513},{257,769},{513,1},{769... | collective-permute-start | bytes 786440 | tf_op jit(solution)/shard_map/ppermute | solution.py:28
  31.0 5.1 %collective-permute-done.2.far = bf16[1024,128]{1,0:T(8,128)(2,1)S(1)} collective-permute-done((bf16[1024,128]{1,0:T(8,128)(2,1)S(1)}, bf16[1024,128]{1,0:T(8,128)(2,1)S(1)}, u32[]{:S(2)}, u32[]{:S(2)}) %collective-permute-start.2) | collective-permute-done | bytes 262176 | tf_op jit(solution)/shard_map/ppermute | solution.py:28
  36.2 1.5 collective-permute-done.1.below
  37.7 5.7 %attend.1 = (bf16[512,128]{1,0:T(8,128)(2,1)}, bf16[512,128]{1,0:T(8,128)(2,1)S(1)}) custom-call(s32[1]{0:T(128)} %bitcast.place, bf16[512,128]{1,0:T(8,128)(2,1)} %bitcast.29, bf16[512,128]{1,0:T(8,128)(2,1)} %bitcast.31, bf16[512,128]{1,0:T(8,128)(2,1)} %bitcast.33, bf16[512,128]{1,0:T(8,128)(2,1)} %bitcast.35, ...), custom_call_target="tpu_custom_call" | custom-call | flops 939524096 | bytes 2097152 | tf_op jit(solution)/shard_map/attend/pallas_call | solution.py:145
  43.4 53.3 %all_gather.6 = bf16[2048,128]{1,0:T(8,128)(2,1)S(1)} all-gather(bf16[512,128]{1,0:T(8,128)(2,1)S(1)} %get-tuple-element.25), channel_id=1, replica_groups={{0,8,16,24},{1,9,17,25},{2,10,18,26},{3,11,19,27},{4,12,20,28},{5,13,21..., dimensions={0}, use_global_device_ids=true | all-gather | bytes 655360 | tf_op jit(solution)/shard_map/all_gather | solution.py:347
  96.8 4.0 %collective-permute-start.3 = (bf16[4,512,128]{2,1,0:T(8,128)(2,1)S(1)}, bf16[4,512,128]{2,1,0:T(8,128)(2,1)S(1)}, u32[]{:S(2)}, u32[]{:S(2)}) collective-permute-start(bf16[4,512,128]{2,1,0:T(8,128)(2,1)S(1)} %bitcast.20), channel_id=1, source_target_pairs={{0,1},{1,2},{2,3},{3,4},{4,5},{5,6},{6,7},{7,8},{8,9},{9,10},{10,1... | collective-permute-start | bytes 1572872 | tf_op jit(solution)/shard_map/ppermute | solution.py:28
  100.7 3.1 %collective-permute-start.6 = (bf16[4,512,128]{2,1,0:T(8,128)(2,1)S(1)}, bf16[4,512,128]{2,1,0:T(8,128)(2,1)S(1)}, u32[]{:S(2)}, u32[]{:S(2)}) collective-permute-start(bf16[4,512,128]{2,1,0:T(8,128)(2,1)S(1)} %bitcast.21), channel_id=1, source_target_pairs={{0,31},{1,0},{2,1},{3,2},{4,3},{5,4},{6,5},{7,6},{8,7},{9,8},{10,9... | collective-permute-start | bytes 1572872 | tf_op jit(solution)/shard_map/ppermute | solution.py:28
  103.8 8.8 %collective-permute-done.3.refs_1_ = bf16[4,512,128]{2,1,0:T(8,128)(2,1)S(1)} collective-permute-done((bf16[4,512,128]{2,1,0:T(8,128)(2,1)S(1)}, bf16[4,512,128]{2,1,0:T(8,128)(2,1)S(1)}, u32[]{:S(2)}, u32[]{:S(2)}) %collective-permute-start.3) | collective-permute-done | bytes 524320 | tf_op jit(solution)/shard_map/ppermute | solution.py:28
  112.7 3.6 %collective-permute-start.4 = (bf16[4,512,128]{2,1,0:T(8,128)(2,1)S(1)}, bf16[4,512,128]{2,1,0:T(8,128)(2,1)S(1)}, u32[]{:S(2)}, u32[]{:S(2)}) collective-permute-start(bf16[4,512,128]{2,1,0:T(8,128)(2,1)S(1)} %collective-permute-done.3.refs_1_), channel_id=1, source_target_pairs={{0,1},{1,2},{2,3},{3,4},{4,5},{5,6},{6,7},{7,8},{8,9},{9,10},{10,1... | collective-permute-start | bytes 1572872 | tf_op jit(solution)/shard_map/ppermute | solution.py:28
  116.3 3.4 %collective-permute-start.7 = (bf16[4,512,128]{2,1,0:T(8,128)(2,1)S(1)}, bf16[4,512,128]{2,1,0:T(8,128)(2,1)}, u32[]{:S(2)}, u32[]{:S(2)}) collective-permute-start(bf16[4,512,128]{2,1,0:T(8,128)(2,1)S(1)} %collective-permute-done.6.refs_2_), channel_id=1, source_target_pairs={{0,31},{1,0},{2,1},{3,2},{4,3},{5,4},{6,5},{7,6},{8,7},{9,8},{10,9... | collective-permute-start | bytes 1572872 | tf_op jit(solution)/shard_map/ppermute | solution.py:28
  119.7 8.0 %collective-permute-done.4.refs_3_ = bf16[4,512,128]{2,1,0:T(8,128)(2,1)S(1)} collective-permute-done((bf16[4,512,128]{2,1,0:T(8,128)(2,1)S(1)}, bf16[4,512,128]{2,1,0:T(8,128)(2,1)S(1)}, u32[]{:S(2)}, u32[]{:S(2)}) %collective-permute-start.4) | collective-permute-done | bytes 524320 | tf_op jit(solution)/shard_map/ppermute | solution.py:28
  127.7 3.2 %collective-permute-start.5 = (bf16[4,512,128]{2,1,0:T(8,128)(2,1)S(1)}, bf16[4,512,128]{2,1,0:T(8,128)(2,1)S(1)}, u32[]{:S(2)}, u32[]{:S(2)}) collective-permute-start(bf16[4,512,128]{2,1,0:T(8,128)(2,1)S(1)} %collective-permute-done.4.refs_3_), channel_id=1, source_target_pairs={{0,1},{1,2},{2,3},{3,4},{4,5},{5,6},{6,7},{7,8},{8,9},{9,10},{10,1... | collective-permute-start | bytes 1572872 | tf_op jit(solution)/shard_map/ppermute | solution.py:28
  130.9 3.9 %collective-permute-start.8 = (bf16[4,512,128]{2,1,0:T(8,128)(2,1)}, bf16[4,512,128]{2,1,0:T(8,128)(2,1)S(1)}, u32[]{:S(2)}, u32[]{:S(2)}) collective-permute-start(bf16[4,512,128]{2,1,0:T(8,128)(2,1)} %collective-permute-done.7.refs_4_), channel_id=1, source_target_pairs={{0,31},{1,0},{2,1},{3,2},{4,3},{5,4},{6,5},{7,6},{8,7},{9,8},{10,9... | collective-permute-start | bytes 1572872 | tf_op jit(solution)/shard_map/ppermute | solution.py:28
  134.9 4.8 %stage.2 = (f32[528,512]{1,0:T(8,128)S(1)}, f32[512,128]{1,0:T(8,128)S(1)}, f32[512,128]{1,0:T(8,128)S(1)}, f32[512,128]{1,0:T(8,128)S(1)}) custom-call(s32[1]{0:T(128)} %bitcast.9.place, bf16[4,512,128]{2,1,0:T(8,128)(2,1)S(1)} %bitcast.22, bf16[4,512,128]{2,1,0:T(8,128)(2,1)S(1)} %collective-permute-done.3.refs_1_, ...), custom_call_target="tpu_custom_call" | custom-call | flops 1342177280 | bytes 5242880 | tf_op jit(solution)/shard_map/stage/pallas_call | solution.py:265
  139.7 2.2 %collective-permute-done.5.refs_0_ = bf16[4,512,128]{2,1,0:T(8,128)(2,1)S(1)} collective-permute-done((bf16[4,512,128]{2,1,0:T(8,128)(2,1)S(1)}, bf16[4,512,128]{2,1,0:T(8,128)(2,1)S(1)}, u32[]{:S(2)}, u32[]{:S(2)}) %collective-permute-start.5) | collective-permute-done | bytes 524320 | tf_op jit(solution)/shard_map/ppermute | solution.py:28
  141.9 2.8 %collective-permute-done.8.refs_1_ = bf16[4,512,128]{2,1,0:T(8,128)(2,1)S(1)} collective-permute-done((bf16[4,512,128]{2,1,0:T(8,128)(2,1)}, bf16[4,512,128]{2,1,0:T(8,128)(2,1)S(1)}, u32[]{:S(2)}, u32[]{:S(2)}) %collective-permute-start.8) | collective-permute-done | bytes 524320 | tf_op jit(solution)/shard_map/ppermute | solution.py:28
  144.7 4.2 %collective-permute-start.10 = (bf16[2,512,128]{2,1,0:T(8,128)(2,1)S(1)}, bf16[2,512,128]{2,1,0:T(8,128)(2,1)S(1)}, u32[]{:S(2)}, u32[]{:S(2)}) collective-permute-start(bf16[2,512,128]{2,1,0:T(8,128)(2,1)S(1)} %slice.7), channel_id=1, source_target_pairs={{0,31},{1,0},{2,1},{3,2},{4,3},{5,4},{6,5},{7,6},{8,7},{9,8},{10,9... | collective-permute-start | bytes 786440 | tf_op jit(solution)/shard_map/ppermute | solution.py:28
  149.0 1.9 %collective-permute-start.9 = (bf16[2,512,128]{2,1,0:T(8,128)(2,1)S(1)}, bf16[2,512,128]{2,1,0:T(8,128)(2,1)S(1)}, u32[]{:S(2)}, u32[]{:S(2)}) collective-permute-start(bf16[2,512,128]{2,1,0:T(8,128)(2,1)S(1)} %slice.6), channel_id=1, source_target_pairs={{0,1},{1,2},{2,3},{3,4},{4,5},{5,6},{6,7},{7,8},{8,9},{9,10},{10,1... | collective-permute-start | bytes 786440 | tf_op jit(solution)/shard_map/ppermute | solution.py:28
  150.9 2.2 %stage.3 = (f32[528,512]{1,0:T(8,128)S(1)}, f32[512,128]{1,0:T(8,128)S(1)}, f32[512,128]{1,0:T(8,128)S(1)}) custom-call(s32[1]{0:T(128)} %bitcast.9.place, bf16[4,512,128]{2,1,0:T(8,128)(2,1)S(1)} %collective-permute-done.5.refs_0_, bf16[4,512,128]{2,1,0:T(8,128)(2,1)S(1)} %collective-permute-done.8.refs_1_, f32[528,512]{1,0:T(8,128)S(1)} %get-tuple-element.33.refs_2_, ...), custom_call_target="tpu_custom_call" | custom-call | flops 536870912 | bytes 2097152 | tf_op jit(solution)/shard_map/stage/pallas_call | solution.py:265
  153.2 5.3 %collective-permute-done.9.refs_4_ = bf16[2,512,128]{2,1,0:T(8,128)(2,1)S(1)} collective-permute-done((bf16[2,512,128]{2,1,0:T(8,128)(2,1)S(1)}, bf16[2,512,128]{2,1,0:T(8,128)(2,1)S(1)}, u32[]{:S(2)}, u32[]{:S(2)}) %collective-permute-start.9) | collective-permute-done | bytes 262176 | tf_op jit(solution)/shard_map/ppermute | solution.py:28
  158.5 3.1 %last.1 = bf16[512,512]{1,0:T(8,128)(2,1)} custom-call(s32[1]{0:T(128)} %bitcast.9.place, f32[528,512]{1,0:T(8,128)S(1)} %get-tuple-element.37.refs_0_, f32[512,128]{1,0:T(8,128)S(1)} %get-tuple-element.34.refs_3_.refs_1_, f32[512,128]{1,0:T(8,128)S(1)} %get-tuple-element.38.refs_2_, f32[512,128]{1,0:T(8,128)S(1)} %get-tuple-element.39.refs_3_, ...), custom_call_target="tpu_custom_call" | custom-call | flops 268435456 | bytes 7340032 | tf_op jit(solution)/shard_map/last/pallas_call | solution.py:302
  (20 shorter events, 1.5 us)
Async XLA Ops:
  7.2 127.7 %all-gather.2.cloned.1.call-start = ((), (), s32[]{:S(2)}) async-start(), calls=%async_computation | async-start | bytes 4325376 | tf_op jit(solution)/shard_map/all_gather | solution.py:336
  9.3 26.9 %collective-permute-start = (bf16[1408,128]{1,0:T(8,128)(2,1)S(1)}, bf16[1408,128]{1,0:T(8,128)(2,1)S(1)}, u32[]{:S(2)}, u32[]{:S(2)}) collective-permute-start(bf16[1408,128]{1,0:T(8,128)(2,1)S(1)} %get-tuple-element.21), channel_id=1, source_target_pairs={{0,256},{256,512},{512,768},{768,0},{1,257},{257,513},{513,769},{7... | collective-permute-start | bytes 1081352 | tf_op jit(solution)/shard_map/ppermute | solution.py:28
  24.3 13.3 %collective-permute-start.1 = (bf16[1408,128]{1,0:T(8,128)(2,1)S(1)}, bf16[1408,128]{1,0:T(8,128)(2,1)S(1)}, u32[]{:S(2)}, u32[]{:S(2)}) collective-permute-start(bf16[1408,128]{1,0:T(8,128)(2,1)S(1)} %get-tuple-element.22), channel_id=1, source_target_pairs={{0,768},{256,0},{512,256},{768,512},{1,769},{257,1},{513,257},{769... | collective-permute-start | bytes 1081352 | tf_op jit(solution)/shard_map/ppermute | solution.py:28
  26.3 9.9 %collective-permute-start.2 = (bf16[1024,128]{1,0:T(8,128)(2,1)S(1)}, bf16[1024,128]{1,0:T(8,128)(2,1)S(1)}, u32[]{:S(2)}, u32[]{:S(2)}) collective-permute-start(bf16[1024,128]{1,0:T(8,128)(2,1)S(1)} %get-tuple-element.23), channel_id=1, source_target_pairs={{0,512},{256,768},{512,0},{768,256},{1,513},{257,769},{513,1},{769... | collective-permute-start | bytes 786440 | tf_op jit(solution)/shard_map/ppermute | solution.py:28
  37.7 97.1 %copy-start = (bf16[4096]{0:T(1024)(128)(2,1)S(1)}, bf16[4096]{0:T(1024)(128)(2,1)}, u32[]{:S(2)}) copy-start(bf16[4096]{0:T(1024)(128)(2,1)} %param.16) | copy-start | bytes 24580
  37.7 97.1 %copy-start.1 = (bf16[4096]{0:T(1024)(128)(2,1)S(1)}, bf16[4096]{0:T(1024)(128)(2,1)}, u32[]{:S(2)}) copy-start(bf16[4096]{0:T(1024)(128)(2,1)} %param.17) | copy-start | bytes 24580
  96.8 15.9 %collective-permute-start.3 = (bf16[4,512,128]{2,1,0:T(8,128)(2,1)S(1)}, bf16[4,512,128]{2,1,0:T(8,128)(2,1)S(1)}, u32[]{:S(2)}, u32[]{:S(2)}) collective-permute-start(bf16[4,512,128]{2,1,0:T(8,128)(2,1)S(1)} %bitcast.20), channel_id=1, source_target_pairs={{0,1},{1,2},{2,3},{3,4},{4,5},{5,6},{6,7},{7,8},{8,9},{9,10},{10,1... | collective-permute-start | bytes 1572872 | tf_op jit(solution)/shard_map/ppermute | solution.py:28
  100.7 15.5 %collective-permute-start.6 = (bf16[4,512,128]{2,1,0:T(8,128)(2,1)S(1)}, bf16[4,512,128]{2,1,0:T(8,128)(2,1)S(1)}, u32[]{:S(2)}, u32[]{:S(2)}) collective-permute-start(bf16[4,512,128]{2,1,0:T(8,128)(2,1)S(1)} %bitcast.21), channel_id=1, source_target_pairs={{0,31},{1,0},{2,1},{3,2},{4,3},{5,4},{6,5},{7,6},{8,7},{9,8},{10,9... | collective-permute-start | bytes 1572872 | tf_op jit(solution)/shard_map/ppermute | solution.py:28
  112.7 15.1 %collective-permute-start.4 = (bf16[4,512,128]{2,1,0:T(8,128)(2,1)S(1)}, bf16[4,512,128]{2,1,0:T(8,128)(2,1)S(1)}, u32[]{:S(2)}, u32[]{:S(2)}) collective-permute-start(bf16[4,512,128]{2,1,0:T(8,128)(2,1)S(1)} %collective-permute-done.3.refs_1_), channel_id=1, source_target_pairs={{0,1},{1,2},{2,3},{3,4},{4,5},{5,6},{6,7},{7,8},{8,9},{9,10},{10,1... | collective-permute-start | bytes 1572872 | tf_op jit(solution)/shard_map/ppermute | solution.py:28
  116.3 14.6 %collective-permute-start.7 = (bf16[4,512,128]{2,1,0:T(8,128)(2,1)S(1)}, bf16[4,512,128]{2,1,0:T(8,128)(2,1)}, u32[]{:S(2)}, u32[]{:S(2)}) collective-permute-start(bf16[4,512,128]{2,1,0:T(8,128)(2,1)S(1)} %collective-permute-done.6.refs_2_), channel_id=1, source_target_pairs={{0,31},{1,0},{2,1},{3,2},{4,3},{5,4},{6,5},{7,6},{8,7},{9,8},{10,9... | collective-permute-start | bytes 1572872 | tf_op jit(solution)/shard_map/ppermute | solution.py:28
  127.7 14.2 %collective-permute-start.5 = (bf16[4,512,128]{2,1,0:T(8,128)(2,1)S(1)}, bf16[4,512,128]{2,1,0:T(8,128)(2,1)S(1)}, u32[]{:S(2)}, u32[]{:S(2)}) collective-permute-start(bf16[4,512,128]{2,1,0:T(8,128)(2,1)S(1)} %collective-permute-done.4.refs_3_), channel_id=1, source_target_pairs={{0,1},{1,2},{2,3},{3,4},{4,5},{5,6},{6,7},{7,8},{8,9},{9,10},{10,1... | collective-permute-start | bytes 1572872 | tf_op jit(solution)/shard_map/ppermute | solution.py:28
  130.9 13.8 %collective-permute-start.8 = (bf16[4,512,128]{2,1,0:T(8,128)(2,1)}, bf16[4,512,128]{2,1,0:T(8,128)(2,1)S(1)}, u32[]{:S(2)}, u32[]{:S(2)}) collective-permute-start(bf16[4,512,128]{2,1,0:T(8,128)(2,1)} %collective-permute-done.7.refs_4_), channel_id=1, source_target_pairs={{0,31},{1,0},{2,1},{3,2},{4,3},{5,4},{6,5},{7,6},{8,7},{9,8},{10,9... | collective-permute-start | bytes 1572872 | tf_op jit(solution)/shard_map/ppermute | solution.py:28
  134.9 16.0 %copy-start.2 = (bf16[512]{0:T(512)(128)(2,1)S(1)}, bf16[512]{0:T(512)(128)(2,1)}, u32[]{:S(2)}) copy-start(bf16[512]{0:T(512)(128)(2,1)} %param.19) | copy-start | bytes 3076
  144.7 8.5 %collective-permute-start.10 = (bf16[2,512,128]{2,1,0:T(8,128)(2,1)S(1)}, bf16[2,512,128]{2,1,0:T(8,128)(2,1)S(1)}, u32[]{:S(2)}, u32[]{:S(2)}) collective-permute-start(bf16[2,512,128]{2,1,0:T(8,128)(2,1)S(1)} %slice.7), channel_id=1, source_target_pairs={{0,31},{1,0},{2,1},{3,2},{4,3},{5,4},{6,5},{7,6},{8,7},{9,8},{10,9... | collective-permute-start | bytes 786440 | tf_op jit(solution)/shard_map/ppermute | solution.py:28
  149.0 9.5 %collective-permute-start.9 = (bf16[2,512,128]{2,1,0:T(8,128)(2,1)S(1)}, bf16[2,512,128]{2,1,0:T(8,128)(2,1)S(1)}, u32[]{:S(2)}, u32[]{:S(2)}) collective-permute-start(bf16[2,512,128]{2,1,0:T(8,128)(2,1)S(1)} %slice.6), channel_id=1, source_target_pairs={{0,1},{1,2},{2,3},{3,4},{4,5},{5,6},{6,7},{7,8},{8,9},{9,10},{10,1... | collective-permute-start | bytes 786440 | tf_op jit(solution)/shard_map/ppermute | solution.py:28
Sparse Core Ops, SparseCore 0:
  12.9 89.0 all-gather.1

commit v3 on v2

--- a/solution.py
+++ b/solution.py
@@ -28,19 +28,47 @@
     return lax.ppermute(array, axis, [(i, (i + by) % peers) for i in range(peers)])
 
 
-def pack_kernel(place, k, v, q, x, weight_in, gain_in, kv, lower, upper, scaled, weight, gain, sems):
-    first, end = slice(0, EDGE), slice(POS - EDGE, POS)
-    moves = [(weight_in, weight), (gain_in, gain), (k, kv.at[0:POS]), (v, kv.at[POS:])]
-    for message, edge in ((lower, end), (upper, first)):
-        moves += [
-            (k, message.at[0:POS]),
-            (v, message.at[POS : 2 * POS]),
-            (q.at[edge], message.at[2 * POS : 2 * POS + EDGE]),
-            (x.at[edge], message.at[2 * POS + EDGE :]),
-        ]
-    copies = [pltpu.make_async_copy(a, b, sems.at[i]) for i, (a, b) in enumerate(moves)]
+def move(pairs, sems):
+    copies = [pltpu.make_async_copy(a, b, sems.at[i]) for i, (a, b) in enumerate(pairs)]
     for copy in copies:
         copy.start()
+    return copies
+
+
+def message_moves(k, v, q, x, message, edge):
+    return [
+        (k, message.at[0:POS]),
+        (v, message.at[POS : 2 * POS]),
+        (q.at[edge], message.at[2 * POS : 2 * POS + EDGE]),
+        (x.at[edge], message.at[2 * POS + EDGE :]),
+    ]
+
+
+def pack_kernel(k, v, q, x, qx, lower, sems):
+    own = [(q, qx.at[0:POS]), (x, qx.at[POS:])]
+    edge = slice(POS - EDGE, POS)
+    for copy in move(own + message_moves(k, v, q, x, lower, edge), sems):
+        copy.wait()
+
+
+def pack(k, v, q, x):
+    vmem, here = pl.BlockSpec(memory_space=pltpu.VMEM), pl.BlockSpec(memory_space=pltpu.HBM)
+    two = jax.ShapeDtypeStruct((2 * POS, HEAD_DIM), BF16)
+    message = jax.ShapeDtypeStruct((2 * (POS + EDGE), HEAD_DIM), BF16)
+    return pl.pallas_call(
+        pack_kernel,
+        out_shape=(two, message),
+        in_specs=[here] * 4,
+        out_specs=(vmem,) * 2,
+        scratch_shapes=[pltpu.SemaphoreType.DMA((6,))],
+        compiler_params=pltpu.CompilerParams(vmem_limit_bytes=8 << 20),
+        name="pack",
+    )(k, v, q, x)
+
+
+def scale_kernel(place, k, v, q, x, weight_in, gain_in, kv, upper, scaled, weight, gain, sems):
+    pairs = [(weight_in, weight), (gain_in, gain), (k, kv.at[0:POS]), (v, kv.at[POS:])]
+    copies = move(pairs + message_moves(k, v, q, x, upper, slice(0, EDGE)), sems)
     for copy in copies[:2]:
         copy.wait()
     depth = weight.shape[0]
@@ -54,41 +82,64 @@
         copy.wait()
 
 
-def pack(place, k, v, q, x, weight, gain):
+def scale(place, k, v, q, x, weight, gain):
     vmem, here = pl.BlockSpec(memory_space=pltpu.VMEM), pl.BlockSpec(memory_space=pltpu.HBM)
-    two = jax.ShapeDtypeStruct((2 * POS, HEAD_DIM), BF16)
     message = jax.ShapeDtypeStruct((2 * (POS + EDGE), HEAD_DIM), BF16)
     return pl.pallas_call(
-        pack_kernel,
-        out_shape=(two, message, message, jax.ShapeDtypeStruct(weight.shape, BF16)),
+        scale_kernel,
+        out_shape=(
+            jax.ShapeDtypeStruct((2 * POS, HEAD_DIM), BF16),
+            message,
+            jax.ShapeDtypeStruct(weight.shape, BF16),
+        ),
         in_specs=[pl.BlockSpec(memory_space=pltpu.SMEM)] + [here] * 6,
-        out_specs=(vmem,) * 4,
+        out_specs=(vmem,) * 3,
         scratch_shapes=[
             pltpu.VMEM(weight.shape, BF16),
             pltpu.VMEM(gain.shape, BF16),
-            pltpu.SemaphoreType.DMA((12,)),
+            pltpu.SemaphoreType.DMA((8,)),
         ],
         compiler_params=pltpu.CompilerParams(vmem_limit_bytes=8 << 20),
-        name="pack",
+        name="scale",
     )(place, k, v, q, x, weight, gain)
 
 
-def attend_kernel(place, k, v, q, x, above, below, far, taps, bias, res, conv, kv, qs, xs, image, sems):
-    middle = slice(EDGE, EDGE + POS)
-    moves = ((k, kv.at[0:POS]), (v, kv.at[POS:]), (q, qs.at[middle]), (x, xs.at[middle]))
-    copies = [pltpu.make_async_copy(a, b, sems.at[i]) for i, (a, b) in enumerate(moves)]
+def join_kernel(*refs):
+    *refs, out, sems = refs
+    count = len(refs)
+    copies = [pltpu.make_async_copy(refs[i], out.at[i], sems.at[i]) for i in range(count)]
     for copy in copies:
         copy.start()
+    for copy in copies:
+        copy.wait()
+
+
+def join(parts):
+    count, here = len(parts), pl.BlockSpec(memory_space=pltpu.HBM)
+    shape = (count,) + parts[0].shape
+    parts = [pltpu.with_memory_space_constraint(part, pltpu.HBM) for part in parts]
+    return pl.pallas_call(
+        join_kernel,
+        out_shape=pltpu.HBM(shape, BF16),
+        in_specs=[here] * count,
+        out_specs=here,
+        scratch_shapes=[pltpu.SemaphoreType.DMA((count,))],
+        cost_estimate=pl.CostEstimate(flops=0, bytes_accessed=math.prod(shape), transcendentals=0),
+        name="join",
+    )(*parts)
+
+
+def attend_kernel(place, kv, qx, above, below, far, taps, bias, res, conv, qs, xs, image):
     qs[0:EDGE] = above[2 * POS : 2 * POS + EDGE]
+    qs[EDGE : EDGE + POS] = qx[0:POS]
     qs[EDGE + POS :] = below[2 * POS : 2 * POS + EDGE]
     xs[0:EDGE] = above[2 * POS + EDGE :]
+    xs[EDGE : EDGE + POS] = qx[POS:]
     xs[EDGE + POS :] = below[2 * POS + EDGE :]
     tall = ROWS + 2 * MARGIN
     blank = jnp.zeros((tall, 8, HEAD_DIM), F32)
     image[:, 0:LEFT, :] = blank
     image[:, LEFT + IMG_W : LEFT + IMG_W + 8, :] = blank
-    for copy in copies:
-        copy.wait()
     keys = [part[0:POS] for part in (kv, above, below, far)]
     values = [part[POS : 2 * POS] for part in (kv, above, below, far)]
     to_log2 = math.log2(math.e) / math.sqrt(HEAD_DIM)
@@ -138,50 +189,68 @@
             conv[i * IMG_W + c0 : i * IMG_W + c0 + wide] = sums[i].astype(BF16)
 
 
-def attend(place, k, v, q, x, above, below, far, taps, bias):
+def attend(place, kv, qx, above, below, far, taps, bias):
     out = jax.ShapeDtypeStruct((POS, HEAD_DIM), BF16)
-    vmem, here = pl.BlockSpec(memory_space=pltpu.VMEM), pl.BlockSpec(memory_space=pltpu.HBM)
-    flops = 4 * (POS + 2 * EDGE) * SEQ * POS * HEAD_DIM
+    vmem = pl.BlockSpec(memory_space=pltpu.VMEM)
+    flops = 128 * (POS + 2 * EDGE) * SEQ * POS * HEAD_DIM
     return pl.pallas_call(
         attend_kernel,
         out_shape=(out, out),
-        in_specs=[pl.BlockSpec(memory_space=pltpu.SMEM)] + [here] * 4 + [vmem] * 5,
+        in_specs=[pl.BlockSpec(memory_space=pltpu.SMEM)] + [vmem] * 7,
         out_specs=(vmem, vmem),
         scratch_shapes=[
-            pltpu.VMEM((2 * POS, HEAD_DIM), BF16),
             pltpu.VMEM((POS + 2 * EDGE, HEAD_DIM), BF16),
             pltpu.VMEM((POS + 2 * EDGE, HEAD_DIM), BF16),
             pltpu.VMEM((ROWS + 2 * MARGIN, IMG_W + 16, HEAD_DIM), F32),
-            pltpu.SemaphoreType.DMA((4,)),
         ],
         compiler_params=pltpu.CompilerParams(vmem_limit_bytes=16 << 20),
         cost_estimate=pl.CostEstimate(flops=flops, bytes_accessed=2 << 20, transcendentals=2 << 20),
         name="attend",
-    )(place, k, v, q, x, above, below, far, taps, bias)
+    )(place, kv, qx, above, below, far, taps, bias)
 
 
 AUX = 16
 
 
-def fetch(weights, groups, slabs, sems):
+NEAR = (0, -1, 1, 2)
+PIECES = 2 * len(NEAR)
+
+
+def fetch(place, pieces, groups, slabs, sems):
+    seq, row = place[1], place[2]
+    rows = pieces[0].shape[1]
     copies = []
     for n, group in enumerate(groups):
-        rows = weights.shape[2]
-        copies.append(
+        away = lax.rem(group // 2 - row // 2 + SEQ, SEQ)
+        along_y = jnp.where(away == 3, 1, jnp.where(away == 0, 0, away + 1))
+        same = lax.rem(group, 2) == lax.rem(row, 2)
+        starts = [pl.multiple_of(lax.rem(seq + by + SEQ, SEQ) * rows, rows) for by in NEAR]
+        mine, other = (
             [
                 pltpu.make_async_copy(
-                    weights.at[j, group], slabs.at[n, j * rows : (j + 1) * rows], sems.at[n, j]
+                    piece.at[along_y], slabs.at[n, pl.ds(start, rows)], sems.at[n, i]
                 )
-                for j in range(SEQ)
+                for i, (piece, start) in enumerate(zip(half, starts))
             ]
+            for half in (pieces[: len(NEAR)], pieces[len(NEAR) :])
         )
-        for copy in copies[-1]:
-            copy.start()
+
+        @pl.when(same)
+        def _():
+            for copy in mine:
+                copy.start()
+
+        @pl.when(jnp.logical_not(same))
+        def _():
+            for copy in other:
+                copy.start()
+
+        copies.append(mine)
     return copies
 
 
-def slab_scratch(count, weights):
-    _, _, rows, columns = weights.shape
+def slab_scratch(count, pieces):
+    _, rows, columns = pieces[0].shape
     return [
         pltpu.VMEM((count, SEQ * rows, columns), BF16),
         pltpu.SemaphoreType.DMA((count, SEQ)),
@@ -225,9 +294,10 @@
 def first_kernel(offsets, place, *refs):
     count = len(offsets)
     parts, refs = refs[:count], refs[count:]
-    weights, gain, offset, acc, pivot, sum1, sum2, slabs, sems = refs
+    pieces, refs = refs[:PIECES], refs[PIECES:]
+    gain, offset, acc, pivot, sum1, sum2, slabs, sems = refs
     groups = [lax.rem(place[0] + away + CLASSES, CLASSES) for away in offsets]
-    copies = fetch(weights, groups, slabs, sems)
+    copies = fetch(place, pieces, groups, slabs, sems)
     lead = jnp.mean(parts[0][0].astype(F32), axis=1, keepdims=True)
     pivot[...] = jnp.broadcast_to(lead, (POS, HEAD_DIM))
     sum1[...] = jnp.zeros((POS, HEAD_DIM), F32)
@@ -245,9 +315,11 @@
 def more_kernel(offsets, place, *refs):
     count = len(offsets)
     parts, refs = refs[:count], refs[count:]
-    acc, pivot, sum1, sum2, weights, gain, offset, acc_out, sum1_out, sum2_out, slabs, sems = refs
+    acc, pivot, sum1, sum2, *refs = refs
+    pieces, refs = refs[:PIECES], refs[PIECES:]
+    gain, offset, acc_out, sum1_out, sum2_out, slabs, sems = refs
     groups = [lax.rem(place[0] + away + CLASSES, CLASSES) for away in offsets]
-    copies = fetch(weights, groups, slabs, sems)
+    copies = fetch(place, pieces, groups, slabs, sems)
     for n, part in enumerate(parts):
         blocks = [part.at[j] for j in range(SEQ)]
         before = (acc, sum1, sum2) if n == 0 else (acc_out, sum1_out, sum2_out)
@@ -256,9 +328,9 @@
         add_stats(blocks, pivot, before[1], before[2], sum1_out, sum2_out)
 
 
-def stage(kernel, offsets, place, parts, before, weights, gain, offset):
+def stage(kernel, offsets, place, parts, before, pieces, gain, offset):
     vmem, here = pl.BlockSpec(memory_space=pltpu.VMEM), pl.BlockSpec(memory_space=pltpu.HBM)
-    hidden = weights.shape[-1]
+    hidden = pieces[0].shape[-1]
     stat = jax.ShapeDtypeStruct((POS, HEAD_DIM), F32)
     total = jax.ShapeDtypeStruct((POS + AUX, hidden), F32)
     out_shape = (total, stat, stat) if before else (total, stat, stat, stat)
@@ -267,21 +339,23 @@
         out_shape=out_shape,
         in_specs=[pl.BlockSpec(memory_space=pltpu.SMEM)]
         + [vmem] * (len(parts) + len(before))
-        + [here, vmem, vmem],
+        + [here] * PIECES + [vmem, vmem],
         out_specs=(vmem,) * len(out_shape),
-        scratch_shapes=slab_scratch(len(parts), weights),
+        scratch_shapes=slab_scratch(len(parts), pieces),
         compiler_params=pltpu.CompilerParams(vmem_limit_bytes=16 << 20),
         cost_estimate=pl.CostEstimate(
             flops=len(parts) << 28, bytes_accessed=len(parts) << 20, transcendentals=0
         ),
         name="stage",
-    )(place, *parts, *before, weights, gain, offset)
+    )(place, *parts, *before, *pieces, gain, offset)
 
 
 def last_kernel(place, *refs):
-    acc, pivot, sum1, sum2, above, below, weights, gain, offset, bias, out, one, two, slabs, sems = refs
+    acc, pivot, sum1, sum2, above, below, *refs = refs
+    pieces, refs = refs[:PIECES], refs[PIECES:]
+    gain, offset, bias, out, one, two, slabs, sems = refs
     group = lax.rem(place[0] + 4, CLASSES)
-    (copies,) = fetch(weights, [group], slabs, sems)
+    (copies,) = fetch(place, pieces, [group], slabs, sems)
     blocks = [above.at[0], above.at[1], below.at[0], below.at[1]]
     add_stats(blocks, pivot, sum1, sum2, one, two)
     product = acc[...] + product_of(blocks, copies, slabs.at[0], gain, offset, group)
@@ -296,19 +370,19 @@
     out[...] = (0.5 * project * (1.0 + lax.erf(project * math.sqrt(0.5)))).astype(BF16)
 
 
-def last(place, acc, stats, above, below, weights, gain, offset, bias):
+def last(place, acc, stats, above, below, pieces, gain, offset, bias):
     vmem, here = pl.BlockSpec(memory_space=pltpu.VMEM), pl.BlockSpec(memory_space=pltpu.HBM)
-    hidden = weights.shape[-1]
+    hidden = pieces[0].shape[-1]
     return pl.pallas_call(
         last_kernel,
         out_shape=jax.ShapeDtypeStruct((POS, hidden), BF16),
-        in_specs=[pl.BlockSpec(memory_space=pltpu.SMEM)] + [vmem] * 6 + [here] + [vmem] * 3,
+        in_specs=[pl.BlockSpec(memory_space=pltpu.SMEM)] + [vmem] * 6 + [here] * PIECES + [vmem] * 3,
         out_specs=vmem,
-        scratch_shapes=[pltpu.VMEM((POS, HEAD_DIM), F32)] * 2 + slab_scratch(1, weights),
+        scratch_shapes=[pltpu.VMEM((POS, HEAD_DIM), F32)] * 2 + slab_scratch(1, pieces),
         compiler_params=pltpu.CompilerParams(vmem_limit_bytes=16 << 20),
         cost_estimate=pl.CostEstimate(flops=1 << 28, bytes_accessed=7 << 20, transcendentals=1 << 18),
         name="last",
-    )(place, acc, *stats, above, below, weights, gain, offset, bias)
+    )(place, acc, *stats, above, below, *pieces, gain, offset, bias)
 
 
 def on_device(
@@ -330,36 +404,41 @@
     x, q, k, v = (pltpu.with_memory_space_constraint(a, pltpu.HBM) for a in (x, q, k, v))
     mine = (seq * CLASSES + row).astype(jnp.int32).reshape(1)
     held = (pltpu.with_memory_space_constraint(a, pltpu.HBM) for a in (expand_weight, gain))
-    kv, lower, upper, scaled = pack(mine, k, v, q, x, *held)
-    far = shift(kv, "seq", 2)
-    above, below = shift(lower, "seq", 1), shift(upper, "seq", -1)
-    weights = lax.all_gather(scaled, ("seq", "row"), axis=0, tiled=True)
-    weights = weights.reshape(SEQ, CLASSES, depth, hidden)
-    weights = pltpu.with_memory_space_constraint(weights, pltpu.HBM)
+    kv, upper, scaled = scale(mine, k, v, q, x, *held)
+    far, below = shift(kv, "seq", 2), shift(upper, "seq", -1)
+    qx, lower = pack(k, v, q, x)
+    above = shift(lower, "seq", 1)
+    along_y = join([scaled] + [shift(scaled, "row", 2 * by) for by in (1, -1, 2)])
+    far, above, below, along_y = lax.optimization_barrier((far, above, below, along_y))
+    along_x = [along_y] + [shift(along_y, "seq", by) for by in (1, -1, 2)]
     gain, offset = gain.astype(F32), offset.astype(F32)
     taps = depth_weight.astype(F32).reshape(KERNEL * KERNEL, HEAD_DIM)
     bias = depth_bias.astype(F32).reshape(1, HEAD_DIM)
     residual, convolved = attend(
-        seq.astype(jnp.int32).reshape(1), k, v, q, x, above, below, far, taps, bias
+        seq.astype(jnp.int32).reshape(1), kv, qx, above, below, far, taps, bias
     )
 
     strides = [[i + CLASSES * j for j in range(SEQ)] for i in range(CLASSES)]
     own = lax.all_gather(convolved, "col", axis=0, tiled=True, axis_index_groups=strides)
     own = own.reshape(SEQ, POS, HEAD_DIM)
-    pairs, up, down = [], own, own
-    for _ in range(3):
+    own, *along_x = lax.optimization_barrier((own, *along_x))
+    swap = [(i, i ^ 1) for i in range(lax.axis_size("row"))]
+    pairs, up, down, pieces = [], own, own, []
+    for n in range(3):
         up, down = shift(up, "col", 1), shift(down, "col", -1)
+        two = [lax.ppermute(piece, "row", swap) for piece in along_x[2 * n - 2 : 2 * n]] if n else []
+        up, down, *two = lax.optimization_barrier((up, down, *two))
         pairs.append((up, down))
-    place = col.astype(jnp.int32).reshape(1)
+        pieces += two
+    pieces = [pltpu.with_memory_space_constraint(a, pltpu.HBM) for a in along_x + pieces]
+    place = jnp.stack([col, seq, row]).astype(jnp.int32)
     parts = (own, *pairs[0], *pairs[1])
-    before = stage(first_kernel, (0, -1, 1, -2, 2), place, parts, (), weights, gain, offset)
-    up, down, before = lax.optimization_barrier((up, down, before))
-    pairs[2] = (up, down)
+    before = stage(first_kernel, (0, -1, 1, -2, 2), place, parts, (), pieces, gain, offset)
     up, down = shift(up[:2], "col", 1), shift(down[2:], "col", -1)
-    acc, *sums = stage(more_kernel, (-3, 3), place, pairs[2], before, weights, gain, offset)
+    acc, *sums = stage(more_kernel, (-3, 3), place, pairs[2], before, pieces, gain, offset)
     pivot = before[1]
     bias = expand_bias.astype(F32).reshape(1, hidden)
-    out = last(place, acc, (pivot, *sums), up, down, weights, gain, offset, bias)
+    out = last(place, acc, (pivot, *sums), up, down, pieces, gain, offset, bias)
     return (
         residual.reshape(inputs.shape),
         out.reshape(inputs.shape[:3] + (hidden,)),

time: 172 us -> 191 us (1.11)
  starting transfers between devices: 47.6 us -> 76.9 us
  Pallas kernels: 17.9 us -> 35.4 us
  between operations: 14.3 us -> 1.14 us
  waiting for transfers between devices: 33.8 us -> 22.8 us
  blocking collectives: 53.3 us -> 51.3 us
    ppermute x11 -> x17, starting transfers between devices: 47.6 us -> 68.3 us  [shift(): lax.ppermute(array, axis, [(i, (i + by) % peers) for i in range(peers)])]
    pallas_call x1 -> x3, Pallas kernels: 2.06 us -> 19.4 us  [the longest x1 17 us: join(): pl.pallas_call(join_kernel, out_shape=pltpu.HBM(shape, BF16), in_specs=[h...]
    ppermute x11 -> x17, waiting for transfers between devices: 33.7 us -> 22.8 us  [shift(): lax.ppermute(array, axis, [(i, (i + by) % peers) for i in range(peers)])]
    ppermute x0 -> x4, starting transfers between devices: none -> 8.66 us  [on_device(): lax.ppermute(piece, 'row', swap)]
    all_gather x1, blocking collectives: 53.3 us -> 51.3 us  [on_device(): lax.all_gather(convolved, 'col', axis=0, tiled=True, axis_index_groups=st...]
  transfers between devices with their start and end apart: 12 -> 21, of which waited for: 7 -> 8; matrix products, arithmetic and copies ran while one was open for 1% -> 0% of each run, Pallas kernels for 8% -> 16%
where the time goes in v3:
time: 191 us; the launch traced here: 188 us
  starting transfers between devices  76.9 us (40%)
  blocking collectives  51.3 us (27%)
  Pallas kernels  35.4 us (19%)
  waiting for transfers between devices  22.8 us (12%)
    ppermute x17, starting transfers between devices, shift(): lax.ppermute(array, axis, [(i, (i + by) % peers) for i in range(peers)])  68.3 us
    all_gather x1, blocking collectives, on_device(): lax.all_gather(convolved, 'col', axis=0, tiled=True, axis_index_groups=st...  51.3 us
    ppermute x17, waiting for transfers between devices, shift(): lax.ppermute(array, axis, [(i, (i + by) % peers) for i in range(peers)])  22.8 us
    pallas_call x1, Pallas kernels, join(): pl.pallas_call(join_kernel, out_shape=pltpu.HBM(shape, BF16), in_specs=[h...  17 us
    ppermute x4, starting transfers between devices, on_device(): lax.ppermute(piece, 'row', swap)  8.66 us
    pallas_call x2, Pallas kernels, stage(): pl.pallas_call(functools.partial(kernel, offsets), out_shape=out_shape, i...  7.66 us
    pallas_call x1, Pallas kernels, attend(): pl.pallas_call(attend_kernel, out_shape=(out, out), in_specs=[pl.BlockSpe...  4.67 us
  transfers between devices with their start and end apart: 21, of which 8 were waited for; matrix products, arithmetic and copies ran while one was open for 0% of the time, Pallas kernels for 16%

profile of v3, /device:TPU:6, one launch (start us, length us, event | category | flops | bytes accessed | tf_op | source)
XLA Modules:
  0.0 188.5 jit_solution(14182673601192062327)
XLA Ops:
  1.8 15.0 %collective-permute-start.1 = (bf16[1408,128]{1,0:T(8,128)(2,1)S(1)}, bf16[1408,128]{1,0:T(8,128)(2,1)S(1)}, u32[]{:S(2)}, u32[]{:S(2)}) collective-permute-start(bf16[1408,128]{1,0:T(8,128)(2,1)S(1)} %get-tuple-element.37), channel_id=1, source_target_pairs={{0,256},{256,512},{512,768},{768,0},{1,257},{257,513},{513,769},{7... | collective-permute-start | bytes 1081352 | tf_op jit(solution)/shard_map/ppermute | solution.py:28
  22.0 3.4 %collective-permute-start = (bf16[1024,128]{1,0:T(8,128)(2,1)S(1)}, bf16[1024,128]{1,0:T(8,128)(2,1)S(1)}, u32[]{:S(2)}, u32[]{:S(2)}) collective-permute-start(bf16[1024,128]{1,0:T(8,128)(2,1)S(1)} %get-tuple-element.35.kv), channel_id=1, source_target_pairs={{0,512},{256,768},{512,0},{768,256},{1,513},{257,769},{513,1},{769... | collective-permute-start | bytes 786440 | tf_op jit(solution)/shard_map/ppermute | solution.py:28
  25.4 5.1 %collective-permute-start.4 = (bf16[128,512]{1,0:T(8,128)(2,1)S(1)}, bf16[128,512]{1,0:T(8,128)(2,1)S(1)}, u32[]{:S(2)}, u32[]{:S(2)}) collective-permute-start(bf16[128,512]{1,0:T(8,128)(2,1)S(1)} %get-tuple-element.39.refs_0_), channel_id=1, source_target_pairs={{0,192},{32,224},{64,0},{96,32},{128,64},{160,96},{192,128},{224,1... | collective-permute-start | bytes 393224 | tf_op jit(solution)/shard_map/ppermute | solution.py:28
  33.0 5.9 %collective-permute-done.5.refs_3_ = bf16[128,512]{1,0:T(8,128)(2,1)S(1)} collective-permute-done((bf16[128,512]{1,0:T(8,128)(2,1)S(1)}, bf16[128,512]{1,0:T(8,128)(2,1)S(1)}, u32[]{:S(2)}, u32[]{:S(2)}) %collective-permute-start.5) | collective-permute-done | bytes 131104 | tf_op jit(solution)/shard_map/ppermute | solution.py:28
  39.6 17.0 %join.1.refs_5_.refs_6_ = bf16[4,128,512]{2,1,0:T(8,128)(2,1)} custom-call(bf16[128,512]{1,0:T(8,128)(2,1)} %copy-done, bf16[128,512]{1,0:T(8,128)(2,1)} %copy-done.5, bf16[128,512]{1,0:T(8,128)(2,1)} %copy-done.6, bf16[128,512]{1,0:T(8,128)(2,1)} %copy-done.7), custom_call_target="tpu_custom_call" | custom-call | bytes 262144 | tf_op jit(solution)/shard_map/join/pallas_call | solution.py:121
  56.7 3.7 %collective-permute-start.6 = (bf16[4,128,512]{2,1,0:T(8,128)(2,1)}, bf16[4,128,512]{2,1,0:T(8,128)(2,1)S(1)}, u32[]{:S(2)}, u32[]{:S(2)}) collective-permute-start(bf16[4,128,512]{2,1,0:T(8,128)(2,1)} %join.1.refs_5_.refs_6_), channel_id=1, source_target_pairs={{0,256},{256,512},{512,768},{768,0},{1,257},{257,513},{513,769},{7... | collective-permute-start | bytes 1572872 | tf_op jit(solution)/shard_map/ppermute | solution.py:28
  60.4 2.8 %collective-permute-start.7 = (bf16[4,128,512]{2,1,0:T(8,128)(2,1)}, bf16[4,128,512]{2,1,0:T(8,128)(2,1)}, u32[]{:S(2)}, u32[]{:S(2)}) collective-permute-start(bf16[4,128,512]{2,1,0:T(8,128)(2,1)} %join.1.refs_5_.refs_6_), channel_id=1, source_target_pairs={{0,768},{256,0},{512,256},{768,512},{1,769},{257,1},{513,257},{769... | collective-permute-start | bytes 1572872 | tf_op jit(solution)/shard_map/ppermute | solution.py:28
  63.1 4.0 %collective-permute-start.8 = (bf16[4,128,512]{2,1,0:T(8,128)(2,1)}, bf16[4,128,512]{2,1,0:T(8,128)(2,1)}, u32[]{:S(2)}, u32[]{:S(2)}) collective-permute-start(bf16[4,128,512]{2,1,0:T(8,128)(2,1)} %join.1.refs_5_.refs_6_), channel_id=1, source_target_pairs={{0,512},{256,768},{512,0},{768,256},{1,513},{257,769},{513,1},{769... | collective-permute-start | bytes 1572872 | tf_op jit(solution)/shard_map/ppermute | solution.py:28
  67.2 4.7 %attend.1 = (bf16[512,128]{1,0:T(8,128)(2,1)}, bf16[512,128]{1,0:T(8,128)(2,1)S(1)}) custom-call(s32[1]{0:T(128)} %bitcast.place, bf16[1024,128]{1,0:T(8,128)(2,1)S(1)} %get-tuple-element.35.kv, bf16[1024,128]{1,0:T(8,128)(2,1)S(1)} %get-tuple-element.36.qx, bf16[1408,128]{1,0:T(8,128)(2,1)S(1)} %collective-permute-done.1.above, ...), custom_call_target="tpu_custom_call" | custom-call | flops 30064771072 | bytes 2097152 | tf_op jit(solution)/shard_map/attend/pallas_call | solution.py:196
  71.8 51.3 %all_gather.3 = bf16[2048,128]{1,0:T(8,128)(2,1)S(1)} all-gather(bf16[512,128]{1,0:T(8,128)(2,1)S(1)} %get-tuple-element.44), channel_id=1, replica_groups={{0,8,16,24},{1,9,17,25},{2,10,18,26},{3,11,19,27},{4,12,20,28},{5,13,21..., dimensions={0}, use_global_device_ids=true | all-gather | bytes 655360 | tf_op jit(solution)/shard_map/all_gather | solution.py:422
  123.2 4.6 %collective-permute-start.9 = (bf16[4,512,128]{2,1,0:T(8,128)(2,1)S(1)}, bf16[4,512,128]{2,1,0:T(8,128)(2,1)S(1)}, u32[]{:S(2)}, u32[]{:S(2)}) collective-permute-start(bf16[4,512,128]{2,1,0:T(8,128)(2,1)S(1)} %bitcast.20), channel_id=1, source_target_pairs={{0,1},{1,2},{2,3},{3,4},{4,5},{5,6},{6,7},{7,8},{8,9},{9,10},{10,1... | collective-permute-start | bytes 1572872 | tf_op jit(solution)/shard_map/ppermute | solution.py:28
  127.8 2.4 %collective-permute-start.10 = (bf16[4,512,128]{2,1,0:T(8,128)(2,1)S(1)}, bf16[4,512,128]{2,1,0:T(8,128)(2,1)S(1)}, u32[]{:S(2)}, u32[]{:S(2)}) collective-permute-start(bf16[4,512,128]{2,1,0:T(8,128)(2,1)S(1)} %bitcast.21), channel_id=1, source_target_pairs={{0,31},{1,0},{2,1},{3,2},{4,3},{5,4},{6,5},{7,6},{8,7},{9,8},{10,9... | collective-permute-start | bytes 1572872 | tf_op jit(solution)/shard_map/ppermute | solution.py:28
  132.2 2.4 %collective-permute-start.14 = (bf16[4,128,512]{2,1,0:T(8,128)(2,1)S(1)}, bf16[4,128,512]{2,1,0:T(8,128)(2,1)S(1)}, u32[]{:S(2)}, u32[]{:S(2)}) collective-permute-start(bf16[4,128,512]{2,1,0:T(8,128)(2,1)S(1)} %collective-permute-done.6.refs_6_.refs_7_), channel_id=1, source_target_pairs={{0,32},{32,0},{64,96},{96,64},{128,160},{160,128},{192,224},{224,1... | collective-permute-start | bytes 1572872 | tf_op jit(solution)/shard_map/ppermute | solution.py:429
  135.4 3.4 %collective-permute-done.10.refs_2_ = bf16[4,512,128]{2,1,0:T(8,128)(2,1)S(1)} collective-permute-done((bf16[4,512,128]{2,1,0:T(8,128)(2,1)S(1)}, bf16[4,512,128]{2,1,0:T(8,128)(2,1)S(1)}, u32[]{:S(2)}, u32[]{:S(2)}) %collective-permute-start.10) | collective-permute-done | bytes 524320 | tf_op jit(solution)/shard_map/ppermute | solution.py:28
  140.8 5.1 %collective-permute-start.12 = (bf16[4,512,128]{2,1,0:T(8,128)(2,1)S(1)}, bf16[4,512,128]{2,1,0:T(8,128)(2,1)}, u32[]{:S(2)}, u32[]{:S(2)}) collective-permute-start(bf16[4,512,128]{2,1,0:T(8,128)(2,1)S(1)} %collective-permute-done.10.refs_2_), channel_id=1, source_target_pairs={{0,31},{1,0},{2,1},{3,2},{4,3},{5,4},{6,5},{7,6},{8,7},{9,8},{10,9... | collective-permute-start | bytes 1572872 | tf_op jit(solution)/shard_map/ppermute | solution.py:28
  147.9 2.4 %collective-permute-start.18 = (bf16[4,128,512]{2,1,0:T(8,128)(2,1)}, bf16[4,128,512]{2,1,0:T(8,128)(2,1)}, u32[]{:S(2)}, u32[]{:S(2)}) collective-permute-start(bf16[4,128,512]{2,1,0:T(8,128)(2,1)} %collective-permute-done.8.refs_8_.refs_9_), channel_id=1, source_target_pairs={{0,32},{32,0},{64,96},{96,64},{128,160},{160,128},{192,224},{224,1... | collective-permute-start | bytes 1572872 | tf_op jit(solution)/shard_map/ppermute | solution.py:429
  151.5 2.0 %collective-permute-done.12.refs_4_ = bf16[4,512,128]{2,1,0:T(8,128)(2,1)} collective-permute-done((bf16[4,512,128]{2,1,0:T(8,128)(2,1)S(1)}, bf16[4,512,128]{2,1,0:T(8,128)(2,1)}, u32[]{:S(2)}, u32[]{:S(2)}) %collective-permute-start.12) | collective-permute-done | bytes 524320 | tf_op jit(solution)/shard_map/ppermute | solution.py:28
  153.6 2.2 %collective-permute-start.15 = (bf16[4,512,128]{2,1,0:T(8,128)(2,1)S(1)}, bf16[4,512,128]{2,1,0:T(8,128)(2,1)S(1)}, u32[]{:S(2)}, u32[]{:S(2)}) collective-permute-start(bf16[4,512,128]{2,1,0:T(8,128)(2,1)S(1)} %collective-permute-done.11.refs_3_), channel_id=1, source_target_pairs={{0,1},{1,2},{2,3},{3,4},{4,5},{5,6},{6,7},{7,8},{8,9},{9,10},{10,1... | collective-permute-start | bytes 1572872 | tf_op jit(solution)/shard_map/ppermute | solution.py:28
  155.8 4.9 %collective-permute-start.16 = (bf16[4,512,128]{2,1,0:T(8,128)(2,1)}, bf16[4,512,128]{2,1,0:T(8,128)(2,1)S(1)}, u32[]{:S(2)}, u32[]{:S(2)}) collective-permute-start(bf16[4,512,128]{2,1,0:T(8,128)(2,1)} %collective-permute-done.12.refs_4_), channel_id=1, source_target_pairs={{0,31},{1,0},{2,1},{3,2},{4,3},{5,4},{6,5},{7,6},{8,7},{9,8},{10,9... | collective-permute-start | bytes 1572872 | tf_op jit(solution)/shard_map/ppermute | solution.py:28
  160.7 7.3 %collective-permute-done.15.refs_0_ = bf16[4,512,128]{2,1,0:T(8,128)(2,1)S(1)} collective-permute-done((bf16[4,512,128]{2,1,0:T(8,128)(2,1)S(1)}, bf16[4,512,128]{2,1,0:T(8,128)(2,1)S(1)}, u32[]{:S(2)}, u32[]{:S(2)}) %collective-permute-start.15) | collective-permute-done | bytes 524320 | tf_op jit(solution)/shard_map/ppermute | solution.py:28
  171.5 5.5 %collective-permute-start.20 = (bf16[2,512,128]{2,1,0:T(8,128)(2,1)S(1)}, bf16[2,512,128]{2,1,0:T(8,128)(2,1)S(1)}, u32[]{:S(2)}, u32[]{:S(2)}) collective-permute-start(bf16[2,512,128]{2,1,0:T(8,128)(2,1)S(1)} %slice.7), channel_id=1, source_target_pairs={{0,31},{1,0},{2,1},{3,2},{4,3},{5,4},{6,5},{7,6},{8,7},{9,8},{10,9... | collective-permute-start | bytes 786440 | tf_op jit(solution)/shard_map/ppermute | solution.py:28
  177.1 4.8 %stage.2 = (f32[528,512]{1,0:T(8,128)S(1)}, f32[512,128]{1,0:T(8,128)S(1)}, f32[512,128]{1,0:T(8,128)S(1)}, f32[512,128]{1,0:T(8,128)S(1)}) custom-call(s32[3]{0:T(128)S(1)} %pad_add_fusion.place, bf16[4,512,128]{2,1,0:T(8,128)(2,1)S(1)} %bitcast.22, bf16[4,512,128]{2,1,0:T(8,128)(2,1)S(1)} %collective-permute-done.9.refs_1_, ...), custom_call_target="tpu_custom_call" | custom-call | flops 1342177280 | bytes 5242880 | tf_op jit(solution)/shard_map/stage/pallas_call | solution.py:337
  181.9 2.8 %stage.3 = (f32[528,512]{1,0:T(8,128)S(1)}, f32[512,128]{1,0:T(8,128)S(1)}, f32[512,128]{1,0:T(8,128)S(1)}) custom-call(s32[3]{0:T(128)S(1)} %pad_add_fusion.place, bf16[4,512,128]{2,1,0:T(8,128)(2,1)S(1)} %collective-permute-done.15.refs_0_, bf16[4,512,128]{2,1,0:T(8,128)(2,1)S(1)} %collective-permute-done.16.refs_1_, ...), custom_call_target="tpu_custom_call" | custom-call | flops 536870912 | bytes 2097152 | tf_op jit(solution)/shard_map/stage/pallas_call | solution.py:337
  184.8 3.7 %last.1 = bf16[512,512]{1,0:T(8,128)(2,1)} custom-call(s32[3]{0:T(128)S(1)} %pad_add_fusion.place, f32[528,512]{1,0:T(8,128)S(1)} %get-tuple-element.65.refs_0_, f32[512,128]{1,0:T(8,128)S(1)} %get-tuple-element.62.refs_3_.refs_1_, f32[512,128]{1,0:T(8,128)S(1)} %get-tuple-element.66.refs_2_, f32[512,128]{1,0:T(8,128)S(1)} %get-tuple-element.67.refs_3_, ...), custom_call_target="tpu_custom_call" | custom-call | flops 268435456 | bytes 7340032 | tf_op jit(solution)/shard_map/last/pallas_call | solution.py:376
  (60 shorter events, 20.8 us)
Async XLA Ops:
  1.8 54.8 %collective-permute-start.1 = (bf16[1408,128]{1,0:T(8,128)(2,1)S(1)}, bf16[1408,128]{1,0:T(8,128)(2,1)S(1)}, u32[]{:S(2)}, u32[]{:S(2)}) collective-permute-start(bf16[1408,128]{1,0:T(8,128)(2,1)S(1)} %get-tuple-element.37), channel_id=1, source_target_pairs={{0,256},{256,512},{512,768},{768,0},{1,257},{257,513},{513,769},{7... | collective-permute-start | bytes 1081352 | tf_op jit(solution)/shard_map/ppermute | solution.py:28
  18.1 38.5 %collective-permute-start.2 = (bf16[1408,128]{1,0:T(8,128)(2,1)S(1)}, bf16[1408,128]{1,0:T(8,128)(2,1)S(1)}, u32[]{:S(2)}, u32[]{:S(2)}) collective-permute-start(bf16[1408,128]{1,0:T(8,128)(2,1)S(1)} %get-tuple-element.38), channel_id=1, source_target_pairs={{0,768},{256,0},{512,256},{768,512},{1,769},{257,1},{513,257},{769... | collective-permute-start | bytes 1081352 | tf_op jit(solution)/shard_map/ppermute | solution.py:28
  20.1 10.5 %collective-permute-start.3 = (bf16[128,512]{1,0:T(8,128)(2,1)S(1)}, bf16[128,512]{1,0:T(8,128)(2,1)S(1)}, u32[]{:S(2)}, u32[]{:S(2)}) collective-permute-start(bf16[128,512]{1,0:T(8,128)(2,1)S(1)} %get-tuple-element.39.refs_0_), channel_id=1, source_target_pairs={{0,64},{32,96},{64,128},{96,160},{128,192},{160,224},{192,0},{224,... | collective-permute-start | bytes 393224 | tf_op jit(solution)/shard_map/ppermute | solution.py:28
  22.0 34.6 %collective-permute-start = (bf16[1024,128]{1,0:T(8,128)(2,1)S(1)}, bf16[1024,128]{1,0:T(8,128)(2,1)S(1)}, u32[]{:S(2)}, u32[]{:S(2)}) collective-permute-start(bf16[1024,128]{1,0:T(8,128)(2,1)S(1)} %get-tuple-element.35.kv), channel_id=1, source_target_pairs={{0,512},{256,768},{512,0},{768,256},{1,513},{257,769},{513,1},{769... | collective-permute-start | bytes 786440 | tf_op jit(solution)/shard_map/ppermute | solution.py:28
  25.4 7.6 %collective-permute-start.4 = (bf16[128,512]{1,0:T(8,128)(2,1)S(1)}, bf16[128,512]{1,0:T(8,128)(2,1)S(1)}, u32[]{:S(2)}, u32[]{:S(2)}) collective-permute-start(bf16[128,512]{1,0:T(8,128)(2,1)S(1)} %get-tuple-element.39.refs_0_), channel_id=1, source_target_pairs={{0,192},{32,224},{64,0},{96,32},{128,64},{160,96},{192,128},{224,1... | collective-permute-start | bytes 393224 | tf_op jit(solution)/shard_map/ppermute | solution.py:28
  30.6 8.4 %collective-permute-start.5 = (bf16[128,512]{1,0:T(8,128)(2,1)S(1)}, bf16[128,512]{1,0:T(8,128)(2,1)S(1)}, u32[]{:S(2)}, u32[]{:S(2)}) collective-permute-start(bf16[128,512]{1,0:T(8,128)(2,1)S(1)} %get-tuple-element.39.refs_0_), channel_id=1, source_target_pairs={{0,128},{32,160},{64,192},{96,224},{128,0},{160,32},{192,64},{224,... | collective-permute-start | bytes 393224 | tf_op jit(solution)/shard_map/ppermute | solution.py:28
  56.7 66.5 %collective-permute-start.6 = (bf16[4,128,512]{2,1,0:T(8,128)(2,1)}, bf16[4,128,512]{2,1,0:T(8,128)(2,1)S(1)}, u32[]{:S(2)}, u32[]{:S(2)}) collective-permute-start(bf16[4,128,512]{2,1,0:T(8,128)(2,1)} %join.1.refs_5_.refs_6_), channel_id=1, source_target_pairs={{0,256},{256,512},{512,768},{768,0},{1,257},{257,513},{513,769},{7... | collective-permute-start | bytes 1572872 | tf_op jit(solution)/shard_map/ppermute | solution.py:28
  60.4 62.8 %collective-permute-start.7 = (bf16[4,128,512]{2,1,0:T(8,128)(2,1)}, bf16[4,128,512]{2,1,0:T(8,128)(2,1)}, u32[]{:S(2)}, u32[]{:S(2)}) collective-permute-start(bf16[4,128,512]{2,1,0:T(8,128)(2,1)} %join.1.refs_5_.refs_6_), channel_id=1, source_target_pairs={{0,768},{256,0},{512,256},{768,512},{1,769},{257,1},{513,257},{769... | collective-permute-start | bytes 1572872 | tf_op jit(solution)/shard_map/ppermute | solution.py:28
  63.1 60.0 %collective-permute-start.8 = (bf16[4,128,512]{2,1,0:T(8,128)(2,1)}, bf16[4,128,512]{2,1,0:T(8,128)(2,1)}, u32[]{:S(2)}, u32[]{:S(2)}) collective-permute-start(bf16[4,128,512]{2,1,0:T(8,128)(2,1)} %join.1.refs_5_.refs_6_), channel_id=1, source_target_pairs={{0,512},{256,768},{512,0},{768,256},{1,513},{257,769},{513,1},{769... | collective-permute-start | bytes 1572872 | tf_op jit(solution)/shard_map/ppermute | solution.py:28
  67.1 93.5 %copy-start.11 = (bf16[512]{0:T(512)(128)(2,1)S(1)}, bf16[512]{0:T(512)(128)(2,1)}, u32[]{:S(2)}) copy-start(bf16[512]{0:T(512)(128)(2,1)} %param.19) | copy-start | bytes 3076
  67.1 93.5 %copy-start.8 = (bf16[4096]{0:T(1024)(128)(2,1)S(1)}, bf16[4096]{0:T(1024)(128)(2,1)}, u32[]{:S(2)}) copy-start(bf16[4096]{0:T(1024)(128)(2,1)} %param.16) | copy-start | bytes 24580
  67.2 93.5 %copy-start.10 = (bf16[4096]{0:T(1024)(128)(2,1)S(1)}, bf16[4096]{0:T(1024)(128)(2,1)}, u32[]{:S(2)}) copy-start(bf16[4096]{0:T(1024)(128)(2,1)} %param.17) | copy-start | bytes 24580
  123.2 12.3 %collective-permute-start.9 = (bf16[4,512,128]{2,1,0:T(8,128)(2,1)S(1)}, bf16[4,512,128]{2,1,0:T(8,128)(2,1)S(1)}, u32[]{:S(2)}, u32[]{:S(2)}) collective-permute-start(bf16[4,512,128]{2,1,0:T(8,128)(2,1)S(1)} %bitcast.20), channel_id=1, source_target_pairs={{0,1},{1,2},{2,3},{3,4},{4,5},{5,6},{6,7},{7,8},{8,9},{9,10},{10,1... | collective-permute-start | bytes 1572872 | tf_op jit(solution)/shard_map/ppermute | solution.py:28
  127.8 11.1 %collective-permute-start.10 = (bf16[4,512,128]{2,1,0:T(8,128)(2,1)S(1)}, bf16[4,512,128]{2,1,0:T(8,128)(2,1)S(1)}, u32[]{:S(2)}, u32[]{:S(2)}) collective-permute-start(bf16[4,512,128]{2,1,0:T(8,128)(2,1)S(1)} %bitcast.21), channel_id=1, source_target_pairs={{0,31},{1,0},{2,1},{3,2},{4,3},{5,4},{6,5},{7,6},{8,7},{9,8},{10,9... | collective-permute-start | bytes 1572872 | tf_op jit(solution)/shard_map/ppermute | solution.py:28
  130.2 17.6 %collective-permute-start.13 = (bf16[4,128,512]{2,1,0:T(8,128)(2,1)S(1)}, bf16[4,128,512]{2,1,0:T(8,128)(2,1)S(1)}, u32[]{:S(2)}, u32[]{:S(2)}) collective-permute-start(bf16[4,128,512]{2,1,0:T(8,128)(2,1)S(1)} %copy-done.1), channel_id=1, source_target_pairs={{0,32},{32,0},{64,96},{96,64},{128,160},{160,128},{192,224},{224,1... | collective-permute-start | bytes 1572872 | tf_op jit(solution)/shard_map/ppermute | solution.py:429
  132.2 18.1 %collective-permute-start.14 = (bf16[4,128,512]{2,1,0:T(8,128)(2,1)S(1)}, bf16[4,128,512]{2,1,0:T(8,128)(2,1)S(1)}, u32[]{:S(2)}, u32[]{:S(2)}) collective-permute-start(bf16[4,128,512]{2,1,0:T(8,128)(2,1)S(1)} %collective-permute-done.6.refs_6_.refs_7_), channel_id=1, source_target_pairs={{0,32},{32,0},{64,96},{96,64},{128,160},{160,128},{192,224},{224,1... | collective-permute-start | bytes 1572872 | tf_op jit(solution)/shard_map/ppermute | solution.py:429
  138.8 12.7 %collective-permute-start.11 = (bf16[4,512,128]{2,1,0:T(8,128)(2,1)S(1)}, bf16[4,512,128]{2,1,0:T(8,128)(2,1)S(1)}, u32[]{:S(2)}, u32[]{:S(2)}) collective-permute-start(bf16[4,512,128]{2,1,0:T(8,128)(2,1)S(1)} %collective-permute-done.9.refs_1_), channel_id=1, source_target_pairs={{0,1},{1,2},{2,3},{3,4},{4,5},{5,6},{6,7},{7,8},{8,9},{9,10},{10,1... | collective-permute-start | bytes 1572872 | tf_op jit(solution)/shard_map/ppermute | solution.py:28
  140.8 12.8 %collective-permute-start.12 = (bf16[4,512,128]{2,1,0:T(8,128)(2,1)S(1)}, bf16[4,512,128]{2,1,0:T(8,128)(2,1)}, u32[]{:S(2)}, u32[]{:S(2)}) collective-permute-start(bf16[4,512,128]{2,1,0:T(8,128)(2,1)S(1)} %collective-permute-done.10.refs_2_), channel_id=1, source_target_pairs={{0,31},{1,0},{2,1},{3,2},{4,3},{5,4},{6,5},{7,6},{8,7},{9,8},{10,9... | collective-permute-start | bytes 1572872 | tf_op jit(solution)/shard_map/ppermute | solution.py:28
  145.9 14.8 %collective-permute-start.17 = (bf16[4,128,512]{2,1,0:T(8,128)(2,1)}, bf16[4,128,512]{2,1,0:T(8,128)(2,1)}, u32[]{:S(2)}, u32[]{:S(2)}) collective-permute-start(bf16[4,128,512]{2,1,0:T(8,128)(2,1)} %collective-permute-done.7.refs_7_.refs_8_), channel_id=1, source_target_pairs={{0,32},{32,0},{64,96},{96,64},{128,160},{160,128},{192,224},{224,1... | collective-permute-start | bytes 1572872 | tf_op jit(solution)/shard_map/ppermute | solution.py:429
  147.9 12.9 %collective-permute-start.18 = (bf16[4,128,512]{2,1,0:T(8,128)(2,1)}, bf16[4,128,512]{2,1,0:T(8,128)(2,1)}, u32[]{:S(2)}, u32[]{:S(2)}) collective-permute-start(bf16[4,128,512]{2,1,0:T(8,128)(2,1)} %collective-permute-done.8.refs_8_.refs_9_), channel_id=1, source_target_pairs={{0,32},{32,0},{64,96},{96,64},{128,160},{160,128},{192,224},{224,1... | collective-permute-start | bytes 1572872 | tf_op jit(solution)/shard_map/ppermute | solution.py:429
  153.6 14.4 %collective-permute-start.15 = (bf16[4,512,128]{2,1,0:T(8,128)(2,1)S(1)}, bf16[4,512,128]{2,1,0:T(8,128)(2,1)S(1)}, u32[]{:S(2)}, u32[]{:S(2)}) collective-permute-start(bf16[4,512,128]{2,1,0:T(8,128)(2,1)S(1)} %collective-permute-done.11.refs_3_), channel_id=1, source_target_pairs={{0,1},{1,2},{2,3},{3,4},{4,5},{5,6},{6,7},{7,8},{8,9},{9,10},{10,1... | collective-permute-start | bytes 1572872 | tf_op jit(solution)/shard_map/ppermute | solution.py:28
  155.8 13.7 %collective-permute-start.16 = (bf16[4,512,128]{2,1,0:T(8,128)(2,1)}, bf16[4,512,128]{2,1,0:T(8,128)(2,1)S(1)}, u32[]{:S(2)}, u32[]{:S(2)}) collective-permute-start(bf16[4,512,128]{2,1,0:T(8,128)(2,1)} %collective-permute-done.12.refs_4_), channel_id=1, source_target_pairs={{0,31},{1,0},{2,1},{3,2},{4,3},{5,4},{6,5},{7,6},{8,7},{9,8},{10,9... | collective-permute-start | bytes 1572872 | tf_op jit(solution)/shard_map/ppermute | solution.py:28
  169.5 15.2 %collective-permute-start.19 = (bf16[2,512,128]{2,1,0:T(8,128)(2,1)S(1)}, bf16[2,512,128]{2,1,0:T(8,128)(2,1)S(1)}, u32[]{:S(2)}, u32[]{:S(2)}) collective-permute-start(bf16[2,512,128]{2,1,0:T(8,128)(2,1)S(1)} %slice.6), channel_id=1, source_target_pairs={{0,1},{1,2},{2,3},{3,4},{4,5},{5,6},{6,7},{7,8},{8,9},{9,10},{10,1... | collective-permute-start | bytes 786440 | tf_op jit(solution)/shard_map/ppermute | solution.py:28
  171.5 13.3 %collective-permute-start.20 = (bf16[2,512,128]{2,1,0:T(8,128)(2,1)S(1)}, bf16[2,512,128]{2,1,0:T(8,128)(2,1)S(1)}, u32[]{:S(2)}, u32[]{:S(2)}) collective-permute-start(bf16[2,512,128]{2,1,0:T(8,128)(2,1)S(1)} %slice.7), channel_id=1, source_target_pairs={{0,31},{1,0},{2,1},{3,2},{4,3},{5,4},{6,5},{7,6},{8,7},{9,8},{10,9... | collective-permute-start | bytes 786440 | tf_op jit(solution)/shard_map/ppermute | solution.py:28
  (10 other events, 198.1 us)

commit v4 on v2

--- a/solution.py
+++ b/solution.py
@@ -28,19 +28,47 @@
     return lax.ppermute(array, axis, [(i, (i + by) % peers) for i in range(peers)])
 
 
-def pack_kernel(place, k, v, q, x, weight_in, gain_in, kv, lower, upper, scaled, weight, gain, sems):
-    first, end = slice(0, EDGE), slice(POS - EDGE, POS)
-    moves = [(weight_in, weight), (gain_in, gain), (k, kv.at[0:POS]), (v, kv.at[POS:])]
-    for message, edge in ((lower, end), (upper, first)):
-        moves += [
-            (k, message.at[0:POS]),
-            (v, message.at[POS : 2 * POS]),
-            (q.at[edge], message.at[2 * POS : 2 * POS + EDGE]),
-            (x.at[edge], message.at[2 * POS + EDGE :]),
-        ]
-    copies = [pltpu.make_async_copy(a, b, sems.at[i]) for i, (a, b) in enumerate(moves)]
+def move(pairs, sems):
+    copies = [pltpu.make_async_copy(a, b, sems.at[i]) for i, (a, b) in enumerate(pairs)]
     for copy in copies:
         copy.start()
+    return copies
+
+
+def message_moves(k, v, q, x, message, edge):
+    return [
+        (k, message.at[0:POS]),
+        (v, message.at[POS : 2 * POS]),
+        (q.at[edge], message.at[2 * POS : 2 * POS + EDGE]),
+        (x.at[edge], message.at[2 * POS + EDGE :]),
+    ]
+
+
+def pack_kernel(k, v, q, x, qx, lower, sems):
+    own = [(q, qx.at[0:POS]), (x, qx.at[POS:])]
+    edge = slice(POS - EDGE, POS)
+    for copy in move(own + message_moves(k, v, q, x, lower, edge), sems):
+        copy.wait()
+
+
+def pack(k, v, q, x):
+    vmem, here = pl.BlockSpec(memory_space=pltpu.VMEM), pl.BlockSpec(memory_space=pltpu.HBM)
+    two = jax.ShapeDtypeStruct((2 * POS, HEAD_DIM), BF16)
+    message = jax.ShapeDtypeStruct((2 * (POS + EDGE), HEAD_DIM), BF16)
+    return pl.pallas_call(
+        pack_kernel,
+        out_shape=(two, message),
+        in_specs=[here] * 4,
+        out_specs=(vmem,) * 2,
+        scratch_shapes=[pltpu.SemaphoreType.DMA((6,))],
+        compiler_params=pltpu.CompilerParams(vmem_limit_bytes=8 << 20),
+        name="pack",
+    )(k, v, q, x)
+
+
+def scale_kernel(place, k, v, q, x, weight_in, gain_in, kv, upper, scaled, weight, gain, sems):
+    pairs = [(weight_in, weight), (gain_in, gain), (k, kv.at[0:POS]), (v, kv.at[POS:])]
+    copies = move(pairs + message_moves(k, v, q, x, upper, slice(0, EDGE)), sems)
     for copy in copies[:2]:
         copy.wait()
     depth = weight.shape[0]
@@ -54,63 +82,99 @@
         copy.wait()
 
 
-def pack(place, k, v, q, x, weight, gain):
+def scale(place, k, v, q, x, weight, gain):
     vmem, here = pl.BlockSpec(memory_space=pltpu.VMEM), pl.BlockSpec(memory_space=pltpu.HBM)
-    two = jax.ShapeDtypeStruct((2 * POS, HEAD_DIM), BF16)
     message = jax.ShapeDtypeStruct((2 * (POS + EDGE), HEAD_DIM), BF16)
     return pl.pallas_call(
-        pack_kernel,
-        out_shape=(two, message, message, jax.ShapeDtypeStruct(weight.shape, BF16)),
+        scale_kernel,
+        out_shape=(
+            jax.ShapeDtypeStruct((2 * POS, HEAD_DIM), BF16),
+            message,
+            jax.ShapeDtypeStruct(weight.shape, BF16),
+        ),
         in_specs=[pl.BlockSpec(memory_space=pltpu.SMEM)] + [here] * 6,
-        out_specs=(vmem,) * 4,
+        out_specs=(vmem,) * 3,
         scratch_shapes=[
             pltpu.VMEM(weight.shape, BF16),
             pltpu.VMEM(gain.shape, BF16),
-            pltpu.SemaphoreType.DMA((12,)),
+            pltpu.SemaphoreType.DMA((8,)),
         ],
         compiler_params=pltpu.CompilerParams(vmem_limit_bytes=8 << 20),
-        name="pack",
+        name="scale",
     )(place, k, v, q, x, weight, gain)
 
 
-def attend_kernel(place, k, v, q, x, above, below, far, taps, bias, res, conv, kv, qs, xs, image, sems):
-    middle = slice(EDGE, EDGE + POS)
-    moves = ((k, kv.at[0:POS]), (v, kv.at[POS:]), (q, qs.at[middle]), (x, xs.at[middle]))
-    copies = [pltpu.make_async_copy(a, b, sems.at[i]) for i, (a, b) in enumerate(moves)]
-    for copy in copies:
-        copy.start()
-    qs[0:EDGE] = above[2 * POS : 2 * POS + EDGE]
-    qs[EDGE + POS :] = below[2 * POS : 2 * POS + EDGE]
-    xs[0:EDGE] = above[2 * POS + EDGE :]
-    xs[EDGE + POS :] = below[2 * POS + EDGE :]
-    tall = ROWS + 2 * MARGIN
+TALL = ROWS + 2 * MARGIN
+TO_LOG2 = math.log2(math.e) / math.sqrt(HEAD_DIM)
+TILE = 2 * IMG_W
+
+
+def spread_rows(above, own, below, rows, at):
+    rows[0:EDGE] = above[at : at + EDGE]
+    rows[EDGE : EDGE + POS] = own
+    rows[EDGE + POS :] = below[at : at + EDGE]
+
+
+def weigh(queries, parts, peak):
+    scores = [
+        lax.dot_general(queries, part[0:POS], (((1,), (1,)), ((), ())), preferred_element_type=F32)
+        for part in parts
+    ]
+    highest = jnp.max(functools.reduce(jnp.maximum, scores), axis=1, keepdims=True)
+    if peak is not None:
+        highest = jnp.maximum(highest, peak)
+    weights = [jnp.exp2((score - highest) * TO_LOG2) for score in scores]
+    total = jnp.sum(functools.reduce(jnp.add, weights), axis=1, keepdims=True)
+    summed = functools.reduce(
+        jnp.add,
+        [
+            jnp.dot(weight.astype(BF16), part[POS : 2 * POS], preferred_element_type=F32)
+            for weight, part in zip(weights, parts)
+        ],
+    )
+    return highest, total, summed
+
+
+def near_kernel(kv, qx, above, below, summed_out, peak_out, total_out, qs):
+    spread_rows(above, qx[0:POS], below, qs, 2 * POS)
+    for t in range(TALL // 2):
+        own = slice(t * TILE, (t + 1) * TILE)
+        peak, total, summed = weigh(qs[own], (kv, above, below), None)
+        summed_out[own] = summed
+        peak_out[own] = jnp.broadcast_to(peak, summed.shape)
+        total_out[own] = jnp.broadcast_to(total, summed.shape)
+
+
+def near(kv, qx, above, below):
+    vmem = pl.BlockSpec(memory_space=pltpu.VMEM)
+    out = jax.ShapeDtypeStruct((POS + 2 * EDGE, HEAD_DIM), F32)
+    flops = 3 * (POS + 2 * EDGE) * SEQ * POS * HEAD_DIM
+    return pl.pallas_call(
+        near_kernel,
+        out_shape=(out,) * 3,
+        in_specs=[vmem] * 4,
+        out_specs=(vmem,) * 3,
+        scratch_shapes=[pltpu.VMEM((POS + 2 * EDGE, HEAD_DIM), BF16)],
+        compiler_params=pltpu.CompilerParams(vmem_limit_bytes=16 << 20),
+        cost_estimate=pl.CostEstimate(flops=flops, bytes_accessed=3 << 20, transcendentals=2 << 20),
+        name="near",
+    )(kv, qx, above, below)
+
+
+def attend_kernel(place, qx, above, below, far, summed_in, peak_in, total_in, taps, bias, res, conv, qs, xs, image):
+    spread_rows(above, qx[0:POS], below, qs, 2 * POS)
+    spread_rows(above, qx[POS:], below, xs, 2 * POS + EDGE)
+    tall = TALL
     blank = jnp.zeros((tall, 8, HEAD_DIM), F32)
     image[:, 0:LEFT, :] = blank
     image[:, LEFT + IMG_W : LEFT + IMG_W + 8, :] = blank
-    for copy in copies:
-        copy.wait()
-    keys = [part[0:POS] for part in (kv, above, below, far)]
-    values = [part[POS : 2 * POS] for part in (kv, above, below, far)]
-    to_log2 = math.log2(math.e) / math.sqrt(HEAD_DIM)
-    tile = 2 * IMG_W
     for t in range(tall // 2):
-        own = slice(t * tile, (t + 1) * tile)
-        queries = qs[own]
-        scores = [
-            lax.dot_general(queries, key, (((1,), (1,)), ((), ())), preferred_element_type=F32)
-            for key in keys
-        ]
-        peak = functools.reduce(jnp.maximum, scores)
-        peak = jnp.max(peak, axis=1, keepdims=True)
-        weights = [jnp.exp2((score - peak) * to_log2) for score in scores]
-        total = jnp.sum(functools.reduce(jnp.add, weights), axis=1, keepdims=True)
-        summed = functools.reduce(
-            jnp.add,
-            [
-                jnp.dot(weight.astype(BF16), value, preferred_element_type=F32)
-                for weight, value in zip(weights, values)
-            ],
-        )
+        own = slice(t * TILE, (t + 1) * TILE)
+        before = peak_in[own]
+        peak, total, summed = weigh(qs[own], (far,), before[:, 0:1])
+        factor = jnp.exp2((before - peak) * TO_LOG2)
+        total = total_in[own] * factor + total
+        summed = summed_in[own] * factor + summed
         out = (xs[own].astype(F32) + summed / total).astype(BF16).astype(F32)
         image[2 * t : 2 * t + 2, LEFT : LEFT + IMG_W, :] = out.reshape(2, IMG_W, HEAD_DIM)
 
@@ -138,26 +202,24 @@
             conv[i * IMG_W + c0 : i * IMG_W + c0 + wide] = sums[i].astype(BF16)
 
 
-def attend(place, k, v, q, x, above, below, far, taps, bias):
+def attend(place, qx, above, below, far, begun, taps, bias):
     out = jax.ShapeDtypeStruct((POS, HEAD_DIM), BF16)
-    vmem, here = pl.BlockSpec(memory_space=pltpu.VMEM), pl.BlockSpec(memory_space=pltpu.HBM)
-    flops = 4 * (POS + 2 * EDGE) * SEQ * POS * HEAD_DIM
+    vmem = pl.BlockSpec(memory_space=pltpu.VMEM)
+    flops = (POS + 2 * EDGE) * SEQ * POS * HEAD_DIM
     return pl.pallas_call(
         attend_kernel,
         out_shape=(out, out),
-        in_specs=[pl.BlockSpec(memory_space=pltpu.SMEM)] + [here] * 4 + [vmem] * 5,
+        in_specs=[pl.BlockSpec(memory_space=pltpu.SMEM)] + [vmem] * 9,
         out_specs=(vmem, vmem),
         scratch_shapes=[
-            pltpu.VMEM((2 * POS, HEAD_DIM), BF16),
             pltpu.VMEM((POS + 2 * EDGE, HEAD_DIM), BF16),
             pltpu.VMEM((POS + 2 * EDGE, HEAD_DIM), BF16),
-            pltpu.VMEM((ROWS + 2 * MARGIN, IMG_W + 16, HEAD_DIM), F32),
-            pltpu.SemaphoreType.DMA((4,)),
+            pltpu.VMEM((TALL, IMG_W + 16, HEAD_DIM), F32),
         ],
         compiler_params=pltpu.CompilerParams(vmem_limit_bytes=16 << 20),
-        cost_estimate=pl.CostEstimate(flops=flops, bytes_accessed=2 << 20, transcendentals=2 << 20),
+        cost_estimate=pl.CostEstimate(flops=flops, bytes_accessed=2 << 20, transcendentals=1 << 19),
         name="attend",
-    )(place, k, v, q, x, above, below, far, taps, bias)
+    )(place, qx, above, below, far, *begun, taps, bias)
 
 
 AUX = 16
@@ -330,17 +392,19 @@
     x, q, k, v = (pltpu.with_memory_space_constraint(a, pltpu.HBM) for a in (x, q, k, v))
     mine = (seq * CLASSES + row).astype(jnp.int32).reshape(1)
     held = (pltpu.with_memory_space_constraint(a, pltpu.HBM) for a in (expand_weight, gain))
-    kv, lower, upper, scaled = pack(mine, k, v, q, x, *held)
-    far = shift(kv, "seq", 2)
-    above, below = shift(lower, "seq", 1), shift(upper, "seq", -1)
+    qx, lower = pack(k, v, q, x)
+    above = shift(lower, "seq", 1)
+    kv, upper, scaled = scale(mine, k, v, q, x, *held)
+    below, far = shift(upper, "seq", -1), shift(kv, "seq", 2)
     weights = lax.all_gather(scaled, ("seq", "row"), axis=0, tiled=True)
     weights = weights.reshape(SEQ, CLASSES, depth, hidden)
     weights = pltpu.with_memory_space_constraint(weights, pltpu.HBM)
     gain, offset = gain.astype(F32), offset.astype(F32)
     taps = depth_weight.astype(F32).reshape(KERNEL * KERNEL, HEAD_DIM)
     bias = depth_bias.astype(F32).reshape(1, HEAD_DIM)
+    begun = near(kv, qx, above, below)
     residual, convolved = attend(
-        seq.astype(jnp.int32).reshape(1), k, v, q, x, above, below, far, taps, bias
+        seq.astype(jnp.int32).reshape(1), qx, above, below, far, begun, taps, bias
     )
 
     strides = [[i + CLASSES * j for j in range(SEQ)] for i in range(CLASSES)]

time: 172 us -> 170 us (0.988)
  waiting for transfers between devices: 33.8 us -> 30.1 us
  blocking collectives: 53.3 us -> 55.7 us
  Pallas kernels: 17.9 us -> 19.8 us
    pallas_call x1 -> x3, Pallas kernels: 2.06 us -> 6.17 us  [the longest x1 3.1 us: near(): pl.pallas_call(near_kernel, out_shape=(out,) * 3, in_specs=[vmem] * 4, ou...]
    ppermute x11, waiting for transfers between devices: 33.7 us -> 30 us  [shift(): lax.ppermute(array, axis, [(i, (i + by) % peers) for i in range(peers)])]
    all_gather x1, blocking collectives: 53.3 us -> 55.7 us  [on_device(): lax.all_gather(convolved, 'col', axis=0, tiled=True, axis_index_groups=st...]
    pallas_call x1, Pallas kernels: 5.73 us -> 3.45 us  [attend(): pl.pallas_call(attend_kernel, out_shape=(out, out), in_specs=[pl.BlockSpe...]
  transfers between devices with their start and end apart: 12 -> 12, of which waited for: 7 -> 8; matrix products, arithmetic and copies ran while one was open for 1% -> 0% of each run, Pallas kernels for 8% -> 9%
where the time goes in v4:
time: 170 us; the launch traced here: 168 us
  blocking collectives  55.7 us (33%)
  starting transfers between devices  48.2 us (28%)
  waiting for transfers between devices  30.1 us (18%)
  Pallas kernels  19.8 us (12%)
  between operations  14.3 us (8%)
    all_gather x1, blocking collectives, on_device(): lax.all_gather(convolved, 'col', axis=0, tiled=True, axis_index_groups=st...  55.7 us
    ppermute x11, starting transfers between devices, shift(): lax.ppermute(array, axis, [(i, (i + by) % peers) for i in range(peers)])  48.2 us
    ppermute x11, waiting for transfers between devices, shift(): lax.ppermute(array, axis, [(i, (i + by) % peers) for i in range(peers)])  30 us
    pallas_call x2, Pallas kernels, stage(): pl.pallas_call(functools.partial(kernel, offsets), out_shape=out_shape, i...  7.06 us
    pallas_call x1, Pallas kernels, attend(): pl.pallas_call(attend_kernel, out_shape=(out, out), in_specs=[pl.BlockSpe...  3.45 us
  transfers between devices with their start and end apart: 12, of which 8 were waited for; matrix products, arithmetic and copies ran while one was open for 0% of the time, Pallas kernels for 9%

profile of v4, /device:TPU:6, one launch (start us, length us, event | category | flops | bytes accessed | tf_op | source)
XLA Modules:
  0.0 168.1 jit_solution(14697485587334984443)
XLA Ops:
  7.2 1.9 %scale.1 = (bf16[1024,128]{1,0:T(8,128)(2,1)S(1)}, bf16[1408,128]{1,0:T(8,128)(2,1)S(1)}, bf16[128,512]{1,0:T(8,128)(2,1)}) custom-call(s32[1]{0:T(128)} %bitcast.5.place, bf16[512,128]{1,0:T(8,128)(2,1)} %bitcast.27, bf16[512,128]{1,0:T(8,128)(2,1)} %bitcast.29, bf16[512,128]{1,0:T(8,128)(2,1)} %bitcast.31, bf16[512,128]{1,0:T(8,128)(2,1)} %bitcast.33, ...), custom_call_target="tpu_custom_call" | custom-call | tf_op jit(solution)/shard_map/scale/pallas_call | solution.py:88
  9.2 2.7 %collective-permute-start.1 = (bf16[1408,128]{1,0:T(8,128)(2,1)S(1)}, bf16[1408,128]{1,0:T(8,128)(2,1)S(1)}, u32[]{:S(2)}, u32[]{:S(2)}) collective-permute-start(bf16[1408,128]{1,0:T(8,128)(2,1)S(1)} %get-tuple-element.27), channel_id=1, source_target_pairs={{0,768},{256,0},{512,256},{768,512},{1,769},{257,1},{513,257},{769... | collective-permute-start | bytes 1081352 | tf_op jit(solution)/shard_map/ppermute | solution.py:28
  13.1 14.2 %collective-permute-start = (bf16[1408,128]{1,0:T(8,128)(2,1)S(1)}, bf16[1408,128]{1,0:T(8,128)(2,1)S(1)}, u32[]{:S(2)}, u32[]{:S(2)}) collective-permute-start(bf16[1408,128]{1,0:T(8,128)(2,1)S(1)} %get-tuple-element.26), channel_id=1, source_target_pairs={{0,256},{256,512},{512,768},{768,0},{1,257},{257,513},{513,769},{7... | collective-permute-start | bytes 1081352 | tf_op jit(solution)/shard_map/ppermute | solution.py:28
  27.3 3.4 %collective-permute-start.2 = (bf16[1024,128]{1,0:T(8,128)(2,1)S(1)}, bf16[1024,128]{1,0:T(8,128)(2,1)S(1)}, u32[]{:S(2)}, u32[]{:S(2)}) collective-permute-start(bf16[1024,128]{1,0:T(8,128)(2,1)S(1)} %get-tuple-element.28.kv), channel_id=1, source_target_pairs={{0,512},{256,768},{512,0},{768,256},{1,513},{257,769},{513,1},{769... | collective-permute-start | bytes 786440 | tf_op jit(solution)/shard_map/ppermute | solution.py:28
  32.2 3.1 %near.1 = (f32[896,128]{1,0:T(8,128)S(1)}, f32[896,128]{1,0:T(8,128)S(1)}, f32[896,128]{1,0:T(8,128)S(1)}) custom-call(bf16[1024,128]{1,0:T(8,128)(2,1)S(1)} %get-tuple-element.28.kv, bf16[1024,128]{1,0:T(8,128)(2,1)S(1)} %get-tuple-element.25.qx, bf16[1408,128]{1,0:T(8,128)(2,1)S(1)} %collective-permute-done.above, ...), custom_call_target="tpu_custom_call" | custom-call | flops 704643072 | bytes 3145728 | tf_op jit(solution)/shard_map/near/pallas_call | solution.py:152
  35.3 1.7 %collective-permute-done.2.far = bf16[1024,128]{1,0:T(8,128)(2,1)S(1)} collective-permute-done((bf16[1024,128]{1,0:T(8,128)(2,1)S(1)}, bf16[1024,128]{1,0:T(8,128)(2,1)S(1)}, u32[]{:S(2)}, u32[]{:S(2)}) %collective-permute-start.2) | collective-permute-done | bytes 262176 | tf_op jit(solution)/shard_map/ppermute | solution.py:28
  37.1 3.4 %attend.1 = (bf16[512,128]{1,0:T(8,128)(2,1)}, bf16[512,128]{1,0:T(8,128)(2,1)S(1)}) custom-call(s32[1]{0:T(128)} %bitcast.place, bf16[1024,128]{1,0:T(8,128)(2,1)S(1)} %get-tuple-element.25.qx, bf16[1408,128]{1,0:T(8,128)(2,1)S(1)} %collective-permute-done.above, bf16[1408,128]{1,0:T(8,128)(2,1)S(1)} %collective-permute-done.1.below, ...), custom_call_target="tpu_custom_call" | custom-call | flops 234881024 | bytes 2097152 | tf_op jit(solution)/shard_map/attend/pallas_call | solution.py:209
  40.5 55.7 %all_gather.6 = bf16[2048,128]{1,0:T(8,128)(2,1)S(1)} all-gather(bf16[512,128]{1,0:T(8,128)(2,1)S(1)} %get-tuple-element.33), channel_id=1, replica_groups={{0,8,16,24},{1,9,17,25},{2,10,18,26},{3,11,19,27},{4,12,20,28},{5,13,21..., dimensions={0}, use_global_device_ids=true | all-gather | bytes 655360 | tf_op jit(solution)/shard_map/all_gather | solution.py:411
  96.2 3.3 %collective-permute-start.3 = (bf16[4,512,128]{2,1,0:T(8,128)(2,1)S(1)}, bf16[4,512,128]{2,1,0:T(8,128)(2,1)S(1)}, u32[]{:S(2)}, u32[]{:S(2)}) collective-permute-start(bf16[4,512,128]{2,1,0:T(8,128)(2,1)S(1)} %bitcast.20), channel_id=1, source_target_pairs={{0,1},{1,2},{2,3},{3,4},{4,5},{5,6},{6,7},{7,8},{8,9},{9,10},{10,1... | collective-permute-start | bytes 1572872 | tf_op jit(solution)/shard_map/ppermute | solution.py:28
  99.5 3.9 %collective-permute-start.6 = (bf16[4,512,128]{2,1,0:T(8,128)(2,1)S(1)}, bf16[4,512,128]{2,1,0:T(8,128)(2,1)S(1)}, u32[]{:S(2)}, u32[]{:S(2)}) collective-permute-start(bf16[4,512,128]{2,1,0:T(8,128)(2,1)S(1)} %bitcast.21), channel_id=1, source_target_pairs={{0,31},{1,0},{2,1},{3,2},{4,3},{5,4},{6,5},{7,6},{8,7},{9,8},{10,9... | collective-permute-start | bytes 1572872 | tf_op jit(solution)/shard_map/ppermute | solution.py:28
  103.5 6.0 %collective-permute-done.3.refs_1_ = bf16[4,512,128]{2,1,0:T(8,128)(2,1)S(1)} collective-permute-done((bf16[4,512,128]{2,1,0:T(8,128)(2,1)S(1)}, bf16[4,512,128]{2,1,0:T(8,128)(2,1)S(1)}, u32[]{:S(2)}, u32[]{:S(2)}) %collective-permute-start.3) | collective-permute-done | bytes 524320 | tf_op jit(solution)/shard_map/ppermute | solution.py:28
  109.4 4.7 %collective-permute-start.4 = (bf16[4,512,128]{2,1,0:T(8,128)(2,1)S(1)}, bf16[4,512,128]{2,1,0:T(8,128)(2,1)S(1)}, u32[]{:S(2)}, u32[]{:S(2)}) collective-permute-start(bf16[4,512,128]{2,1,0:T(8,128)(2,1)S(1)} %collective-permute-done.3.refs_1_), channel_id=1, source_target_pairs={{0,1},{1,2},{2,3},{3,4},{4,5},{5,6},{6,7},{7,8},{8,9},{9,10},{10,1... | collective-permute-start | bytes 1572872 | tf_op jit(solution)/shard_map/ppermute | solution.py:28
  114.1 2.6 %collective-permute-start.7 = (bf16[4,512,128]{2,1,0:T(8,128)(2,1)S(1)}, bf16[4,512,128]{2,1,0:T(8,128)(2,1)}, u32[]{:S(2)}, u32[]{:S(2)}) collective-permute-start(bf16[4,512,128]{2,1,0:T(8,128)(2,1)S(1)} %collective-permute-done.6.refs_2_), channel_id=1, source_target_pairs={{0,31},{1,0},{2,1},{3,2},{4,3},{5,4},{6,5},{7,6},{8,7},{9,8},{10,9... | collective-permute-start | bytes 1572872 | tf_op jit(solution)/shard_map/ppermute | solution.py:28
  116.7 8.3 %collective-permute-done.4.refs_3_ = bf16[4,512,128]{2,1,0:T(8,128)(2,1)S(1)} collective-permute-done((bf16[4,512,128]{2,1,0:T(8,128)(2,1)S(1)}, bf16[4,512,128]{2,1,0:T(8,128)(2,1)S(1)}, u32[]{:S(2)}, u32[]{:S(2)}) %collective-permute-start.4) | collective-permute-done | bytes 524320 | tf_op jit(solution)/shard_map/ppermute | solution.py:28
  125.1 5.6 %collective-permute-start.5 = (bf16[4,512,128]{2,1,0:T(8,128)(2,1)S(1)}, bf16[4,512,128]{2,1,0:T(8,128)(2,1)S(1)}, u32[]{:S(2)}, u32[]{:S(2)}) collective-permute-start(bf16[4,512,128]{2,1,0:T(8,128)(2,1)S(1)} %collective-permute-done.4.refs_3_), channel_id=1, source_target_pairs={{0,1},{1,2},{2,3},{3,4},{4,5},{5,6},{6,7},{7,8},{8,9},{9,10},{10,1... | collective-permute-start | bytes 1572872 | tf_op jit(solution)/shard_map/ppermute | solution.py:28
  130.6 1.7 %collective-permute-done.7.refs_4_ = bf16[4,512,128]{2,1,0:T(8,128)(2,1)} collective-permute-done((bf16[4,512,128]{2,1,0:T(8,128)(2,1)S(1)}, bf16[4,512,128]{2,1,0:T(8,128)(2,1)}, u32[]{:S(2)}, u32[]{:S(2)}) %collective-permute-start.7) | collective-permute-done | bytes 524320 | tf_op jit(solution)/shard_map/ppermute | solution.py:28
  132.4 1.9 %collective-permute-start.8 = (bf16[4,512,128]{2,1,0:T(8,128)(2,1)}, bf16[4,512,128]{2,1,0:T(8,128)(2,1)S(1)}, u32[]{:S(2)}, u32[]{:S(2)}) collective-permute-start(bf16[4,512,128]{2,1,0:T(8,128)(2,1)} %collective-permute-done.7.refs_4_), channel_id=1, source_target_pairs={{0,31},{1,0},{2,1},{3,2},{4,3},{5,4},{6,5},{7,6},{8,7},{9,8},{10,9... | collective-permute-start | bytes 1572872 | tf_op jit(solution)/shard_map/ppermute | solution.py:28
  134.4 4.8 %stage.2 = (f32[528,512]{1,0:T(8,128)S(1)}, f32[512,128]{1,0:T(8,128)S(1)}, f32[512,128]{1,0:T(8,128)S(1)}, f32[512,128]{1,0:T(8,128)S(1)}) custom-call(s32[1]{0:T(128)} %bitcast.9.place, bf16[4,512,128]{2,1,0:T(8,128)(2,1)S(1)} %bitcast.22, bf16[4,512,128]{2,1,0:T(8,128)(2,1)S(1)} %collective-permute-done.3.refs_1_, ...), custom_call_target="tpu_custom_call" | custom-call | flops 1342177280 | bytes 5242880 | tf_op jit(solution)/shard_map/stage/pallas_call | solution.py:327
  139.2 6.0 %collective-permute-done.8.refs_1_ = bf16[4,512,128]{2,1,0:T(8,128)(2,1)S(1)} collective-permute-done((bf16[4,512,128]{2,1,0:T(8,128)(2,1)}, bf16[4,512,128]{2,1,0:T(8,128)(2,1)S(1)}, u32[]{:S(2)}, u32[]{:S(2)}) %collective-permute-start.8) | collective-permute-done | bytes 524320 | tf_op jit(solution)/shard_map/ppermute | solution.py:28
  145.2 3.4 %collective-permute-start.10 = (bf16[2,512,128]{2,1,0:T(8,128)(2,1)S(1)}, bf16[2,512,128]{2,1,0:T(8,128)(2,1)S(1)}, u32[]{:S(2)}, u32[]{:S(2)}) collective-permute-start(bf16[2,512,128]{2,1,0:T(8,128)(2,1)S(1)} %slice.7), channel_id=1, source_target_pairs={{0,31},{1,0},{2,1},{3,2},{4,3},{5,4},{6,5},{7,6},{8,7},{9,8},{10,9... | collective-permute-start | bytes 786440 | tf_op jit(solution)/shard_map/ppermute | solution.py:28
  148.7 2.4 %collective-permute-start.9 = (bf16[2,512,128]{2,1,0:T(8,128)(2,1)S(1)}, bf16[2,512,128]{2,1,0:T(8,128)(2,1)S(1)}, u32[]{:S(2)}, u32[]{:S(2)}) collective-permute-start(bf16[2,512,128]{2,1,0:T(8,128)(2,1)S(1)} %slice.6), channel_id=1, source_target_pairs={{0,1},{1,2},{2,3},{3,4},{4,5},{5,6},{6,7},{7,8},{8,9},{9,10},{10,1... | collective-permute-start | bytes 786440 | tf_op jit(solution)/shard_map/ppermute | solution.py:28
  151.1 2.2 %stage.3 = (f32[528,512]{1,0:T(8,128)S(1)}, f32[512,128]{1,0:T(8,128)S(1)}, f32[512,128]{1,0:T(8,128)S(1)}) custom-call(s32[1]{0:T(128)} %bitcast.9.place, bf16[4,512,128]{2,1,0:T(8,128)(2,1)S(1)} %collective-permute-done.5.refs_0_, bf16[4,512,128]{2,1,0:T(8,128)(2,1)S(1)} %collective-permute-done.8.refs_1_, f32[528,512]{1,0:T(8,128)S(1)} %get-tuple-element.41.refs_2_, ...), custom_call_target="tpu_custom_call" | custom-call | flops 536870912 | bytes 2097152 | tf_op jit(solution)/shard_map/stage/pallas_call | solution.py:327
  153.5 4.7 %collective-permute-done.9.refs_4_ = bf16[2,512,128]{2,1,0:T(8,128)(2,1)S(1)} collective-permute-done((bf16[2,512,128]{2,1,0:T(8,128)(2,1)S(1)}, bf16[2,512,128]{2,1,0:T(8,128)(2,1)S(1)}, u32[]{:S(2)}, u32[]{:S(2)}) %collective-permute-start.9) | collective-permute-done | bytes 262176 | tf_op jit(solution)/shard_map/ppermute | solution.py:28
  158.2 3.1 %last.1 = bf16[512,512]{1,0:T(8,128)(2,1)} custom-call(s32[1]{0:T(128)} %bitcast.9.place, f32[528,512]{1,0:T(8,128)S(1)} %get-tuple-element.45.refs_0_, f32[512,128]{1,0:T(8,128)S(1)} %get-tuple-element.42.refs_3_.refs_1_, f32[512,128]{1,0:T(8,128)S(1)} %get-tuple-element.46.refs_2_, f32[512,128]{1,0:T(8,128)S(1)} %get-tuple-element.47.refs_3_, ...), custom_call_target="tpu_custom_call" | custom-call | flops 268435456 | bytes 7340032 | tf_op jit(solution)/shard_map/last/pallas_call | solution.py:364
  (26 shorter events, 2.9 us)
Async XLA Ops:
  7.2 23.5 %copy-start.1 = (bf16[7,7,128]{2,1,0:T(8,128)(2,1)S(1)}, bf16[7,7,128]{2,1,0:T(8,128)(2,1)}, u32[]{:S(2)}) copy-start(bf16[7,7,128]{2,1,0:T(8,128)(2,1)} %param.14) | copy-start | bytes 37636
  7.2 23.6 %copy-start.4 = (bf16[128]{0:T(256)(128)(2,1)S(1)}, bf16[128]{0:T(256)(128)(2,1)}, u32[]{:S(2)}) copy-start(bf16[128]{0:T(256)(128)(2,1)} %param.15) | copy-start | bytes 772
  7.2 127.2 %all-gather.2.cloned.1.call-start = ((), (), s32[]{:S(2)}) async-start(), calls=%async_computation | async-start | bytes 4325376 | tf_op jit(solution)/shard_map/all_gather | solution.py:399
  9.2 21.6 %collective-permute-start.1 = (bf16[1408,128]{1,0:T(8,128)(2,1)S(1)}, bf16[1408,128]{1,0:T(8,128)(2,1)S(1)}, u32[]{:S(2)}, u32[]{:S(2)}) collective-permute-start(bf16[1408,128]{1,0:T(8,128)(2,1)S(1)} %get-tuple-element.27), channel_id=1, source_target_pairs={{0,768},{256,0},{512,256},{768,512},{1,769},{257,1},{513,257},{769... | collective-permute-start | bytes 1081352 | tf_op jit(solution)/shard_map/ppermute | solution.py:28
  13.1 19.1 %collective-permute-start = (bf16[1408,128]{1,0:T(8,128)(2,1)S(1)}, bf16[1408,128]{1,0:T(8,128)(2,1)S(1)}, u32[]{:S(2)}, u32[]{:S(2)}) collective-permute-start(bf16[1408,128]{1,0:T(8,128)(2,1)S(1)} %get-tuple-element.26), channel_id=1, source_target_pairs={{0,256},{256,512},{512,768},{768,0},{1,257},{257,513},{513,769},{7... | collective-permute-start | bytes 1081352 | tf_op jit(solution)/shard_map/ppermute | solution.py:28
  27.3 9.8 %collective-permute-start.2 = (bf16[1024,128]{1,0:T(8,128)(2,1)S(1)}, bf16[1024,128]{1,0:T(8,128)(2,1)S(1)}, u32[]{:S(2)}, u32[]{:S(2)}) collective-permute-start(bf16[1024,128]{1,0:T(8,128)(2,1)S(1)} %get-tuple-element.28.kv), channel_id=1, source_target_pairs={{0,512},{256,768},{512,0},{768,256},{1,513},{257,769},{513,1},{769... | collective-permute-start | bytes 786440 | tf_op jit(solution)/shard_map/ppermute | solution.py:28
  37.1 97.2 %copy-start = (bf16[4096]{0:T(1024)(128)(2,1)S(1)}, bf16[4096]{0:T(1024)(128)(2,1)}, u32[]{:S(2)}) copy-start(bf16[4096]{0:T(1024)(128)(2,1)} %param.16) | copy-start | bytes 24580
  37.1 97.2 %copy-start.2 = (bf16[4096]{0:T(1024)(128)(2,1)S(1)}, bf16[4096]{0:T(1024)(128)(2,1)}, u32[]{:S(2)}) copy-start(bf16[4096]{0:T(1024)(128)(2,1)} %param.17) | copy-start | bytes 24580
  96.2 13.2 %collective-permute-start.3 = (bf16[4,512,128]{2,1,0:T(8,128)(2,1)S(1)}, bf16[4,512,128]{2,1,0:T(8,128)(2,1)S(1)}, u32[]{:S(2)}, u32[]{:S(2)}) collective-permute-start(bf16[4,512,128]{2,1,0:T(8,128)(2,1)S(1)} %bitcast.20), channel_id=1, source_target_pairs={{0,1},{1,2},{2,3},{3,4},{4,5},{5,6},{6,7},{7,8},{8,9},{9,10},{10,1... | collective-permute-start | bytes 1572872 | tf_op jit(solution)/shard_map/ppermute | solution.py:28
  99.5 14.6 %collective-permute-start.6 = (bf16[4,512,128]{2,1,0:T(8,128)(2,1)S(1)}, bf16[4,512,128]{2,1,0:T(8,128)(2,1)S(1)}, u32[]{:S(2)}, u32[]{:S(2)}) collective-permute-start(bf16[4,512,128]{2,1,0:T(8,128)(2,1)S(1)} %bitcast.21), channel_id=1, source_target_pairs={{0,31},{1,0},{2,1},{3,2},{4,3},{5,4},{6,5},{7,6},{8,7},{9,8},{10,9... | collective-permute-start | bytes 1572872 | tf_op jit(solution)/shard_map/ppermute | solution.py:28
  109.4 15.7 %collective-permute-start.4 = (bf16[4,512,128]{2,1,0:T(8,128)(2,1)S(1)}, bf16[4,512,128]{2,1,0:T(8,128)(2,1)S(1)}, u32[]{:S(2)}, u32[]{:S(2)}) collective-permute-start(bf16[4,512,128]{2,1,0:T(8,128)(2,1)S(1)} %collective-permute-done.3.refs_1_), channel_id=1, source_target_pairs={{0,1},{1,2},{2,3},{3,4},{4,5},{5,6},{6,7},{7,8},{8,9},{9,10},{10,1... | collective-permute-start | bytes 1572872 | tf_op jit(solution)/shard_map/ppermute | solution.py:28
  114.1 18.3 %collective-permute-start.7 = (bf16[4,512,128]{2,1,0:T(8,128)(2,1)S(1)}, bf16[4,512,128]{2,1,0:T(8,128)(2,1)}, u32[]{:S(2)}, u32[]{:S(2)}) collective-permute-start(bf16[4,512,128]{2,1,0:T(8,128)(2,1)S(1)} %collective-permute-done.6.refs_2_), channel_id=1, source_target_pairs={{0,31},{1,0},{2,1},{3,2},{4,3},{5,4},{6,5},{7,6},{8,7},{9,8},{10,9... | collective-permute-start | bytes 1572872 | tf_op jit(solution)/shard_map/ppermute | solution.py:28
  125.1 14.1 %collective-permute-start.5 = (bf16[4,512,128]{2,1,0:T(8,128)(2,1)S(1)}, bf16[4,512,128]{2,1,0:T(8,128)(2,1)S(1)}, u32[]{:S(2)}, u32[]{:S(2)}) collective-permute-start(bf16[4,512,128]{2,1,0:T(8,128)(2,1)S(1)} %collective-permute-done.4.refs_3_), channel_id=1, source_target_pairs={{0,1},{1,2},{2,3},{3,4},{4,5},{5,6},{6,7},{7,8},{8,9},{9,10},{10,1... | collective-permute-start | bytes 1572872 | tf_op jit(solution)/shard_map/ppermute | solution.py:28
  132.4 12.8 %collective-permute-start.8 = (bf16[4,512,128]{2,1,0:T(8,128)(2,1)}, bf16[4,512,128]{2,1,0:T(8,128)(2,1)S(1)}, u32[]{:S(2)}, u32[]{:S(2)}) collective-permute-start(bf16[4,512,128]{2,1,0:T(8,128)(2,1)} %collective-permute-done.7.refs_4_), channel_id=1, source_target_pairs={{0,31},{1,0},{2,1},{3,2},{4,3},{5,4},{6,5},{7,6},{8,7},{9,8},{10,9... | collective-permute-start | bytes 1572872 | tf_op jit(solution)/shard_map/ppermute | solution.py:28
  134.4 16.8 %copy-start.3 = (bf16[512]{0:T(512)(128)(2,1)S(1)}, bf16[512]{0:T(512)(128)(2,1)}, u32[]{:S(2)}) copy-start(bf16[512]{0:T(512)(128)(2,1)} %param.19) | copy-start | bytes 3076
  145.2 8.3 %collective-permute-start.10 = (bf16[2,512,128]{2,1,0:T(8,128)(2,1)S(1)}, bf16[2,512,128]{2,1,0:T(8,128)(2,1)S(1)}, u32[]{:S(2)}, u32[]{:S(2)}) collective-permute-start(bf16[2,512,128]{2,1,0:T(8,128)(2,1)S(1)} %slice.7), channel_id=1, source_target_pairs={{0,31},{1,0},{2,1},{3,2},{4,3},{5,4},{6,5},{7,6},{8,7},{9,8},{10,9... | collective-permute-start | bytes 786440 | tf_op jit(solution)/shard_map/ppermute | solution.py:28
  148.7 9.5 %collective-permute-start.9 = (bf16[2,512,128]{2,1,0:T(8,128)(2,1)S(1)}, bf16[2,512,128]{2,1,0:T(8,128)(2,1)S(1)}, u32[]{:S(2)}, u32[]{:S(2)}) collective-permute-start(bf16[2,512,128]{2,1,0:T(8,128)(2,1)S(1)} %slice.6), channel_id=1, source_target_pairs={{0,1},{1,2},{2,3},{3,4},{4,5},{5,6},{6,7},{7,8},{8,9},{9,10},{10,1... | collective-permute-start | bytes 786440 | tf_op jit(solution)/shard_map/ppermute | solution.py:28
Sparse Core Ops, SparseCore 0:
  12.9 89.0 all-gather.1

commit v5 on v4

--- a/solution.py
+++ b/solution.py
@@ -341,10 +341,10 @@
 
 
 def last_kernel(place, *refs):
-    acc, pivot, sum1, sum2, above, below, weights, gain, offset, bias, out, one, two, slabs, sems = refs
+    acc, pivot, sum1, sum2, part, weights, gain, offset, bias, out, one, two, slabs, sems = refs
     group = lax.rem(place[0] + 4, CLASSES)
     (copies,) = fetch(weights, [group], slabs, sems)
-    blocks = [above.at[0], above.at[1], below.at[0], below.at[1]]
+    blocks = [part.at[j] for j in range(SEQ)]
     add_stats(blocks, pivot, sum1, sum2, one, two)
     product = acc[...] + product_of(blocks, copies, slabs.at[0], gain, offset, group)
     mean1 = jnp.sum(one[...], axis=1, keepdims=True) * (1.0 / C)
@@ -358,19 +358,19 @@
     out[...] = (0.5 * project * (1.0 + lax.erf(project * math.sqrt(0.5)))).astype(BF16)
 
 
-def last(place, acc, stats, above, below, weights, gain, offset, bias):
+def last(place, acc, stats, part, weights, gain, offset, bias):
     vmem, here = pl.BlockSpec(memory_space=pltpu.VMEM), pl.BlockSpec(memory_space=pltpu.HBM)
     hidden = weights.shape[-1]
     return pl.pallas_call(
         last_kernel,
         out_shape=jax.ShapeDtypeStruct((POS, hidden), BF16),
-        in_specs=[pl.BlockSpec(memory_space=pltpu.SMEM)] + [vmem] * 6 + [here] + [vmem] * 3,
+        in_specs=[pl.BlockSpec(memory_space=pltpu.SMEM)] + [vmem] * 5 + [here] + [vmem] * 3,
         out_specs=vmem,
         scratch_shapes=[pltpu.VMEM((POS, HEAD_DIM), F32)] * 2 + slab_scratch(1, weights),
         compiler_params=pltpu.CompilerParams(vmem_limit_bytes=16 << 20),
         cost_estimate=pl.CostEstimate(flops=1 << 28, bytes_accessed=7 << 20, transcendentals=1 << 18),
         name="last",
-    )(place, acc, *stats, above, below, weights, gain, offset, bias)
+    )(place, acc, *stats, part, weights, gain, offset, bias)
 
 
 def on_device(
@@ -417,13 +417,13 @@
     place = col.astype(jnp.int32).reshape(1)
     parts = (own, *pairs[0], *pairs[1])
     before = stage(first_kernel, (0, -1, 1, -2, 2), place, parts, (), weights, gain, offset)
-    up, down, before = lax.optimization_barrier((up, down, before))
+    up, before = lax.optimization_barrier((up, before))
     pairs[2] = (up, down)
-    up, down = shift(up[:2], "col", 1), shift(down[2:], "col", -1)
+    up = shift(up, "col", 1)
     acc, *sums = stage(more_kernel, (-3, 3), place, pairs[2], before, weights, gain, offset)
     pivot = before[1]
     bias = expand_bias.astype(F32).reshape(1, hidden)
-    out = last(place, acc, (pivot, *sums), up, down, weights, gain, offset, bias)
+    out = last(place, acc, (pivot, *sums), up, weights, gain, offset, bias)
     return (
         residual.reshape(inputs.shape),
         out.reshape(inputs.shape[:3] + (hidden,)),

time: 170 us -> 169 us (level)
  the two profiles are of different devices: /device:TPU:6 before, /device:TPU:8 now
where the time goes in v5:
time: 169 us
  blocking collectives  58 us (34%)
  waiting for transfers between devices  39.5 us (23%)
  starting transfers between devices  37.3 us (22%)
  Pallas kernels  19.8 us (12%)
  between operations  14.3 us (8%)
    all_gather x1, blocking collectives, on_device(): lax.all_gather(convolved, 'col', axis=0, tiled=True, axis_index_groups=st...  58 us
    ppermute x10, waiting for transfers between devices, shift(): lax.ppermute(array, axis, [(i, (i + by) % peers) for i in range(peers)])  39.5 us
    ppermute x10, starting transfers between devices, shift(): lax.ppermute(array, axis, [(i, (i + by) % peers) for i in range(peers)])  37.2 us
    pallas_call x2, Pallas kernels, stage(): pl.pallas_call(functools.partial(kernel, offsets), out_shape=out_shape, i...  7.04 us
    pallas_call x1, Pallas kernels, attend(): pl.pallas_call(attend_kernel, out_shape=(out, out), in_specs=[pl.BlockSpe...  3.45 us
  transfers between devices with their start and end apart: 11, of which 7 were waited for; matrix products, arithmetic and copies ran while one was open for 0% of the time, Pallas kernels for 9%

profile of v5, /device:TPU:8, one launch (start us, length us, event | category | flops | bytes accessed | tf_op | source)
XLA Modules:
  0.0 169.0 jit_solution(13620598836545143750)
XLA Ops:
  7.2 1.9 %scale.1 = (bf16[1024,128]{1,0:T(8,128)(2,1)S(1)}, bf16[1408,128]{1,0:T(8,128)(2,1)S(1)}, bf16[128,512]{1,0:T(8,128)(2,1)}) custom-call(s32[1]{0:T(128)} %bitcast.5.place, bf16[512,128]{1,0:T(8,128)(2,1)} %bitcast.27, bf16[512,128]{1,0:T(8,128)(2,1)} %bitcast.29, bf16[512,128]{1,0:T(8,128)(2,1)} %bitcast.31, bf16[512,128]{1,0:T(8,128)(2,1)} %bitcast.33, ...), custom_call_target="tpu_custom_call" | custom-call | tf_op jit(solution)/shard_map/scale/pallas_call | solution.py:88
  9.2 4.7 %collective-permute-start.1 = (bf16[1408,128]{1,0:T(8,128)(2,1)S(1)}, bf16[1408,128]{1,0:T(8,128)(2,1)S(1)}, u32[]{:S(2)}, u32[]{:S(2)}) collective-permute-start(bf16[1408,128]{1,0:T(8,128)(2,1)S(1)} %get-tuple-element.26), channel_id=1, source_target_pairs={{0,768},{256,0},{512,256},{768,512},{1,769},{257,1},{513,257},{769... | collective-permute-start | bytes 1081352 | tf_op jit(solution)/shard_map/ppermute | solution.py:28
  13.9 1.2 pack.1
  15.0 1.9 %collective-permute-start = (bf16[1408,128]{1,0:T(8,128)(2,1)S(1)}, bf16[1408,128]{1,0:T(8,128)(2,1)S(1)}, u32[]{:S(2)}, u32[]{:S(2)}) collective-permute-start(bf16[1408,128]{1,0:T(8,128)(2,1)S(1)} %get-tuple-element.25), channel_id=1, source_target_pairs={{0,256},{256,512},{512,768},{768,0},{1,257},{257,513},{513,769},{7... | collective-permute-start | bytes 1081352 | tf_op jit(solution)/shard_map/ppermute | solution.py:28
  16.9 4.2 %collective-permute-start.2 = (bf16[1024,128]{1,0:T(8,128)(2,1)S(1)}, bf16[1024,128]{1,0:T(8,128)(2,1)S(1)}, u32[]{:S(2)}, u32[]{:S(2)}) collective-permute-start(bf16[1024,128]{1,0:T(8,128)(2,1)S(1)} %get-tuple-element.27.kv), channel_id=1, source_target_pairs={{0,512},{256,768},{512,0},{768,256},{1,513},{257,769},{513,1},{769... | collective-permute-start | bytes 786440 | tf_op jit(solution)/shard_map/ppermute | solution.py:28
  21.2 0.3 collective-permute-done.1.below
  21.5 12.1 %collective-permute-done.above = bf16[1408,128]{1,0:T(8,128)(2,1)S(1)} collective-permute-done((bf16[1408,128]{1,0:T(8,128)(2,1)S(1)}, bf16[1408,128]{1,0:T(8,128)(2,1)S(1)}, u32[]{:S(2)}, u32[]{:S(2)}) %collective-permute-start) | collective-permute-done | bytes 360480 | tf_op jit(solution)/shard_map/ppermute | solution.py:28
  33.6 3.1 %near.1 = (f32[896,128]{1,0:T(8,128)S(1)}, f32[896,128]{1,0:T(8,128)S(1)}, f32[896,128]{1,0:T(8,128)S(1)}) custom-call(bf16[1024,128]{1,0:T(8,128)(2,1)S(1)} %get-tuple-element.27.kv, bf16[1024,128]{1,0:T(8,128)(2,1)S(1)} %get-tuple-element.24.qx, bf16[1408,128]{1,0:T(8,128)(2,1)S(1)} %collective-permute-done.above, ...), custom_call_target="tpu_custom_call" | custom-call | flops 704643072 | bytes 3145728 | tf_op jit(solution)/shard_map/near/pallas_call | solution.py:152
  36.8 3.5 %attend.1 = (bf16[512,128]{1,0:T(8,128)(2,1)}, bf16[512,128]{1,0:T(8,128)(2,1)S(1)}) custom-call(s32[1]{0:T(128)} %bitcast.place, bf16[1024,128]{1,0:T(8,128)(2,1)S(1)} %get-tuple-element.24.qx, bf16[1408,128]{1,0:T(8,128)(2,1)S(1)} %collective-permute-done.above, bf16[1408,128]{1,0:T(8,128)(2,1)S(1)} %collective-permute-done.1.below, ...), custom_call_target="tpu_custom_call" | custom-call | flops 234881024 | bytes 2097152 | tf_op jit(solution)/shard_map/attend/pallas_call | solution.py:209
  40.2 58.0 %all_gather.6 = bf16[2048,128]{1,0:T(8,128)(2,1)S(1)} all-gather(bf16[512,128]{1,0:T(8,128)(2,1)S(1)} %get-tuple-element.32), channel_id=1, replica_groups={{0,8,16,24},{1,9,17,25},{2,10,18,26},{3,11,19,27},{4,12,20,28},{5,13,21..., dimensions={0}, use_global_device_ids=true | all-gather | bytes 655360 | tf_op jit(solution)/shard_map/all_gather | solution.py:411
  98.2 2.1 %collective-permute-start.3 = (bf16[4,512,128]{2,1,0:T(8,128)(2,1)S(1)}, bf16[4,512,128]{2,1,0:T(8,128)(2,1)S(1)}, u32[]{:S(2)}, u32[]{:S(2)}) collective-permute-start(bf16[4,512,128]{2,1,0:T(8,128)(2,1)S(1)} %bitcast.20), channel_id=1, source_target_pairs={{0,1},{1,2},{2,3},{3,4},{4,5},{5,6},{6,7},{7,8},{8,9},{9,10},{10,1... | collective-permute-start | bytes 1572872 | tf_op jit(solution)/shard_map/ppermute | solution.py:28
  100.3 5.0 %collective-permute-start.6 = (bf16[4,512,128]{2,1,0:T(8,128)(2,1)S(1)}, bf16[4,512,128]{2,1,0:T(8,128)(2,1)S(1)}, u32[]{:S(2)}, u32[]{:S(2)}) collective-permute-start(bf16[4,512,128]{2,1,0:T(8,128)(2,1)S(1)} %bitcast.21), channel_id=1, source_target_pairs={{0,31},{1,0},{2,1},{3,2},{4,3},{5,4},{6,5},{7,6},{8,7},{9,8},{10,9... | collective-permute-start | bytes 1572872 | tf_op jit(solution)/shard_map/ppermute | solution.py:28
  105.3 5.8 %collective-permute-done.3.refs_1_ = bf16[4,512,128]{2,1,0:T(8,128)(2,1)S(1)} collective-permute-done((bf16[4,512,128]{2,1,0:T(8,128)(2,1)S(1)}, bf16[4,512,128]{2,1,0:T(8,128)(2,1)S(1)}, u32[]{:S(2)}, u32[]{:S(2)}) %collective-permute-start.3) | collective-permute-done | bytes 524320 | tf_op jit(solution)/shard_map/ppermute | solution.py:28
  111.0 1.9 %collective-permute-start.4 = (bf16[4,512,128]{2,1,0:T(8,128)(2,1)S(1)}, bf16[4,512,128]{2,1,0:T(8,128)(2,1)}, u32[]{:S(2)}, u32[]{:S(2)}) collective-permute-start(bf16[4,512,128]{2,1,0:T(8,128)(2,1)S(1)} %collective-permute-done.3.refs_1_), channel_id=1, source_target_pairs={{0,1},{1,2},{2,3},{3,4},{4,5},{5,6},{6,7},{7,8},{8,9},{9,10},{10,1... | collective-permute-start | bytes 1572872 | tf_op jit(solution)/shard_map/ppermute | solution.py:28
  113.0 5.4 %collective-permute-start.7 = (bf16[4,512,128]{2,1,0:T(8,128)(2,1)S(1)}, bf16[4,512,128]{2,1,0:T(8,128)(2,1)S(1)}, u32[]{:S(2)}, u32[]{:S(2)}) collective-permute-start(bf16[4,512,128]{2,1,0:T(8,128)(2,1)S(1)} %collective-permute-done.6.refs_2_), channel_id=1, source_target_pairs={{0,31},{1,0},{2,1},{3,2},{4,3},{5,4},{6,5},{7,6},{8,7},{9,8},{10,9... | collective-permute-start | bytes 1572872 | tf_op jit(solution)/shard_map/ppermute | solution.py:28
  118.4 6.4 %collective-permute-done.4.refs_3_ = bf16[4,512,128]{2,1,0:T(8,128)(2,1)} collective-permute-done((bf16[4,512,128]{2,1,0:T(8,128)(2,1)S(1)}, bf16[4,512,128]{2,1,0:T(8,128)(2,1)}, u32[]{:S(2)}, u32[]{:S(2)}) %collective-permute-start.4) | collective-permute-done | bytes 524320 | tf_op jit(solution)/shard_map/ppermute | solution.py:28
  124.7 1.9 %collective-permute-start.5 = (bf16[4,512,128]{2,1,0:T(8,128)(2,1)}, bf16[4,512,128]{2,1,0:T(8,128)(2,1)S(1)}, u32[]{:S(2)}, u32[]{:S(2)}) collective-permute-start(bf16[4,512,128]{2,1,0:T(8,128)(2,1)} %collective-permute-done.4.refs_3_), channel_id=1, source_target_pairs={{0,1},{1,2},{2,3},{3,4},{4,5},{5,6},{6,7},{7,8},{8,9},{9,10},{10,1... | collective-permute-start | bytes 1572872 | tf_op jit(solution)/shard_map/ppermute | solution.py:28
  126.9 8.3 %collective-permute-start.8 = (bf16[4,512,128]{2,1,0:T(8,128)(2,1)S(1)}, bf16[4,512,128]{2,1,0:T(8,128)(2,1)S(1)}, u32[]{:S(2)}, u32[]{:S(2)}) collective-permute-start(bf16[4,512,128]{2,1,0:T(8,128)(2,1)S(1)} %collective-permute-done.7.refs_4_), channel_id=1, source_target_pairs={{0,31},{1,0},{2,1},{3,2},{4,3},{5,4},{6,5},{7,6},{8,7},{9,8},{10,9... | collective-permute-start | bytes 1572872 | tf_op jit(solution)/shard_map/ppermute | solution.py:28
  135.3 4.8 %stage.2 = (f32[528,512]{1,0:T(8,128)S(1)}, f32[512,128]{1,0:T(8,128)S(1)}, f32[512,128]{1,0:T(8,128)S(1)}, f32[512,128]{1,0:T(8,128)S(1)}) custom-call(s32[1]{0:T(128)} %bitcast.9.place, bf16[4,512,128]{2,1,0:T(8,128)(2,1)S(1)} %bitcast.22, bf16[4,512,128]{2,1,0:T(8,128)(2,1)S(1)} %collective-permute-done.3.refs_1_, ...), custom_call_target="tpu_custom_call" | custom-call | flops 1342177280 | bytes 5242880 | tf_op jit(solution)/shard_map/stage/pallas_call | solution.py:327
  140.1 6.0 %collective-permute-done.5.refs_0_ = bf16[4,512,128]{2,1,0:T(8,128)(2,1)S(1)} collective-permute-done((bf16[4,512,128]{2,1,0:T(8,128)(2,1)}, bf16[4,512,128]{2,1,0:T(8,128)(2,1)S(1)}, u32[]{:S(2)}, u32[]{:S(2)}) %collective-permute-start.5) | collective-permute-done | bytes 524320 | tf_op jit(solution)/shard_map/ppermute | solution.py:28
  146.1 1.9 %collective-permute-start.9 = (bf16[4,512,128]{2,1,0:T(8,128)(2,1)S(1)}, bf16[4,512,128]{2,1,0:T(8,128)(2,1)S(1)}, u32[]{:S(2)}, u32[]{:S(2)}) collective-permute-start(bf16[4,512,128]{2,1,0:T(8,128)(2,1)S(1)} %collective-permute-done.5.refs_0_), channel_id=1, source_target_pairs={{0,1},{1,2},{2,3},{3,4},{4,5},{5,6},{6,7},{7,8},{8,9},{9,10},{10,1... | collective-permute-start | bytes 1572872 | tf_op jit(solution)/shard_map/ppermute | solution.py:28
  148.1 2.2 %stage.3 = (f32[528,512]{1,0:T(8,128)S(1)}, f32[512,128]{1,0:T(8,128)S(1)}, f32[512,128]{1,0:T(8,128)S(1)}) custom-call(s32[1]{0:T(128)} %bitcast.9.place, bf16[4,512,128]{2,1,0:T(8,128)(2,1)S(1)} %collective-permute-done.5.refs_0_, bf16[4,512,128]{2,1,0:T(8,128)(2,1)S(1)} %collective-permute-done.8.refs_1_, f32[528,512]{1,0:T(8,128)S(1)} %get-tuple-element.39.refs_2_, ...), custom_call_target="tpu_custom_call" | custom-call | flops 536870912 | bytes 2097152 | tf_op jit(solution)/shard_map/stage/pallas_call | solution.py:327
  150.3 8.6 %collective-permute-done.9.refs_4_ = bf16[4,512,128]{2,1,0:T(8,128)(2,1)S(1)} collective-permute-done((bf16[4,512,128]{2,1,0:T(8,128)(2,1)S(1)}, bf16[4,512,128]{2,1,0:T(8,128)(2,1)S(1)}, u32[]{:S(2)}, u32[]{:S(2)}) %collective-permute-start.9) | collective-permute-done | bytes 524320 | tf_op jit(solution)/shard_map/ppermute | solution.py:28
  159.0 3.1 %last.1 = bf16[512,512]{1,0:T(8,128)(2,1)} custom-call(s32[1]{0:T(128)} %bitcast.9.place, f32[528,512]{1,0:T(8,128)S(1)} %get-tuple-element.43.refs_0_, f32[512,128]{1,0:T(8,128)S(1)} %get-tuple-element.40.refs_3_.refs_1_, f32[512,128]{1,0:T(8,128)S(1)} %get-tuple-element.44.refs_2_, f32[512,128]{1,0:T(8,128)S(1)} %get-tuple-element.45.refs_3_, ...), custom_call_target="tpu_custom_call" | custom-call | flops 268435456 | bytes 7340032 | tf_op jit(solution)/shard_map/last/pallas_call | solution.py:364
  (22 shorter events, 0.4 us)
Async XLA Ops:
  7.2 14.0 %copy-start.1 = (bf16[7,7,128]{2,1,0:T(8,128)(2,1)S(1)}, bf16[7,7,128]{2,1,0:T(8,128)(2,1)}, u32[]{:S(2)}) copy-start(bf16[7,7,128]{2,1,0:T(8,128)(2,1)} %param.14) | copy-start | bytes 37636
  7.2 14.0 %copy-start.4 = (bf16[128]{0:T(256)(128)(2,1)S(1)}, bf16[128]{0:T(256)(128)(2,1)}, u32[]{:S(2)}) copy-start(bf16[128]{0:T(256)(128)(2,1)} %param.15) | copy-start | bytes 772
  7.2 128.1 %all-gather.2.cloned.1.call-start = ((), (), s32[]{:S(2)}) async-start(), calls=%async_computation | async-start | bytes 4325376 | tf_op jit(solution)/shard_map/all_gather | solution.py:399
  9.2 12.3 %collective-permute-start.1 = (bf16[1408,128]{1,0:T(8,128)(2,1)S(1)}, bf16[1408,128]{1,0:T(8,128)(2,1)S(1)}, u32[]{:S(2)}, u32[]{:S(2)}) collective-permute-start(bf16[1408,128]{1,0:T(8,128)(2,1)S(1)} %get-tuple-element.26), channel_id=1, source_target_pairs={{0,768},{256,0},{512,256},{768,512},{1,769},{257,1},{513,257},{769... | collective-permute-start | bytes 1081352 | tf_op jit(solution)/shard_map/ppermute | solution.py:28
  15.0 18.6 %collective-permute-start = (bf16[1408,128]{1,0:T(8,128)(2,1)S(1)}, bf16[1408,128]{1,0:T(8,128)(2,1)S(1)}, u32[]{:S(2)}, u32[]{:S(2)}) collective-permute-start(bf16[1408,128]{1,0:T(8,128)(2,1)S(1)} %get-tuple-element.25), channel_id=1, source_target_pairs={{0,256},{256,512},{512,768},{768,0},{1,257},{257,513},{513,769},{7... | collective-permute-start | bytes 1081352 | tf_op jit(solution)/shard_map/ppermute | solution.py:28
  16.9 19.8 %collective-permute-start.2 = (bf16[1024,128]{1,0:T(8,128)(2,1)S(1)}, bf16[1024,128]{1,0:T(8,128)(2,1)S(1)}, u32[]{:S(2)}, u32[]{:S(2)}) collective-permute-start(bf16[1024,128]{1,0:T(8,128)(2,1)S(1)} %get-tuple-element.27.kv), channel_id=1, source_target_pairs={{0,512},{256,768},{512,0},{768,256},{1,513},{257,769},{513,1},{769... | collective-permute-start | bytes 786440 | tf_op jit(solution)/shard_map/ppermute | solution.py:28
  36.7 89.9 %copy-start = (bf16[4096]{0:T(1024)(128)(2,1)S(1)}, bf16[4096]{0:T(1024)(128)(2,1)}, u32[]{:S(2)}) copy-start(bf16[4096]{0:T(1024)(128)(2,1)} %param.16) | copy-start | bytes 24580
  36.7 89.9 %copy-start.2 = (bf16[4096]{0:T(1024)(128)(2,1)S(1)}, bf16[4096]{0:T(1024)(128)(2,1)}, u32[]{:S(2)}) copy-start(bf16[4096]{0:T(1024)(128)(2,1)} %param.17) | copy-start | bytes 24580
  98.2 12.8 %collective-permute-start.3 = (bf16[4,512,128]{2,1,0:T(8,128)(2,1)S(1)}, bf16[4,512,128]{2,1,0:T(8,128)(2,1)S(1)}, u32[]{:S(2)}, u32[]{:S(2)}) collective-permute-start(bf16[4,512,128]{2,1,0:T(8,128)(2,1)S(1)} %bitcast.20), channel_id=1, source_target_pairs={{0,1},{1,2},{2,3},{3,4},{4,5},{5,6},{6,7},{7,8},{8,9},{9,10},{10,1... | collective-permute-start | bytes 1572872 | tf_op jit(solution)/shard_map/ppermute | solution.py:28
  100.3 12.7 %collective-permute-start.6 = (bf16[4,512,128]{2,1,0:T(8,128)(2,1)S(1)}, bf16[4,512,128]{2,1,0:T(8,128)(2,1)S(1)}, u32[]{:S(2)}, u32[]{:S(2)}) collective-permute-start(bf16[4,512,128]{2,1,0:T(8,128)(2,1)S(1)} %bitcast.21), channel_id=1, source_target_pairs={{0,31},{1,0},{2,1},{3,2},{4,3},{5,4},{6,5},{7,6},{8,7},{9,8},{10,9... | collective-permute-start | bytes 1572872 | tf_op jit(solution)/shard_map/ppermute | solution.py:28
  111.0 13.7 %collective-permute-start.4 = (bf16[4,512,128]{2,1,0:T(8,128)(2,1)S(1)}, bf16[4,512,128]{2,1,0:T(8,128)(2,1)}, u32[]{:S(2)}, u32[]{:S(2)}) collective-permute-start(bf16[4,512,128]{2,1,0:T(8,128)(2,1)S(1)} %collective-permute-done.3.refs_1_), channel_id=1, source_target_pairs={{0,1},{1,2},{2,3},{3,4},{4,5},{5,6},{6,7},{7,8},{8,9},{9,10},{10,1... | collective-permute-start | bytes 1572872 | tf_op jit(solution)/shard_map/ppermute | solution.py:28
  113.0 14.0 %collective-permute-start.7 = (bf16[4,512,128]{2,1,0:T(8,128)(2,1)S(1)}, bf16[4,512,128]{2,1,0:T(8,128)(2,1)S(1)}, u32[]{:S(2)}, u32[]{:S(2)}) collective-permute-start(bf16[4,512,128]{2,1,0:T(8,128)(2,1)S(1)} %collective-permute-done.6.refs_2_), channel_id=1, source_target_pairs={{0,31},{1,0},{2,1},{3,2},{4,3},{5,4},{6,5},{7,6},{8,7},{9,8},{10,9... | collective-permute-start | bytes 1572872 | tf_op jit(solution)/shard_map/ppermute | solution.py:28
  124.7 21.4 %collective-permute-start.5 = (bf16[4,512,128]{2,1,0:T(8,128)(2,1)}, bf16[4,512,128]{2,1,0:T(8,128)(2,1)S(1)}, u32[]{:S(2)}, u32[]{:S(2)}) collective-permute-start(bf16[4,512,128]{2,1,0:T(8,128)(2,1)} %collective-permute-done.4.refs_3_), channel_id=1, source_target_pairs={{0,1},{1,2},{2,3},{3,4},{4,5},{5,6},{6,7},{7,8},{8,9},{9,10},{10,1... | collective-permute-start | bytes 1572872 | tf_op jit(solution)/shard_map/ppermute | solution.py:28
  126.9 21.1 %collective-permute-start.8 = (bf16[4,512,128]{2,1,0:T(8,128)(2,1)S(1)}, bf16[4,512,128]{2,1,0:T(8,128)(2,1)S(1)}, u32[]{:S(2)}, u32[]{:S(2)}) collective-permute-start(bf16[4,512,128]{2,1,0:T(8,128)(2,1)S(1)} %collective-permute-done.7.refs_4_), channel_id=1, source_target_pairs={{0,31},{1,0},{2,1},{3,2},{4,3},{5,4},{6,5},{7,6},{8,7},{9,8},{10,9... | collective-permute-start | bytes 1572872 | tf_op jit(solution)/shard_map/ppermute | solution.py:28
  135.3 12.8 %copy-start.3 = (bf16[512]{0:T(512)(128)(2,1)S(1)}, bf16[512]{0:T(512)(128)(2,1)}, u32[]{:S(2)}) copy-start(bf16[512]{0:T(512)(128)(2,1)} %param.19) | copy-start | bytes 3076
  146.1 12.8 %collective-permute-start.9 = (bf16[4,512,128]{2,1,0:T(8,128)(2,1)S(1)}, bf16[4,512,128]{2,1,0:T(8,128)(2,1)S(1)}, u32[]{:S(2)}, u32[]{:S(2)}) collective-permute-start(bf16[4,512,128]{2,1,0:T(8,128)(2,1)S(1)} %collective-permute-done.5.refs_0_), channel_id=1, source_target_pairs={{0,1},{1,2},{2,3},{3,4},{4,5},{5,6},{6,7},{7,8},{8,9},{9,10},{10,1... | collective-permute-start | bytes 1572872 | tf_op jit(solution)/shard_map/ppermute | solution.py:28
Sparse Core Ops, SparseCore 0:
  12.9 89.0 all-gather.1

commit v6 on v5

--- a/solution.py
+++ b/solution.py
@@ -40,34 +40,38 @@
         (k, message.at[0:POS]),
         (v, message.at[POS : 2 * POS]),
         (q.at[edge], message.at[2 * POS : 2 * POS + EDGE]),
-        (x.at[edge], message.at[2 * POS + EDGE :]),
+        (x.at[edge], message.at[2 * POS + EDGE : 2 * (POS + EDGE)]),
     ]
 
 
-def pack_kernel(k, v, q, x, qx, lower, sems):
+def pack_kernel(k, v, q, x, kvw, qx, lower, sems):
     own = [(q, qx.at[0:POS]), (x, qx.at[POS:])]
     edge = slice(POS - EDGE, POS)
-    for copy in move(own + message_moves(k, v, q, x, lower, edge), sems):
+    copies = move(own + message_moves(k, v, q, x, lower, edge), sems)
+    lower[2 * (POS + EDGE) :] = kvw[2 * POS :]
+    for copy in copies:
         copy.wait()
 
 
-def pack(k, v, q, x):
+def pack(k, v, q, x, kvw):
     vmem, here = pl.BlockSpec(memory_space=pltpu.VMEM), pl.BlockSpec(memory_space=pltpu.HBM)
-    two = jax.ShapeDtypeStruct((2 * POS, HEAD_DIM), BF16)
-    message = jax.ShapeDtypeStruct((2 * (POS + EDGE), HEAD_DIM), BF16)
+    size = kvw.shape[0] - 2 * POS
     return pl.pallas_call(
         pack_kernel,
-        out_shape=(two, message),
-        in_specs=[here] * 4,
+        out_shape=(
+            jax.ShapeDtypeStruct((2 * POS, HEAD_DIM), BF16),
+            jax.ShapeDtypeStruct((2 * (POS + EDGE) + size, HEAD_DIM), BF16),
+        ),
+        in_specs=[here] * 4 + [vmem],
         out_specs=(vmem,) * 2,
         scratch_shapes=[pltpu.SemaphoreType.DMA((6,))],
         compiler_params=pltpu.CompilerParams(vmem_limit_bytes=8 << 20),
         name="pack",
-    )(k, v, q, x)
-
-
-def scale_kernel(place, k, v, q, x, weight_in, gain_in, kv, upper, scaled, weight, gain, sems):
-    pairs = [(weight_in, weight), (gain_in, gain), (k, kv.at[0:POS]), (v, kv.at[POS:])]
+    )(k, v, q, x, kvw)
+
+
+def scale_kernel(place, k, v, q, x, weight_in, gain_in, kvw, upper, weight, gain, sems):
+    pairs = [(weight_in, weight), (gain_in, gain), (k, kvw.at[0:POS]), (v, kvw.at[POS : 2 * POS])]
     copies = move(pairs + message_moves(k, v, q, x, upper, slice(0, EDGE)), sems)
     for copy in copies[:2]:
         copy.wait()
@@ -77,23 +81,24 @@
     mine = jnp.sum(jnp.where(line, gains, 0.0), axis=0, keepdims=True)
     mine = jnp.transpose(jnp.broadcast_to(mine, (depth, depth)))
     for c in range(0, weight.shape[1], depth):
-        scaled[:, c : c + depth] = (weight[:, c : c + depth].astype(F32) * mine).astype(BF16)
+        tile = (weight[:, c : c + depth].astype(F32) * mine).astype(BF16)
+        kvw[2 * POS + c : 2 * POS + c + depth] = tile
+        upper[2 * (POS + EDGE) + c : 2 * (POS + EDGE) + c + depth] = tile
     for copy in copies[2:]:
         copy.wait()
 
 
 def scale(place, k, v, q, x, weight, gain):
     vmem, here = pl.BlockSpec(memory_space=pltpu.VMEM), pl.BlockSpec(memory_space=pltpu.HBM)
-    message = jax.ShapeDtypeStruct((2 * (POS + EDGE), HEAD_DIM), BF16)
+    size = weight.size // HEAD_DIM
     return pl.pallas_call(
         scale_kernel,
         out_shape=(
-            jax.ShapeDtypeStruct((2 * POS, HEAD_DIM), BF16),
-            message,
-            jax.ShapeDtypeStruct(weight.shape, BF16),
+            jax.ShapeDtypeStruct((2 * POS + size, HEAD_DIM), BF16),
+            jax.ShapeDtypeStruct((2 * (POS + EDGE) + size, HEAD_DIM), BF16),
         ),
         in_specs=[pl.BlockSpec(memory_space=pltpu.SMEM)] + [here] * 6,
-        out_specs=(vmem,) * 3,
+        out_specs=(vmem,) * 2,
         scratch_shapes=[
             pltpu.VMEM(weight.shape, BF16),
             pltpu.VMEM(gain.shape, BF16),
@@ -161,7 +166,13 @@
     )(kv, qx, above, below)
 
 
-def attend_kernel(place, qx, above, below, far, summed_in, peak_in, total_in, taps, bias, res, conv, qs, xs, image):
+def attend_kernel(place, kvw, qx, above, below, far, summed_in, peak_in, total_in, taps, bias, *refs):
+    res, conv, rows, qs, xs, image = refs
+    size = kvw.shape[0] - 2 * POS
+    edges = 2 * (POS + EDGE)
+    sources = ((kvw, 2 * POS), (above, edges), (far, 2 * POS), (below, edges))
+    for n, (part, at) in enumerate(sources):
+        rows[n * size : (n + 1) * size] = part[at : at + size]
     spread_rows(above, qx[0:POS], below, qs, 2 * POS)
     spread_rows(above, qx[POS:], below, xs, 2 * POS + EDGE)
     tall = TALL
@@ -202,15 +213,16 @@
             conv[i * IMG_W + c0 : i * IMG_W + c0 + wide] = sums[i].astype(BF16)
 
 
-def attend(place, qx, above, below, far, begun, taps, bias):
+def attend(place, kvw, qx, above, below, far, begun, taps, bias):
     out = jax.ShapeDtypeStruct((POS, HEAD_DIM), BF16)
+    rows = jax.ShapeDtypeStruct((SEQ * (kvw.shape[0] - 2 * POS), HEAD_DIM), BF16)
     vmem = pl.BlockSpec(memory_space=pltpu.VMEM)
     flops = (POS + 2 * EDGE) * SEQ * POS * HEAD_DIM
     return pl.pallas_call(
         attend_kernel,
-        out_shape=(out, out),
-        in_specs=[pl.BlockSpec(memory_space=pltpu.SMEM)] + [vmem] * 9,
-        out_specs=(vmem, vmem),
+        out_shape=(out, out, rows),
+        in_specs=[pl.BlockSpec(memory_space=pltpu.SMEM)] + [vmem] * 10,
+        out_specs=(vmem,) * 3,
         scratch_shapes=[
             pltpu.VMEM((POS + 2 * EDGE, HEAD_DIM), BF16),
             pltpu.VMEM((POS + 2 * EDGE, HEAD_DIM), BF16),
@@ -219,33 +231,46 @@
         compiler_params=pltpu.CompilerParams(vmem_limit_bytes=16 << 20),
         cost_estimate=pl.CostEstimate(flops=flops, bytes_accessed=2 << 20, transcendentals=1 << 19),
         name="attend",
-    )(place, qx, above, below, far, *begun, taps, bias)
+    )(place, kvw, qx, above, below, far, *begun, taps, bias)
 
 
 AUX = 16
 
 
-def fetch(weights, groups, slabs, sems):
-    copies = []
+NEAR = (0, -1, 2, 1)
+PIECES = 2 * len(NEAR)
+
+
+def fetch(place, pieces, groups, slabs, sems):
+    seq, row = place[1], place[2]
+    depth = pieces[0].shape[2]
+    starts = [pl.multiple_of(lax.rem(seq + by + SEQ, SEQ) * depth, depth) for by in NEAR]
+    fetched = []
     for n, group in enumerate(groups):
-        rows = weights.shape[2]
-        copies.append(
-            [
+        away = lax.rem(group // 2 - row // 2 + SEQ, SEQ)
+        apart = lax.rem(group + row, 2)
+        for i, piece in enumerate(pieces):
+            copies = [
                 pltpu.make_async_copy(
-                    weights.at[j, group], slabs.at[n, j * rows : (j + 1) * rows], sems.at[n, j]
+                    piece.at[m], slabs.at[n, :, pl.ds(start, depth)], sems.at[n, m]
                 )
-                for j in range(SEQ)
+                for m, start in enumerate(starts)
             ]
-        )
-        for copy in copies[-1]:
-            copy.start()
-    return copies
-
-
-def slab_scratch(count, weights):
-    _, _, rows, columns = weights.shape
+            wanted = (away == NEAR[i % SEQ] % SEQ) & (apart == i // SEQ)
+
+            @pl.when(wanted)
+            def _():
+                for copy in copies:
+                    copy.start()
+
+        fetched.append(copies)
+    return fetched
+
+
+def slab_scratch(count, pieces):
+    _, tiles, depth, columns = pieces[0].shape
     return [
-        pltpu.VMEM((count, SEQ * rows, columns), BF16),
+        pltpu.VMEM((count, tiles, SEQ * depth, columns), BF16),
         pltpu.SemaphoreType.DMA((count, SEQ)),
     ]
 
@@ -269,7 +294,8 @@
     left = jnp.concatenate([left, extra_rows(gain, offset, group)], axis=0)
     for copy in copies:
         copy.wait()
-    return jnp.dot(left, slab[...], preferred_element_type=F32)
+    right = jnp.concatenate([slab[i] for i in range(slab.shape[0])], axis=1)
+    return jnp.dot(left, right, preferred_element_type=F32)
 
 
 def add_stats(blocks, pivot, before1, before2, sum1, sum2, rows=64):
@@ -287,9 +313,10 @@
 def first_kernel(offsets, place, *refs):
     count = len(offsets)
     parts, refs = refs[:count], refs[count:]
-    weights, gain, offset, acc, pivot, sum1, sum2, slabs, sems = refs
+    pieces, refs = refs[:PIECES], refs[PIECES:]
+    gain, offset, acc, pivot, sum1, sum2, slabs, sems = refs
     groups = [lax.rem(place[0] + away + CLASSES, CLASSES) for away in offsets]
-    copies = fetch(weights, groups, slabs, sems)
+    copies = fetch(place, pieces, groups, slabs, sems)
     lead = jnp.mean(parts[0][0].astype(F32), axis=1, keepdims=True)
     pivot[...] = jnp.broadcast_to(lead, (POS, HEAD_DIM))
     sum1[...] = jnp.zeros((POS, HEAD_DIM), F32)
@@ -307,9 +334,11 @@
 def more_kernel(offsets, place, *refs):
     count = len(offsets)
     parts, refs = refs[:count], refs[count:]
-    acc, pivot, sum1, sum2, weights, gain, offset, acc_out, sum1_out, sum2_out, slabs, sems = refs
+    acc, pivot, sum1, sum2, *refs = refs
+    pieces, refs = refs[:PIECES], refs[PIECES:]
+    gain, offset, acc_out, sum1_out, sum2_out, slabs, sems = refs
     groups = [lax.rem(place[0] + away + CLASSES, CLASSES) for away in offsets]
-    copies = fetch(weights, groups, slabs, sems)
+    copies = fetch(place, pieces, groups, slabs, sems)
     for n, part in enumerate(parts):
         blocks = [part.at[j] for j in range(SEQ)]
         before = (acc, sum1, sum2) if n == 0 else (acc_out, sum1_out, sum2_out)
@@ -318,9 +347,9 @@
         add_stats(blocks, pivot, before[1], before[2], sum1_out, sum2_out)
 
 
-def stage(kernel, offsets, place, parts, before, weights, gain, offset):
+def stage(kernel, offsets, place, parts, before, pieces, gain, offset):
     vmem, here = pl.BlockSpec(memory_space=pltpu.VMEM), pl.BlockSpec(memory_space=pltpu.HBM)
-    hidden = weights.shape[-1]
+    hidden = pieces[0].shape[1] * pieces[0].shape[3]
     stat = jax.ShapeDtypeStruct((POS, HEAD_DIM), F32)
     total = jax.ShapeDtypeStruct((POS + AUX, hidden), F32)
     out_shape = (total, stat, stat) if before else (total, stat, stat, stat)
@@ -329,21 +358,24 @@
         out_shape=out_shape,
         in_specs=[pl.BlockSpec(memory_space=pltpu.SMEM)]
         + [vmem] * (len(parts) + len(before))
-        + [here, vmem, vmem],
+        + [here] * PIECES
+        + [vmem] * 2,
         out_specs=(vmem,) * len(out_shape),
-        scratch_shapes=slab_scratch(len(parts), weights),
+        scratch_shapes=slab_scratch(len(parts), pieces),
         compiler_params=pltpu.CompilerParams(vmem_limit_bytes=16 << 20),
         cost_estimate=pl.CostEstimate(
             flops=len(parts) << 28, bytes_accessed=len(parts) << 20, transcendentals=0
         ),
         name="stage",
-    )(place, *parts, *before, weights, gain, offset)
+    )(place, *parts, *before, *pieces, gain, offset)
 
 
 def last_kernel(place, *refs):
-    acc, pivot, sum1, sum2, part, weights, gain, offset, bias, out, one, two, slabs, sems = refs
+    acc, pivot, sum1, sum2, part, *refs = refs
+    pieces, refs = refs[:PIECES], refs[PIECES:]
+    gain, offset, bias, out, one, two, slabs, sems = refs
     group = lax.rem(place[0] + 4, CLASSES)
-    (copies,) = fetch(weights, [group], slabs, sems)
+    (copies,) = fetch(place, pieces, [group], slabs, sems)
     blocks = [part.at[j] for j in range(SEQ)]
     add_stats(blocks, pivot, sum1, sum2, one, two)
     product = acc[...] + product_of(blocks, copies, slabs.at[0], gain, offset, group)
@@ -358,19 +390,19 @@
     out[...] = (0.5 * project * (1.0 + lax.erf(project * math.sqrt(0.5)))).astype(BF16)
 
 
-def last(place, acc, stats, part, weights, gain, offset, bias):
+def last(place, acc, stats, part, pieces, gain, offset, bias):
     vmem, here = pl.BlockSpec(memory_space=pltpu.VMEM), pl.BlockSpec(memory_space=pltpu.HBM)
-    hidden = weights.shape[-1]
+    hidden = pieces[0].shape[1] * pieces[0].shape[3]
     return pl.pallas_call(
         last_kernel,
         out_shape=jax.ShapeDtypeStruct((POS, hidden), BF16),
-        in_specs=[pl.BlockSpec(memory_space=pltpu.SMEM)] + [vmem] * 5 + [here] + [vmem] * 3,
+        in_specs=[pl.BlockSpec(memory_space=pltpu.SMEM)] + [vmem] * 5 + [here] * PIECES + [vmem] * 3,
         out_specs=vmem,
-        scratch_shapes=[pltpu.VMEM((POS, HEAD_DIM), F32)] * 2 + slab_scratch(1, weights),
+        scratch_shapes=[pltpu.VMEM((POS, HEAD_DIM), F32)] * 2 + slab_scratch(1, pieces),
         compiler_params=pltpu.CompilerParams(vmem_limit_bytes=16 << 20),
         cost_estimate=pl.CostEstimate(flops=1 << 28, bytes_accessed=7 << 20, transcendentals=1 << 18),
         name="last",
-    )(place, acc, *stats, part, weights, gain, offset, bias)
+    )(place, acc, *stats, part, *pieces, gain, offset, bias)
 
 
 def on_device(
@@ -392,38 +424,46 @@
     x, q, k, v = (pltpu.with_memory_space_constraint(a, pltpu.HBM) for a in (x, q, k, v))
     mine = (seq * CLASSES + row).astype(jnp.int32).reshape(1)
     held = (pltpu.with_memory_space_constraint(a, pltpu.HBM) for a in (expand_weight, gain))
-    qx, lower = pack(k, v, q, x)
+    kvw, upper = scale(mine, k, v, q, x, *held)
+    below, far = shift(upper, "seq", -1), shift(kvw, "seq", 2)
+    qx, lower = pack(k, v, q, x, kvw)
     above = shift(lower, "seq", 1)
-    kv, upper, scaled = scale(mine, k, v, q, x, *held)
-    below, far = shift(upper, "seq", -1), shift(kv, "seq", 2)
-    weights = lax.all_gather(scaled, ("seq", "row"), axis=0, tiled=True)
-    weights = weights.reshape(SEQ, CLASSES, depth, hidden)
-    weights = pltpu.with_memory_space_constraint(weights, pltpu.HBM)
     gain, offset = gain.astype(F32), offset.astype(F32)
     taps = depth_weight.astype(F32).reshape(KERNEL * KERNEL, HEAD_DIM)
     bias = depth_bias.astype(F32).reshape(1, HEAD_DIM)
-    begun = near(kv, qx, above, below)
-    residual, convolved = attend(
-        seq.astype(jnp.int32).reshape(1), qx, above, below, far, begun, taps, bias
+    begun = near(kvw, qx, above, below)
+    residual, convolved, rows = attend(
+        seq.astype(jnp.int32).reshape(1), kvw, qx, above, below, far, begun, taps, bias
     )
 
     strides = [[i + CLASSES * j for j in range(SEQ)] for i in range(CLASSES)]
     own = lax.all_gather(convolved, "col", axis=0, tiled=True, axis_index_groups=strides)
     own = own.reshape(SEQ, POS, HEAD_DIM)
+    _, rows = lax.optimization_barrier((own, rows))
+    swap = [(i, i ^ 1) for i in range(lax.axis_size("row"))]
+    along_y = [rows] + [shift(rows, "row", 2 * by) for by in (1, 2, -1)]
     pairs, up, down = [], own, own
-    for _ in range(3):
+    for n in range(3):
         up, down = shift(up, "col", 1), shift(down, "col", -1)
+        if n == 0:
+            down, *along_y[1:] = lax.optimization_barrier((down, *along_y[1:]))
+        if n == 1:
+            _, *along_y = lax.optimization_barrier((up, *along_y))
+            other = [lax.ppermute(piece, "row", swap) for piece in along_y]
         pairs.append((up, down))
-    place = col.astype(jnp.int32).reshape(1)
+    depth_tiles = (SEQ, hidden // HEAD_DIM, depth, HEAD_DIM)
+    pieces = [
+        pltpu.with_memory_space_constraint(a.reshape(depth_tiles), pltpu.HBM)
+        for a in along_y + other
+    ]
+    place = jnp.stack([col, seq, row]).astype(jnp.int32)
     parts = (own, *pairs[0], *pairs[1])
-    before = stage(first_kernel, (0, -1, 1, -2, 2), place, parts, (), weights, gain, offset)
-    up, before = lax.optimization_barrier((up, before))
-    pairs[2] = (up, down)
+    before = stage(first_kernel, (0, -1, 1, -2, 2), place, parts, (), pieces, gain, offset)
     up = shift(up, "col", 1)
-    acc, *sums = stage(more_kernel, (-3, 3), place, pairs[2], before, weights, gain, offset)
+    acc, *sums = stage(more_kernel, (-3, 3), place, pairs[2], before, pieces, gain, offset)
     pivot = before[1]
     bias = expand_bias.astype(F32).reshape(1, hidden)
-    out = last(place, acc, (pivot, *sums), up, weights, gain, offset, bias)
+    out = last(place, acc, (pivot, *sums), up, pieces, gain, offset, bias)
     return (
         residual.reshape(inputs.shape),
         out.reshape(inputs.shape[:3] + (hidden,)),

time: 169 us -> 173 us (1.024)
  the two profiles are of different devices: /device:TPU:8 before, /device:TPU:10 now
where the time goes in v6:
time: 173 us; the launch traced here: 172 us
  blocking collectives  60.5 us (35%)
  starting transfers between devices  52.3 us (30%)
  waiting for transfers between devices  35.9 us (21%)
  Pallas kernels  20.8 us (12%)
  local copies, waits for them, and re-layouts  1.86 us (1%)
    all_gather x1, blocking collectives, on_device(): lax.all_gather(convolved, 'col', axis=0, tiled=True, axis_index_groups=st...  60.5 us
    ppermute x13, starting transfers between devices, shift(): lax.ppermute(array, axis, [(i, (i + by) % peers) for i in range(peers)])  44.2 us
    ppermute x13, waiting for transfers between devices, shift(): lax.ppermute(array, axis, [(i, (i + by) % peers) for i in range(peers)])  35.9 us
    ppermute x4, starting transfers between devices, on_device(): other = [lax.ppermute(piece, 'row', swap) for piece in along_y]  8.15 us
    pallas_call x2, Pallas kernels, stage(): pl.pallas_call(functools.partial(kernel, offsets), out_shape=out_shape, i...  7.71 us
    pallas_call x1, Pallas kernels, last(): pl.pallas_call(last_kernel, out_shape=jax.ShapeDtypeStruct((POS, hidden),...  4.2 us
  transfers between devices with their start and end apart: 17, of which 9 were waited for; matrix products, arithmetic and copies ran while one was open for 0% of the time, Pallas kernels for 6%

profile of v6, /device:TPU:10, one launch (start us, length us, event | category | flops | bytes accessed | tf_op | source)
XLA Modules:
  0.0 172.5 jit_solution(16248860200353907124)
XLA Ops:
  3.1 3.4 %collective-permute-start = (bf16[1920,128]{1,0:T(8,128)(2,1)S(1)}, bf16[1920,128]{1,0:T(8,128)(2,1)S(1)}, u32[]{:S(2)}, u32[]{:S(2)}) collective-permute-start(bf16[1920,128]{1,0:T(8,128)(2,1)S(1)} %get-tuple-element.30), channel_id=1, source_target_pairs={{0,256},{256,512},{512,768},{768,0},{1,257},{257,513},{513,769},{7... | collective-permute-start | bytes 1474568 | tf_op jit(solution)/shard_map/ppermute | solution.py:28
  6.5 2.4 %collective-permute-start.1 = (bf16[1920,128]{1,0:T(8,128)(2,1)S(1)}, bf16[1920,128]{1,0:T(8,128)(2,1)S(1)}, u32[]{:S(2)}, u32[]{:S(2)}) collective-permute-start(bf16[1920,128]{1,0:T(8,128)(2,1)S(1)} %get-tuple-element.31), channel_id=1, source_target_pairs={{0,768},{256,0},{512,256},{768,512},{1,769},{257,1},{513,257},{769... | collective-permute-start | bytes 1474568 | tf_op jit(solution)/shard_map/ppermute | solution.py:28
  8.9 4.0 %collective-permute-start.2 = (bf16[1536,128]{1,0:T(8,128)(2,1)S(1)}, bf16[1536,128]{1,0:T(8,128)(2,1)S(1)}, u32[]{:S(2)}, u32[]{:S(2)}) collective-permute-start(bf16[1536,128]{1,0:T(8,128)(2,1)S(1)} %get-tuple-element.28.kvw.kv), channel_id=1, source_target_pairs={{0,512},{256,768},{512,0},{768,256},{1,513},{257,769},{513,1},{769... | collective-permute-start | bytes 1179656 | tf_op jit(solution)/shard_map/ppermute | solution.py:28
  13.0 6.0 %collective-permute-done.above = bf16[1920,128]{1,0:T(8,128)(2,1)S(1)} collective-permute-done((bf16[1920,128]{1,0:T(8,128)(2,1)S(1)}, bf16[1920,128]{1,0:T(8,128)(2,1)S(1)}, u32[]{:S(2)}, u32[]{:S(2)}) %collective-permute-start) | collective-permute-done | bytes 491552 | tf_op jit(solution)/shard_map/ppermute | solution.py:28
  19.1 2.8 %collective-permute-done.1.below = bf16[1920,128]{1,0:T(8,128)(2,1)S(1)} collective-permute-done((bf16[1920,128]{1,0:T(8,128)(2,1)S(1)}, bf16[1920,128]{1,0:T(8,128)(2,1)S(1)}, u32[]{:S(2)}, u32[]{:S(2)}) %collective-permute-start.1) | collective-permute-done | bytes 491552 | tf_op jit(solution)/shard_map/ppermute | solution.py:28
  21.9 3.0 %near.1 = (f32[896,128]{1,0:T(8,128)S(1)}, f32[896,128]{1,0:T(8,128)S(1)}, f32[896,128]{1,0:T(8,128)S(1)}) custom-call(bf16[1536,128]{1,0:T(8,128)(2,1)S(1)} %get-tuple-element.28.kvw.kv, bf16[1024,128]{1,0:T(8,128)(2,1)S(1)} %get-tuple-element.29.qx, bf16[1920,128]{1,0:T(8,128)(2,1)S(1)} %collective-permute-done.above, ...), custom_call_target="tpu_custom_call" | custom-call | flops 704643072 | bytes 3145728 | tf_op jit(solution)/shard_map/near/pallas_call | solution.py:157
  24.9 5.2 %collective-permute-done.2.far = bf16[1536,128]{1,0:T(8,128)(2,1)S(1)} collective-permute-done((bf16[1536,128]{1,0:T(8,128)(2,1)S(1)}, bf16[1536,128]{1,0:T(8,128)(2,1)S(1)}, u32[]{:S(2)}, u32[]{:S(2)}) %collective-permute-start.2) | collective-permute-done | bytes 393248 | tf_op jit(solution)/shard_map/ppermute | solution.py:28
  30.1 3.5 %attend.1 = (bf16[512,128]{1,0:T(8,128)(2,1)}, bf16[512,128]{1,0:T(8,128)(2,1)S(1)}, bf16[2048,128]{1,0:T(8,128)(2,1)S(1)}) custom-call(s32[1]{0:T(128)} %bitcast.place, bf16[1536,128]{1,0:T(8,128)(2,1)S(1)} %get-tuple-element.28.kvw.kv, bf16[1024,128]{1,0:T(8,128)(2,1)S(1)} %get-tuple-element.29.qx, bf16[1920,128]{1,0:T(8,128)(2,1)S(1)} %collective-permute-done.above, ...), custom_call_target="tpu_custom_call" | custom-call | flops 234881024 | bytes 2097152 | tf_op jit(solution)/shard_map/attend/pallas_call | solution.py:221
  33.6 60.5 %all_gather.3 = bf16[2048,128]{1,0:T(8,128)(2,1)S(1)} all-gather(bf16[512,128]{1,0:T(8,128)(2,1)S(1)} %get-tuple-element.36), channel_id=1, replica_groups={{0,8,16,24},{1,9,17,25},{2,10,18,26},{3,11,19,27},{4,12,20,28},{5,13,21..., dimensions={0}, use_global_device_ids=true | all-gather | bytes 655360 | tf_op jit(solution)/shard_map/all_gather | solution.py:440
  94.1 4.5 %collective-permute-start.3 = (bf16[4,512,128]{2,1,0:T(8,128)(2,1)S(1)}, bf16[4,512,128]{2,1,0:T(8,128)(2,1)S(1)}, u32[]{:S(2)}, u32[]{:S(2)}) collective-permute-start(bf16[4,512,128]{2,1,0:T(8,128)(2,1)S(1)} %bitcast.31), channel_id=1, source_target_pairs={{0,1},{1,2},{2,3},{3,4},{4,5},{5,6},{6,7},{7,8},{8,9},{9,10},{10,1... | collective-permute-start | bytes 1572872 | tf_op jit(solution)/shard_map/ppermute | solution.py:28
  98.6 4.9 %collective-permute-start.7 = (bf16[2048,128]{1,0:T(8,128)(2,1)S(1)}, bf16[2048,128]{1,0:T(8,128)(2,1)}, u32[]{:S(2)}, u32[]{:S(2)}) collective-permute-start(bf16[2048,128]{1,0:T(8,128)(2,1)S(1)} %get-tuple-element.43), channel_id=1, source_target_pairs={{0,64},{32,96},{64,128},{96,160},{128,192},{160,224},{192,0},{224,... | collective-permute-start | bytes 1572872 | tf_op jit(solution)/shard_map/ppermute | solution.py:28
  103.5 2.6 %collective-permute-start.8 = (bf16[2048,128]{1,0:T(8,128)(2,1)S(1)}, bf16[2048,128]{1,0:T(8,128)(2,1)}, u32[]{:S(2)}, u32[]{:S(2)}) collective-permute-start(bf16[2048,128]{1,0:T(8,128)(2,1)S(1)} %get-tuple-element.43), channel_id=1, source_target_pairs={{0,128},{32,160},{64,192},{96,224},{128,0},{160,32},{192,64},{224,... | collective-permute-start | bytes 1572872 | tf_op jit(solution)/shard_map/ppermute | solution.py:28
  106.1 4.5 %collective-permute-start.9 = (bf16[2048,128]{1,0:T(8,128)(2,1)S(1)}, bf16[2048,128]{1,0:T(8,128)(2,1)}, u32[]{:S(2)}, u32[]{:S(2)}) collective-permute-start(bf16[2048,128]{1,0:T(8,128)(2,1)S(1)} %get-tuple-element.43), channel_id=1, source_target_pairs={{0,192},{32,224},{64,0},{96,32},{128,64},{160,96},{192,128},{224,1... | collective-permute-start | bytes 1572872 | tf_op jit(solution)/shard_map/ppermute | solution.py:28
  112.6 3.9 %collective-permute-start.4 = (bf16[4,512,128]{2,1,0:T(8,128)(2,1)S(1)}, bf16[4,512,128]{2,1,0:T(8,128)(2,1)S(1)}, u32[]{:S(2)}, u32[]{:S(2)}) collective-permute-start(bf16[4,512,128]{2,1,0:T(8,128)(2,1)S(1)} %collective-permute-done.3.refs_1_), channel_id=1, source_target_pairs={{0,1},{1,2},{2,3},{3,4},{4,5},{5,6},{6,7},{7,8},{8,9},{9,10},{10,1... | collective-permute-start | bytes 1572872 | tf_op jit(solution)/shard_map/ppermute | solution.py:28
  116.5 7.6 %collective-permute-done.7 = bf16[2048,128]{1,0:T(8,128)(2,1)} collective-permute-done((bf16[2048,128]{1,0:T(8,128)(2,1)S(1)}, bf16[2048,128]{1,0:T(8,128)(2,1)}, u32[]{:S(2)}, u32[]{:S(2)}) %collective-permute-start.7) | collective-permute-done | bytes 524320 | tf_op jit(solution)/shard_map/ppermute | solution.py:28
  124.1 5.7 %collective-permute-done.9 = bf16[2048,128]{1,0:T(8,128)(2,1)} collective-permute-done((bf16[2048,128]{1,0:T(8,128)(2,1)S(1)}, bf16[2048,128]{1,0:T(8,128)(2,1)}, u32[]{:S(2)}, u32[]{:S(2)}) %collective-permute-start.9) | collective-permute-done | bytes 524320 | tf_op jit(solution)/shard_map/ppermute | solution.py:28
  133.7 3.9 %collective-permute-start.5 = (bf16[4,512,128]{2,1,0:T(8,128)(2,1)S(1)}, bf16[4,512,128]{2,1,0:T(8,128)(2,1)S(1)}, u32[]{:S(2)}, u32[]{:S(2)}) collective-permute-start(bf16[4,512,128]{2,1,0:T(8,128)(2,1)S(1)} %collective-permute-done.4.refs_3_), channel_id=1, source_target_pairs={{0,1},{1,2},{2,3},{3,4},{4,5},{5,6},{6,7},{7,8},{8,9},{9,10},{10,1... | collective-permute-start | bytes 1572872 | tf_op jit(solution)/shard_map/ppermute | solution.py:28
  142.7 2.9 %collective-permute-done.10.refs_4_ = bf16[4,512,128]{2,1,0:T(8,128)(2,1)} collective-permute-done((bf16[4,512,128]{2,1,0:T(8,128)(2,1)S(1)}, bf16[4,512,128]{2,1,0:T(8,128)(2,1)}, u32[]{:S(2)}, u32[]{:S(2)}) %collective-permute-start.10) | collective-permute-done | bytes 524320 | tf_op jit(solution)/shard_map/ppermute | solution.py:28
  147.6 3.4 %collective-permute-start.11 = (bf16[4,512,128]{2,1,0:T(8,128)(2,1)}, bf16[4,512,128]{2,1,0:T(8,128)(2,1)S(1)}, u32[]{:S(2)}, u32[]{:S(2)}) collective-permute-start(bf16[4,512,128]{2,1,0:T(8,128)(2,1)} %collective-permute-done.10.refs_4_), channel_id=1, source_target_pairs={{0,31},{1,0},{2,1},{3,2},{4,3},{5,4},{6,5},{7,6},{8,7},{9,8},{10,9... | collective-permute-start | bytes 1572872 | tf_op jit(solution)/shard_map/ppermute | solution.py:28
  151.1 2.7 %collective-permute-start.16 = (bf16[4,512,128]{2,1,0:T(8,128)(2,1)S(1)}, bf16[4,512,128]{2,1,0:T(8,128)(2,1)}, u32[]{:S(2)}, u32[]{:S(2)}) collective-permute-start(bf16[4,512,128]{2,1,0:T(8,128)(2,1)S(1)} %collective-permute-done.5.refs_0_), channel_id=1, source_target_pairs={{0,1},{1,2},{2,3},{3,4},{4,5},{5,6},{6,7},{7,8},{8,9},{9,10},{10,1... | collective-permute-start | bytes 1572872 | tf_op jit(solution)/shard_map/ppermute | solution.py:28
  155.0 4.9 %stage.2 = (f32[528,512]{1,0:T(8,128)S(1)}, f32[512,128]{1,0:T(8,128)S(1)}, f32[512,128]{1,0:T(8,128)S(1)}, f32[512,128]{1,0:T(8,128)S(1)}) custom-call(s32[3]{0:T(128)S(1)} %pad_add_fusion.place, bf16[4,512,128]{2,1,0:T(8,128)(2,1)S(1)} %bitcast.33, bf16[4,512,128]{2,1,0:T(8,128)(2,1)S(1)} %collective-permute-done.3.refs_1_, ...), custom_call_target="tpu_custom_call" | custom-call | flops 1342177280 | bytes 5242880 | tf_op jit(solution)/shard_map/stage/pallas_call | solution.py:356
  159.9 4.1 %collective-permute-done.11.refs_1_ = bf16[4,512,128]{2,1,0:T(8,128)(2,1)S(1)} collective-permute-done((bf16[4,512,128]{2,1,0:T(8,128)(2,1)}, bf16[4,512,128]{2,1,0:T(8,128)(2,1)S(1)}, u32[]{:S(2)}, u32[]{:S(2)}) %collective-permute-start.11) | collective-permute-done | bytes 524320 | tf_op jit(solution)/shard_map/ppermute | solution.py:28
  164.0 2.8 %stage.3 = (f32[528,512]{1,0:T(8,128)S(1)}, f32[512,128]{1,0:T(8,128)S(1)}, f32[512,128]{1,0:T(8,128)S(1)}) custom-call(s32[3]{0:T(128)S(1)} %pad_add_fusion.place, bf16[4,512,128]{2,1,0:T(8,128)(2,1)S(1)} %collective-permute-done.5.refs_0_, bf16[4,512,128]{2,1,0:T(8,128)(2,1)S(1)} %collective-permute-done.11.refs_1_, ...), custom_call_target="tpu_custom_call" | custom-call | flops 536870912 | bytes 2097152 | tf_op jit(solution)/shard_map/stage/pallas_call | solution.py:356
  168.3 4.2 %last.1 = bf16[512,512]{1,0:T(8,128)(2,1)} custom-call(s32[3]{0:T(128)S(1)} %pad_add_fusion.place, f32[528,512]{1,0:T(8,128)S(1)} %get-tuple-element.51.refs_0_, f32[512,128]{1,0:T(8,128)S(1)} %get-tuple-element.48.refs_3_.refs_1_, f32[512,128]{1,0:T(8,128)S(1)} %get-tuple-element.52.refs_2_, f32[512,128]{1,0:T(8,128)S(1)} %get-tuple-element.53.refs_3_, ...), custom_call_target="tpu_custom_call" | custom-call | flops 268435456 | bytes 7340032 | tf_op jit(solution)/shard_map/last/pallas_call | solution.py:396
  (40 shorter events, 17.9 us)
Async XLA Ops:
  0.6 12.4 %copy-start.4 = (bf16[7,7,128]{2,1,0:T(8,128)(2,1)S(1)}, bf16[7,7,128]{2,1,0:T(8,128)(2,1)}, u32[]{:S(2)}) copy-start(bf16[7,7,128]{2,1,0:T(8,128)(2,1)} %param.14) | copy-start | bytes 37636
  0.6 12.4 %copy-start.7 = (bf16[128]{0:T(256)(128)(2,1)S(1)}, bf16[128]{0:T(256)(128)(2,1)}, u32[]{:S(2)}) copy-start(bf16[128]{0:T(256)(128)(2,1)} %param.15) | copy-start | bytes 772
  3.1 16.0 %collective-permute-start = (bf16[1920,128]{1,0:T(8,128)(2,1)S(1)}, bf16[1920,128]{1,0:T(8,128)(2,1)S(1)}, u32[]{:S(2)}, u32[]{:S(2)}) collective-permute-start(bf16[1920,128]{1,0:T(8,128)(2,1)S(1)} %get-tuple-element.30), channel_id=1, source_target_pairs={{0,256},{256,512},{512,768},{768,0},{1,257},{257,513},{513,769},{7... | collective-permute-start | bytes 1474568 | tf_op jit(solution)/shard_map/ppermute | solution.py:28
  6.5 15.4 %collective-permute-start.1 = (bf16[1920,128]{1,0:T(8,128)(2,1)S(1)}, bf16[1920,128]{1,0:T(8,128)(2,1)S(1)}, u32[]{:S(2)}, u32[]{:S(2)}) collective-permute-start(bf16[1920,128]{1,0:T(8,128)(2,1)S(1)} %get-tuple-element.31), channel_id=1, source_target_pairs={{0,768},{256,0},{512,256},{768,512},{1,769},{257,1},{513,257},{769... | collective-permute-start | bytes 1474568 | tf_op jit(solution)/shard_map/ppermute | solution.py:28
  8.9 21.2 %collective-permute-start.2 = (bf16[1536,128]{1,0:T(8,128)(2,1)S(1)}, bf16[1536,128]{1,0:T(8,128)(2,1)S(1)}, u32[]{:S(2)}, u32[]{:S(2)}) collective-permute-start(bf16[1536,128]{1,0:T(8,128)(2,1)S(1)} %get-tuple-element.28.kvw.kv), channel_id=1, source_target_pairs={{0,512},{256,768},{512,0},{768,256},{1,513},{257,769},{513,1},{769... | collective-permute-start | bytes 1179656 | tf_op jit(solution)/shard_map/ppermute | solution.py:28
  30.1 123.7 %copy-start.3 = (bf16[4096]{0:T(1024)(128)(2,1)S(1)}, bf16[4096]{0:T(1024)(128)(2,1)}, u32[]{:S(2)}) copy-start(bf16[4096]{0:T(1024)(128)(2,1)} %param.16) | copy-start | bytes 24580
  30.1 123.7 %copy-start.6 = (bf16[512]{0:T(512)(128)(2,1)S(1)}, bf16[512]{0:T(512)(128)(2,1)}, u32[]{:S(2)}) copy-start(bf16[512]{0:T(512)(128)(2,1)} %param.19) | copy-start | bytes 3076
  30.1 123.8 %copy-start.5 = (bf16[4096]{0:T(1024)(128)(2,1)S(1)}, bf16[4096]{0:T(1024)(128)(2,1)}, u32[]{:S(2)}) copy-start(bf16[4096]{0:T(1024)(128)(2,1)} %param.17) | copy-start | bytes 24580
  33.6 120.4 %copy-start = (bf16[2048,128]{1,0:T(8,128)(2,1)}, bf16[2048,128]{1,0:T(8,128)(2,1)S(1)}, u32[]{:S(2)}) copy-start(bf16[2048,128]{1,0:T(8,128)(2,1)S(1)} %get-tuple-element.43) | copy-start | bytes 1572868
  94.1 18.5 %collective-permute-start.3 = (bf16[4,512,128]{2,1,0:T(8,128)(2,1)S(1)}, bf16[4,512,128]{2,1,0:T(8,128)(2,1)S(1)}, u32[]{:S(2)}, u32[]{:S(2)}) collective-permute-start(bf16[4,512,128]{2,1,0:T(8,128)(2,1)S(1)} %bitcast.31), channel_id=1, source_target_pairs={{0,1},{1,2},{2,3},{3,4},{4,5},{5,6},{6,7},{7,8},{8,9},{9,10},{10,1... | collective-permute-start | bytes 1572872 | tf_op jit(solution)/shard_map/ppermute | solution.py:28
  98.6 25.5 %collective-permute-start.7 = (bf16[2048,128]{1,0:T(8,128)(2,1)S(1)}, bf16[2048,128]{1,0:T(8,128)(2,1)}, u32[]{:S(2)}, u32[]{:S(2)}) collective-permute-start(bf16[2048,128]{1,0:T(8,128)(2,1)S(1)} %get-tuple-element.43), channel_id=1, source_target_pairs={{0,64},{32,96},{64,128},{96,160},{128,192},{160,224},{192,0},{224,... | collective-permute-start | bytes 1572872 | tf_op jit(solution)/shard_map/ppermute | solution.py:28
  103.5 20.7 %collective-permute-start.8 = (bf16[2048,128]{1,0:T(8,128)(2,1)S(1)}, bf16[2048,128]{1,0:T(8,128)(2,1)}, u32[]{:S(2)}, u32[]{:S(2)}) collective-permute-start(bf16[2048,128]{1,0:T(8,128)(2,1)S(1)} %get-tuple-element.43), channel_id=1, source_target_pairs={{0,128},{32,160},{64,192},{96,224},{128,0},{160,32},{192,64},{224,... | collective-permute-start | bytes 1572872 | tf_op jit(solution)/shard_map/ppermute | solution.py:28
  106.1 23.7 %collective-permute-start.9 = (bf16[2048,128]{1,0:T(8,128)(2,1)S(1)}, bf16[2048,128]{1,0:T(8,128)(2,1)}, u32[]{:S(2)}, u32[]{:S(2)}) collective-permute-start(bf16[2048,128]{1,0:T(8,128)(2,1)S(1)} %get-tuple-element.43), channel_id=1, source_target_pairs={{0,192},{32,224},{64,0},{96,32},{128,64},{160,96},{192,128},{224,1... | collective-permute-start | bytes 1572872 | tf_op jit(solution)/shard_map/ppermute | solution.py:28
  110.6 19.2 %collective-permute-start.6 = (bf16[4,512,128]{2,1,0:T(8,128)(2,1)S(1)}, bf16[4,512,128]{2,1,0:T(8,128)(2,1)S(1)}, u32[]{:S(2)}, u32[]{:S(2)}) collective-permute-start(bf16[4,512,128]{2,1,0:T(8,128)(2,1)S(1)} %bitcast.32), channel_id=1, source_target_pairs={{0,31},{1,0},{2,1},{3,2},{4,3},{5,4},{6,5},{7,6},{8,7},{9,8},{10,9... | collective-permute-start | bytes 1572872 | tf_op jit(solution)/shard_map/ppermute | solution.py:28
  112.6 19.2 %collective-permute-start.4 = (bf16[4,512,128]{2,1,0:T(8,128)(2,1)S(1)}, bf16[4,512,128]{2,1,0:T(8,128)(2,1)S(1)}, u32[]{:S(2)}, u32[]{:S(2)}) collective-permute-start(bf16[4,512,128]{2,1,0:T(8,128)(2,1)S(1)} %collective-permute-done.3.refs_1_), channel_id=1, source_target_pairs={{0,1},{1,2},{2,3},{3,4},{4,5},{5,6},{6,7},{7,8},{8,9},{9,10},{10,1... | collective-permute-start | bytes 1572872 | tf_op jit(solution)/shard_map/ppermute | solution.py:28
  129.8 15.8 %collective-permute-start.10 = (bf16[4,512,128]{2,1,0:T(8,128)(2,1)S(1)}, bf16[4,512,128]{2,1,0:T(8,128)(2,1)}, u32[]{:S(2)}, u32[]{:S(2)}) collective-permute-start(bf16[4,512,128]{2,1,0:T(8,128)(2,1)S(1)} %collective-permute-done.6.refs_2_), channel_id=1, source_target_pairs={{0,31},{1,0},{2,1},{3,2},{4,3},{5,4},{6,5},{7,6},{8,7},{9,8},{10,9... | collective-permute-start | bytes 1572872 | tf_op jit(solution)/shard_map/ppermute | solution.py:28
  131.7 15.8 %collective-permute-start.12 = (bf16[2048,128]{1,0:T(8,128)(2,1)S(1)}, bf16[2048,128]{1,0:T(8,128)(2,1)}, u32[]{:S(2)}, u32[]{:S(2)}) collective-permute-start(bf16[2048,128]{1,0:T(8,128)(2,1)S(1)} %get-tuple-element.43), channel_id=1, source_target_pairs={{0,32},{32,0},{64,96},{96,64},{128,160},{160,128},{192,224},{224,1... | collective-permute-start | bytes 1572872 | tf_op jit(solution)/shard_map/ppermute | solution.py:452
  133.7 17.4 %collective-permute-start.5 = (bf16[4,512,128]{2,1,0:T(8,128)(2,1)S(1)}, bf16[4,512,128]{2,1,0:T(8,128)(2,1)S(1)}, u32[]{:S(2)}, u32[]{:S(2)}) collective-permute-start(bf16[4,512,128]{2,1,0:T(8,128)(2,1)S(1)} %collective-permute-done.4.refs_3_), channel_id=1, source_target_pairs={{0,1},{1,2},{2,3},{3,4},{4,5},{5,6},{6,7},{7,8},{8,9},{9,10},{10,1... | collective-permute-start | bytes 1572872 | tf_op jit(solution)/shard_map/ppermute | solution.py:28
  138.4 15.5 %collective-permute-start.13 = (bf16[2048,128]{1,0:T(8,128)(2,1)}, bf16[2048,128]{1,0:T(8,128)(2,1)}, u32[]{:S(2)}, u32[]{:S(2)}) collective-permute-start(bf16[2048,128]{1,0:T(8,128)(2,1)} %collective-permute-done.7), channel_id=1, source_target_pairs={{0,32},{32,0},{64,96},{96,64},{128,160},{160,128},{192,224},{224,1... | collective-permute-start | bytes 1572872 | tf_op jit(solution)/shard_map/ppermute | solution.py:452
  140.5 13.4 %collective-permute-start.14 = (bf16[2048,128]{1,0:T(8,128)(2,1)}, bf16[2048,128]{1,0:T(8,128)(2,1)}, u32[]{:S(2)}, u32[]{:S(2)}) collective-permute-start(bf16[2048,128]{1,0:T(8,128)(2,1)} %collective-permute-done.8), channel_id=1, source_target_pairs={{0,32},{32,0},{64,96},{96,64},{128,160},{160,128},{192,224},{224,1... | collective-permute-start | bytes 1572872 | tf_op jit(solution)/shard_map/ppermute | solution.py:452
  145.7 8.3 %collective-permute-start.15 = (bf16[2048,128]{1,0:T(8,128)(2,1)}, bf16[2048,128]{1,0:T(8,128)(2,1)}, u32[]{:S(2)}, u32[]{:S(2)}) collective-permute-start(bf16[2048,128]{1,0:T(8,128)(2,1)} %collective-permute-done.9), channel_id=1, source_target_pairs={{0,32},{32,0},{64,96},{96,64},{128,160},{160,128},{192,224},{224,1... | collective-permute-start | bytes 1572872 | tf_op jit(solution)/shard_map/ppermute | solution.py:452
  147.6 16.4 %collective-permute-start.11 = (bf16[4,512,128]{2,1,0:T(8,128)(2,1)}, bf16[4,512,128]{2,1,0:T(8,128)(2,1)S(1)}, u32[]{:S(2)}, u32[]{:S(2)}) collective-permute-start(bf16[4,512,128]{2,1,0:T(8,128)(2,1)} %collective-permute-done.10.refs_4_), channel_id=1, source_target_pairs={{0,31},{1,0},{2,1},{3,2},{4,3},{5,4},{6,5},{7,6},{8,7},{9,8},{10,9... | collective-permute-start | bytes 1572872 | tf_op jit(solution)/shard_map/ppermute | solution.py:28
  151.1 17.2 %collective-permute-start.16 = (bf16[4,512,128]{2,1,0:T(8,128)(2,1)S(1)}, bf16[4,512,128]{2,1,0:T(8,128)(2,1)}, u32[]{:S(2)}, u32[]{:S(2)}) collective-permute-start(bf16[4,512,128]{2,1,0:T(8,128)(2,1)S(1)} %collective-permute-done.5.refs_0_), channel_id=1, source_target_pairs={{0,1},{1,2},{2,3},{3,4},{4,5},{5,6},{6,7},{7,8},{8,9},{9,10},{10,1... | collective-permute-start | bytes 1572872 | tf_op jit(solution)/shard_map/ppermute | solution.py:28
  154.0 1.0 copy-start.2
  (1 other events, 0.8 us)

commit v7 on v6

--- a/solution.py
+++ b/solution.py
@@ -241,7 +241,7 @@
 PIECES = 2 * len(NEAR)
 
 
-def fetch(place, pieces, groups, slabs, sems):
+def fetch(place, pieces, groups, targets, sems):
     seq, row = place[1], place[2]
     depth = pieces[0].shape[2]
     starts = [pl.multiple_of(lax.rem(seq + by + SEQ, SEQ) * depth, depth) for by in NEAR]
@@ -252,7 +252,7 @@
         for i, piece in enumerate(pieces):
             copies = [
                 pltpu.make_async_copy(
-                    piece.at[m], slabs.at[n, :, pl.ds(start, depth)], sems.at[n, m]
+                    piece.at[m], targets[n].at[:, pl.ds(start, depth)], sems.at[n, m]
                 )
                 for m, start in enumerate(starts)
             ]
@@ -271,7 +271,7 @@
     _, tiles, depth, columns = pieces[0].shape
     return [
         pltpu.VMEM((count, tiles, SEQ * depth, columns), BF16),
-        pltpu.SemaphoreType.DMA((count, SEQ)),
+        pltpu.SemaphoreType.DMA((count + 1, SEQ)),
     ]
 
 
@@ -316,7 +316,7 @@
     pieces, refs = refs[:PIECES], refs[PIECES:]
     gain, offset, acc, pivot, sum1, sum2, slabs, sems = refs
     groups = [lax.rem(place[0] + away + CLASSES, CLASSES) for away in offsets]
-    copies = fetch(place, pieces, groups, slabs, sems)
+    copies = fetch(place, pieces, groups, [slabs.at[n] for n in range(count)], sems)
     lead = jnp.mean(parts[0][0].astype(F32), axis=1, keepdims=True)
     pivot[...] = jnp.broadcast_to(lead, (POS, HEAD_DIM))
     sum1[...] = jnp.zeros((POS, HEAD_DIM), F32)
@@ -336,15 +336,18 @@
     parts, refs = refs[:count], refs[count:]
     acc, pivot, sum1, sum2, *refs = refs
     pieces, refs = refs[:PIECES], refs[PIECES:]
-    gain, offset, acc_out, sum1_out, sum2_out, slabs, sems = refs
-    groups = [lax.rem(place[0] + away + CLASSES, CLASSES) for away in offsets]
-    copies = fetch(place, pieces, groups, slabs, sems)
+    gain, offset, acc_out, sum1_out, sum2_out, slab_out, slabs, sems = refs
+    groups = [lax.rem(place[0] + away + CLASSES, CLASSES) for away in (*offsets, SEQ)]
+    targets = [slabs.at[n] for n in range(count)] + [slab_out]
+    copies = fetch(place, pieces, groups, targets, sems)
     for n, part in enumerate(parts):
         blocks = [part.at[j] for j in range(SEQ)]
         before = (acc, sum1, sum2) if n == 0 else (acc_out, sum1_out, sum2_out)
         product = product_of(blocks, copies[n], slabs.at[n], gain, offset, groups[n])
         acc_out[...] = before[0][...] + product
         add_stats(blocks, pivot, before[1], before[2], sum1_out, sum2_out)
+    for copy in copies[count]:
+        copy.wait()
 
 
 def stage(kernel, offsets, place, parts, before, pieces, gain, offset):
@@ -352,7 +355,9 @@
     hidden = pieces[0].shape[1] * pieces[0].shape[3]
     stat = jax.ShapeDtypeStruct((POS, HEAD_DIM), F32)
     total = jax.ShapeDtypeStruct((POS + AUX, hidden), F32)
-    out_shape = (total, stat, stat) if before else (total, stat, stat, stat)
+    _, tiles, depth, columns = pieces[0].shape
+    slab = jax.ShapeDtypeStruct((tiles, SEQ * depth, columns), BF16)
+    out_shape = (total, stat, stat, slab) if before else (total, stat, stat, stat)
     return pl.pallas_call(
         functools.partial(kernel, offsets),
         out_shape=out_shape,
@@ -371,14 +376,11 @@
 
 
 def last_kernel(place, *refs):
-    acc, pivot, sum1, sum2, part, *refs = refs
-    pieces, refs = refs[:PIECES], refs[PIECES:]
-    gain, offset, bias, out, one, two, slabs, sems = refs
-    group = lax.rem(place[0] + 4, CLASSES)
-    (copies,) = fetch(place, pieces, [group], slabs, sems)
+    acc, pivot, sum1, sum2, part, slab, gain, offset, bias, out, one, two = refs
+    group = lax.rem(place[0] + SEQ, CLASSES)
     blocks = [part.at[j] for j in range(SEQ)]
     add_stats(blocks, pivot, sum1, sum2, one, two)
-    product = acc[...] + product_of(blocks, copies, slabs.at[0], gain, offset, group)
+    product = acc[...] + product_of(blocks, (), slab, gain, offset, group)
     mean1 = jnp.sum(one[...], axis=1, keepdims=True) * (1.0 / C)
     mean2 = jnp.sum(two[...], axis=1, keepdims=True) * (1.0 / C)
     centre = pivot[:, 0:1] + mean1
@@ -390,19 +392,18 @@
     out[...] = (0.5 * project * (1.0 + lax.erf(project * math.sqrt(0.5)))).astype(BF16)
 
 
-def last(place, acc, stats, part, pieces, gain, offset, bias):
-    vmem, here = pl.BlockSpec(memory_space=pltpu.VMEM), pl.BlockSpec(memory_space=pltpu.HBM)
-    hidden = pieces[0].shape[1] * pieces[0].shape[3]
+def last(place, acc, stats, part, slab, gain, offset, bias):
+    vmem = pl.BlockSpec(memory_space=pltpu.VMEM)
     return pl.pallas_call(
         last_kernel,
-        out_shape=jax.ShapeDtypeStruct((POS, hidden), BF16),
-        in_specs=[pl.BlockSpec(memory_space=pltpu.SMEM)] + [vmem] * 5 + [here] * PIECES + [vmem] * 3,
+        out_shape=jax.ShapeDtypeStruct((POS, bias.shape[1]), BF16),
+        in_specs=[pl.BlockSpec(memory_space=pltpu.SMEM)] + [vmem] * 9,
         out_specs=vmem,
-        scratch_shapes=[pltpu.VMEM((POS, HEAD_DIM), F32)] * 2 + slab_scratch(1, pieces),
+        scratch_shapes=[pltpu.VMEM((POS, HEAD_DIM), F32)] * 2,
         compiler_params=pltpu.CompilerParams(vmem_limit_bytes=16 << 20),
-        cost_estimate=pl.CostEstimate(flops=1 << 28, bytes_accessed=7 << 20, transcendentals=1 << 18),
+        cost_estimate=pl.CostEstimate(flops=1 << 28, bytes_accessed=4 << 20, transcendentals=1 << 18),
         name="last",
-    )(place, acc, *stats, part, *pieces, gain, offset, bias)
+    )(place, acc, *stats, part, slab, gain, offset, bias)
 
 
 def on_device(
@@ -439,17 +440,16 @@
     strides = [[i + CLASSES * j for j in range(SEQ)] for i in range(CLASSES)]
     own = lax.all_gather(convolved, "col", axis=0, tiled=True, axis_index_groups=strides)
     own = own.reshape(SEQ, POS, HEAD_DIM)
-    _, rows = lax.optimization_barrier((own, rows))
+    along_y = [rows] + [shift(rows, "row", 2 * by) for by in (1, 2, -1)]
+    own, *along_y = lax.optimization_barrier((own, *along_y))
     swap = [(i, i ^ 1) for i in range(lax.axis_size("row"))]
-    along_y = [rows] + [shift(rows, "row", 2 * by) for by in (1, 2, -1)]
-    pairs, up, down = [], own, own
+    other, pairs, up, down = [], [], own, own
     for n in range(3):
         up, down = shift(up, "col", 1), shift(down, "col", -1)
-        if n == 0:
-            down, *along_y[1:] = lax.optimization_barrier((down, *along_y[1:]))
-        if n == 1:
-            _, *along_y = lax.optimization_barrier((up, *along_y))
-            other = [lax.ppermute(piece, "row", swap) for piece in along_y]
+        if n:
+            two = [lax.ppermute(piece, "row", swap) for piece in along_y[2 * n - 2 : 2 * n]]
+            down, *two = lax.optimization_barrier((down, *two))
+            other += two
         pairs.append((up, down))
     depth_tiles = (SEQ, hidden // HEAD_DIM, depth, HEAD_DIM)
     pieces = [
@@ -460,10 +460,10 @@
     parts = (own, *pairs[0], *pairs[1])
     before = stage(first_kernel, (0, -1, 1, -2, 2), place, parts, (), pieces, gain, offset)
     up = shift(up, "col", 1)
-    acc, *sums = stage(more_kernel, (-3, 3), place, pairs[2], before, pieces, gain, offset)
+    acc, *sums, slab = stage(more_kernel, (-3, 3), place, pairs[2], before, pieces, gain, offset)
     pivot = before[1]
     bias = expand_bias.astype(F32).reshape(1, hidden)
-    out = last(place, acc, (pivot, *sums), up, pieces, gain, offset, bias)
+    out = last(place, acc, (pivot, *sums), up, slab, gain, offset, bias)
     return (
         residual.reshape(inputs.shape),
         out.reshape(inputs.shape[:3] + (hidden,)),

time: 173 us -> 176 us (1.017)
  the two profiles are of different devices: /device:TPU:10 before, /device:TPU:30 now
where the time goes in v7:
time: 176 us; the launch traced here: 175 us
  blocking collectives  58.8 us (33%)
  starting transfers between devices  52.3 us (30%)
  waiting for transfers between devices  39.8 us (23%)
  Pallas kernels  19.4 us (11%)
  local copies, waits for them, and re-layouts  3.74 us (2%)
    all_gather x1, blocking collectives, on_device(): lax.all_gather(convolved, 'col', axis=0, tiled=True, axis_index_groups=st...  58.8 us
    ppermute x13, starting transfers between devices, shift(): lax.ppermute(array, axis, [(i, (i + by) % peers) for i in range(peers)])  43.6 us
    ppermute x13, waiting for transfers between devices, shift(): lax.ppermute(array, axis, [(i, (i + by) % peers) for i in range(peers)])  39.8 us
    ppermute x4, starting transfers between devices, on_device(): lax.ppermute(piece, 'row', swap)  8.64 us
    pallas_call x2, Pallas kernels, stage(): pl.pallas_call(functools.partial(kernel, offsets), out_shape=out_shape, i...  7.81 us
    unnamed x26, local copies, waits for them, and re-layouts  3.73 us
  transfers between devices with their start and end apart: 17, of which 7 were waited for; matrix products, arithmetic and copies ran while one was open for 0% of the time, Pallas kernels for 6%

profile of v7, /device:TPU:30, one launch (start us, length us, event | category | flops | bytes accessed | tf_op | source)
XLA Modules:
  0.0 175.1 jit_solution(13806874808397426362)
XLA Ops:
  3.1 2.4 %collective-permute-start = (bf16[1920,128]{1,0:T(8,128)(2,1)S(1)}, bf16[1920,128]{1,0:T(8,128)(2,1)S(1)}, u32[]{:S(2)}, u32[]{:S(2)}) collective-permute-start(bf16[1920,128]{1,0:T(8,128)(2,1)S(1)} %get-tuple-element.33), channel_id=1, source_target_pairs={{0,256},{256,512},{512,768},{768,0},{1,257},{257,513},{513,769},{7... | collective-permute-start | bytes 1474568 | tf_op jit(solution)/shard_map/ppermute | solution.py:28
  5.5 3.5 %collective-permute-start.1 = (bf16[1920,128]{1,0:T(8,128)(2,1)S(1)}, bf16[1920,128]{1,0:T(8,128)(2,1)S(1)}, u32[]{:S(2)}, u32[]{:S(2)}) collective-permute-start(bf16[1920,128]{1,0:T(8,128)(2,1)S(1)} %get-tuple-element.34), channel_id=1, source_target_pairs={{0,768},{256,0},{512,256},{768,512},{1,769},{257,1},{513,257},{769... | collective-permute-start | bytes 1474568 | tf_op jit(solution)/shard_map/ppermute | solution.py:28
  8.9 3.3 %collective-permute-start.2 = (bf16[1536,128]{1,0:T(8,128)(2,1)S(1)}, bf16[1536,128]{1,0:T(8,128)(2,1)S(1)}, u32[]{:S(2)}, u32[]{:S(2)}) collective-permute-start(bf16[1536,128]{1,0:T(8,128)(2,1)S(1)} %get-tuple-element.31.kvw.kv), channel_id=1, source_target_pairs={{0,512},{256,768},{512,0},{768,256},{1,513},{257,769},{513,1},{769... | collective-permute-start | bytes 1179656 | tf_op jit(solution)/shard_map/ppermute | solution.py:28
  12.3 6.8 %collective-permute-done.above = bf16[1920,128]{1,0:T(8,128)(2,1)S(1)} collective-permute-done((bf16[1920,128]{1,0:T(8,128)(2,1)S(1)}, bf16[1920,128]{1,0:T(8,128)(2,1)S(1)}, u32[]{:S(2)}, u32[]{:S(2)}) %collective-permute-start) | collective-permute-done | bytes 491552 | tf_op jit(solution)/shard_map/ppermute | solution.py:28
  19.1 10.6 %collective-permute-done.1.below = bf16[1920,128]{1,0:T(8,128)(2,1)S(1)} collective-permute-done((bf16[1920,128]{1,0:T(8,128)(2,1)S(1)}, bf16[1920,128]{1,0:T(8,128)(2,1)S(1)}, u32[]{:S(2)}, u32[]{:S(2)}) %collective-permute-start.1) | collective-permute-done | bytes 491552 | tf_op jit(solution)/shard_map/ppermute | solution.py:28
  29.7 3.0 %near.1 = (f32[896,128]{1,0:T(8,128)S(1)}, f32[896,128]{1,0:T(8,128)S(1)}, f32[896,128]{1,0:T(8,128)S(1)}) custom-call(bf16[1536,128]{1,0:T(8,128)(2,1)S(1)} %get-tuple-element.31.kvw.kv, bf16[1024,128]{1,0:T(8,128)(2,1)S(1)} %get-tuple-element.32.qx, bf16[1920,128]{1,0:T(8,128)(2,1)S(1)} %collective-permute-done.above, ...), custom_call_target="tpu_custom_call" | custom-call | flops 704643072 | bytes 3145728 | tf_op jit(solution)/shard_map/near/pallas_call | solution.py:157
  32.8 3.5 %attend.1 = (bf16[512,128]{1,0:T(8,128)(2,1)}, bf16[512,128]{1,0:T(8,128)(2,1)S(1)}, bf16[2048,128]{1,0:T(8,128)(2,1)S(1)}) custom-call(s32[1]{0:T(128)} %bitcast.place, bf16[1536,128]{1,0:T(8,128)(2,1)S(1)} %get-tuple-element.31.kvw.kv, bf16[1024,128]{1,0:T(8,128)(2,1)S(1)} %get-tuple-element.32.qx, bf16[1920,128]{1,0:T(8,128)(2,1)S(1)} %collective-permute-done.above, ...), custom_call_target="tpu_custom_call" | custom-call | flops 234881024 | bytes 2097152 | tf_op jit(solution)/shard_map/attend/pallas_call | solution.py:221
  36.3 6.7 %collective-permute-start.3 = (bf16[2048,128]{1,0:T(8,128)(2,1)S(1)}, bf16[2048,128]{1,0:T(8,128)(2,1)S(1)}, u32[]{:S(2)}, u32[]{:S(2)}) collective-permute-start(bf16[2048,128]{1,0:T(8,128)(2,1)S(1)} %get-tuple-element.42), channel_id=1, source_target_pairs={{0,64},{32,96},{64,128},{96,160},{128,192},{160,224},{192,0},{224,... | collective-permute-start | bytes 1572872 | tf_op jit(solution)/shard_map/ppermute | solution.py:28
  43.0 1.9 %collective-permute-start.4 = (bf16[2048,128]{1,0:T(8,128)(2,1)S(1)}, bf16[2048,128]{1,0:T(8,128)(2,1)}, u32[]{:S(2)}, u32[]{:S(2)}) collective-permute-start(bf16[2048,128]{1,0:T(8,128)(2,1)S(1)} %get-tuple-element.42), channel_id=1, source_target_pairs={{0,128},{32,160},{64,192},{96,224},{128,0},{160,32},{192,64},{224,... | collective-permute-start | bytes 1572872 | tf_op jit(solution)/shard_map/ppermute | solution.py:28
  44.9 2.8 %collective-permute-start.5 = (bf16[2048,128]{1,0:T(8,128)(2,1)S(1)}, bf16[2048,128]{1,0:T(8,128)(2,1)}, u32[]{:S(2)}, u32[]{:S(2)}) collective-permute-start(bf16[2048,128]{1,0:T(8,128)(2,1)S(1)} %get-tuple-element.42), channel_id=1, source_target_pairs={{0,192},{32,224},{64,0},{96,32},{128,64},{160,96},{192,128},{224,1... | collective-permute-start | bytes 1572872 | tf_op jit(solution)/shard_map/ppermute | solution.py:28
  47.7 58.8 %all_gather.3 = bf16[2048,128]{1,0:T(8,128)(2,1)S(1)} all-gather(bf16[512,128]{1,0:T(8,128)(2,1)S(1)} %get-tuple-element.39), channel_id=1, replica_groups={{0,8,16,24},{1,9,17,25},{2,10,18,26},{3,11,19,27},{4,12,20,28},{5,13,21..., dimensions={0}, use_global_device_ids=true | all-gather | bytes 655360 | tf_op jit(solution)/shard_map/all_gather | solution.py:441
  106.5 3.2 %collective-permute-start.6 = (bf16[4,512,128]{2,1,0:T(8,128)(2,1)S(1)}, bf16[4,512,128]{2,1,0:T(8,128)(2,1)S(1)}, u32[]{:S(2)}, u32[]{:S(2)}) collective-permute-start(bf16[4,512,128]{2,1,0:T(8,128)(2,1)S(1)} %bitcast.30), channel_id=1, source_target_pairs={{0,1},{1,2},{2,3},{3,4},{4,5},{5,6},{6,7},{7,8},{8,9},{9,10},{10,1... | collective-permute-start | bytes 1572872 | tf_op jit(solution)/shard_map/ppermute | solution.py:28
  109.8 3.8 %collective-permute-start.9 = (bf16[4,512,128]{2,1,0:T(8,128)(2,1)S(1)}, bf16[4,512,128]{2,1,0:T(8,128)(2,1)S(1)}, u32[]{:S(2)}, u32[]{:S(2)}) collective-permute-start(bf16[4,512,128]{2,1,0:T(8,128)(2,1)S(1)} %bitcast.31), channel_id=1, source_target_pairs={{0,31},{1,0},{2,1},{3,2},{4,3},{5,4},{6,5},{7,6},{8,7},{9,8},{10,9... | collective-permute-start | bytes 1572872 | tf_op jit(solution)/shard_map/ppermute | solution.py:28
  113.6 9.7 %collective-permute-done.6.refs_1_ = bf16[4,512,128]{2,1,0:T(8,128)(2,1)S(1)} collective-permute-done((bf16[4,512,128]{2,1,0:T(8,128)(2,1)S(1)}, bf16[4,512,128]{2,1,0:T(8,128)(2,1)S(1)}, u32[]{:S(2)}, u32[]{:S(2)}) %collective-permute-start.6) | collective-permute-done | bytes 524320 | tf_op jit(solution)/shard_map/ppermute | solution.py:28
  123.3 3.1 %collective-permute-start.7 = (bf16[4,512,128]{2,1,0:T(8,128)(2,1)S(1)}, bf16[4,512,128]{2,1,0:T(8,128)(2,1)S(1)}, u32[]{:S(2)}, u32[]{:S(2)}) collective-permute-start(bf16[4,512,128]{2,1,0:T(8,128)(2,1)S(1)} %collective-permute-done.6.refs_1_), channel_id=1, source_target_pairs={{0,1},{1,2},{2,3},{3,4},{4,5},{5,6},{6,7},{7,8},{8,9},{9,10},{10,1... | collective-permute-start | bytes 1572872 | tf_op jit(solution)/shard_map/ppermute | solution.py:28
  128.3 2.4 %collective-permute-start.12 = (bf16[2048,128]{1,0:T(8,128)(2,1)S(1)}, bf16[2048,128]{1,0:T(8,128)(2,1)S(1)}, u32[]{:S(2)}, u32[]{:S(2)}) collective-permute-start(bf16[2048,128]{1,0:T(8,128)(2,1)S(1)} %collective-permute-done.3), channel_id=1, source_target_pairs={{0,32},{32,0},{64,96},{96,64},{128,160},{160,128},{192,224},{224,1... | collective-permute-start | bytes 1572872 | tf_op jit(solution)/shard_map/ppermute | solution.py:450
  130.7 4.0 %collective-permute-start.10 = (bf16[4,512,128]{2,1,0:T(8,128)(2,1)S(1)}, bf16[4,512,128]{2,1,0:T(8,128)(2,1)}, u32[]{:S(2)}, u32[]{:S(2)}) collective-permute-start(bf16[4,512,128]{2,1,0:T(8,128)(2,1)S(1)} %collective-permute-done.9.refs_2_), channel_id=1, source_target_pairs={{0,31},{1,0},{2,1},{3,2},{4,3},{5,4},{6,5},{7,6},{8,7},{9,8},{10,9... | collective-permute-start | bytes 1572872 | tf_op jit(solution)/shard_map/ppermute | solution.py:28
  140.2 2.4 %collective-permute-start.15 = (bf16[2048,128]{1,0:T(8,128)(2,1)}, bf16[2048,128]{1,0:T(8,128)(2,1)}, u32[]{:S(2)}, u32[]{:S(2)}) collective-permute-start(bf16[2048,128]{1,0:T(8,128)(2,1)} %collective-permute-done.5), channel_id=1, source_target_pairs={{0,32},{32,0},{64,96},{96,64},{128,160},{160,128},{192,224},{224,1... | collective-permute-start | bytes 1572872 | tf_op jit(solution)/shard_map/ppermute | solution.py:450
  142.7 3.9 %collective-permute-done.10.refs_4_ = bf16[4,512,128]{2,1,0:T(8,128)(2,1)} collective-permute-done((bf16[4,512,128]{2,1,0:T(8,128)(2,1)S(1)}, bf16[4,512,128]{2,1,0:T(8,128)(2,1)}, u32[]{:S(2)}, u32[]{:S(2)}) %collective-permute-start.10) | collective-permute-done | bytes 524320 | tf_op jit(solution)/shard_map/ppermute | solution.py:28
  146.6 5.2 %collective-permute-start.13 = (bf16[4,512,128]{2,1,0:T(8,128)(2,1)}, bf16[4,512,128]{2,1,0:T(8,128)(2,1)S(1)}, u32[]{:S(2)}, u32[]{:S(2)}) collective-permute-start(bf16[4,512,128]{2,1,0:T(8,128)(2,1)} %collective-permute-done.10.refs_4_), channel_id=1, source_target_pairs={{0,31},{1,0},{2,1},{3,2},{4,3},{5,4},{6,5},{7,6},{8,7},{9,8},{10,9... | collective-permute-start | bytes 1572872 | tf_op jit(solution)/shard_map/ppermute | solution.py:28
  154.2 8.3 %collective-permute-done.13.refs_1_ = bf16[4,512,128]{2,1,0:T(8,128)(2,1)S(1)} collective-permute-done((bf16[4,512,128]{2,1,0:T(8,128)(2,1)}, bf16[4,512,128]{2,1,0:T(8,128)(2,1)S(1)}, u32[]{:S(2)}, u32[]{:S(2)}) %collective-permute-start.13) | collective-permute-done | bytes 524320 | tf_op jit(solution)/shard_map/ppermute | solution.py:28
  164.6 4.9 %stage.2 = (f32[528,512]{1,0:T(8,128)S(1)}, f32[512,128]{1,0:T(8,128)S(1)}, f32[512,128]{1,0:T(8,128)S(1)}, f32[512,128]{1,0:T(8,128)S(1)}) custom-call(s32[3]{0:T(128)S(1)} %pad_add_fusion.place, bf16[4,512,128]{2,1,0:T(8,128)(2,1)S(1)} %bitcast.32, bf16[4,512,128]{2,1,0:T(8,128)(2,1)S(1)} %collective-permute-done.6.refs_1_, ...), custom_call_target="tpu_custom_call" | custom-call | flops 1342177280 | bytes 5242880 | tf_op jit(solution)/shard_map/stage/pallas_call | solution.py:361
  169.6 2.9 %stage.3 = (f32[528,512]{1,0:T(8,128)S(1)}, f32[512,128]{1,0:T(8,128)S(1)}, f32[512,128]{1,0:T(8,128)S(1)}, bf16[4,512,128]{2,1,0:T(8,128)(2,1)S(1)}) custom-call(s32[3]{0:T(128)S(1)} %pad_add_fusion.place, bf16[4,512,128]{2,1,0:T(8,128)(2,1)S(1)} %collective-permute-done.8.refs_0_, bf16[4,512,128]{2,1,0:T(8,128)(2,1)S(1)} %collective-permute-done.13.refs_1_, ...), custom_call_target="tpu_custom_call" | custom-call | flops 536870912 | bytes 2097152 | tf_op jit(solution)/shard_map/stage/pallas_call | solution.py:361
  172.5 2.7 %last.1 = bf16[512,512]{1,0:T(8,128)(2,1)} custom-call(s32[3]{0:T(128)S(1)} %pad_add_fusion.place, f32[528,512]{1,0:T(8,128)S(1)} %get-tuple-element.56.refs_0_, f32[512,128]{1,0:T(8,128)S(1)} %get-tuple-element.53.refs_3_.refs_1_, f32[512,128]{1,0:T(8,128)S(1)} %get-tuple-element.57.refs_2_, f32[512,128]{1,0:T(8,128)S(1)} %get-tuple-element.58.refs_3_, ...), custom_call_target="tpu_custom_call" | custom-call | flops 268435456 | bytes 4194304 | tf_op jit(solution)/shard_map/last/pallas_call | solution.py:397
  (50 shorter events, 14.4 us)
Async XLA Ops:
  0.6 11.7 %copy-start.12 = (bf16[128]{0:T(256)(128)(2,1)S(1)}, bf16[128]{0:T(256)(128)(2,1)}, u32[]{:S(2)}) copy-start(bf16[128]{0:T(256)(128)(2,1)} %param.15) | copy-start | bytes 772
  3.1 16.0 %collective-permute-start = (bf16[1920,128]{1,0:T(8,128)(2,1)S(1)}, bf16[1920,128]{1,0:T(8,128)(2,1)S(1)}, u32[]{:S(2)}, u32[]{:S(2)}) collective-permute-start(bf16[1920,128]{1,0:T(8,128)(2,1)S(1)} %get-tuple-element.33), channel_id=1, source_target_pairs={{0,256},{256,512},{512,768},{768,0},{1,257},{257,513},{513,769},{7... | collective-permute-start | bytes 1474568 | tf_op jit(solution)/shard_map/ppermute | solution.py:28
  5.5 24.2 %collective-permute-start.1 = (bf16[1920,128]{1,0:T(8,128)(2,1)S(1)}, bf16[1920,128]{1,0:T(8,128)(2,1)S(1)}, u32[]{:S(2)}, u32[]{:S(2)}) collective-permute-start(bf16[1920,128]{1,0:T(8,128)(2,1)S(1)} %get-tuple-element.34), channel_id=1, source_target_pairs={{0,768},{256,0},{512,256},{768,512},{1,769},{257,1},{513,257},{769... | collective-permute-start | bytes 1474568 | tf_op jit(solution)/shard_map/ppermute | solution.py:28
  8.9 23.8 %collective-permute-start.2 = (bf16[1536,128]{1,0:T(8,128)(2,1)S(1)}, bf16[1536,128]{1,0:T(8,128)(2,1)S(1)}, u32[]{:S(2)}, u32[]{:S(2)}) collective-permute-start(bf16[1536,128]{1,0:T(8,128)(2,1)S(1)} %get-tuple-element.31.kvw.kv), channel_id=1, source_target_pairs={{0,512},{256,768},{512,0},{768,256},{1,513},{257,769},{513,1},{769... | collective-permute-start | bytes 1179656 | tf_op jit(solution)/shard_map/ppermute | solution.py:28
  32.7 121.3 %copy-start.8 = (bf16[4096]{0:T(1024)(128)(2,1)S(1)}, bf16[4096]{0:T(1024)(128)(2,1)}, u32[]{:S(2)}) copy-start(bf16[4096]{0:T(1024)(128)(2,1)} %param.16) | copy-start | bytes 24580
  32.8 121.3 %copy-start.11 = (bf16[512]{0:T(512)(128)(2,1)S(1)}, bf16[512]{0:T(512)(128)(2,1)}, u32[]{:S(2)}) copy-start(bf16[512]{0:T(512)(128)(2,1)} %param.19) | copy-start | bytes 3076
  32.8 121.4 %copy-start.10 = (bf16[4096]{0:T(1024)(128)(2,1)S(1)}, bf16[4096]{0:T(1024)(128)(2,1)}, u32[]{:S(2)}) copy-start(bf16[4096]{0:T(1024)(128)(2,1)} %param.17) | copy-start | bytes 24580
  36.3 126.3 %copy-start = (bf16[2048,128]{1,0:T(8,128)(2,1)}, bf16[2048,128]{1,0:T(8,128)(2,1)S(1)}, u32[]{:S(2)}) copy-start(bf16[2048,128]{1,0:T(8,128)(2,1)S(1)} %get-tuple-element.42) | copy-start | bytes 1572868
  36.3 70.2 %collective-permute-start.3 = (bf16[2048,128]{1,0:T(8,128)(2,1)S(1)}, bf16[2048,128]{1,0:T(8,128)(2,1)S(1)}, u32[]{:S(2)}, u32[]{:S(2)}) collective-permute-start(bf16[2048,128]{1,0:T(8,128)(2,1)S(1)} %get-tuple-element.42), channel_id=1, source_target_pairs={{0,64},{32,96},{64,128},{96,160},{128,192},{160,224},{192,0},{224,... | collective-permute-start | bytes 1572872 | tf_op jit(solution)/shard_map/ppermute | solution.py:28
  43.0 63.5 %collective-permute-start.4 = (bf16[2048,128]{1,0:T(8,128)(2,1)S(1)}, bf16[2048,128]{1,0:T(8,128)(2,1)}, u32[]{:S(2)}, u32[]{:S(2)}) collective-permute-start(bf16[2048,128]{1,0:T(8,128)(2,1)S(1)} %get-tuple-element.42), channel_id=1, source_target_pairs={{0,128},{32,160},{64,192},{96,224},{128,0},{160,32},{192,64},{224,... | collective-permute-start | bytes 1572872 | tf_op jit(solution)/shard_map/ppermute | solution.py:28
  44.9 61.6 %collective-permute-start.5 = (bf16[2048,128]{1,0:T(8,128)(2,1)S(1)}, bf16[2048,128]{1,0:T(8,128)(2,1)}, u32[]{:S(2)}, u32[]{:S(2)}) collective-permute-start(bf16[2048,128]{1,0:T(8,128)(2,1)S(1)} %get-tuple-element.42), channel_id=1, source_target_pairs={{0,192},{32,224},{64,0},{96,32},{128,64},{160,96},{192,128},{224,1... | collective-permute-start | bytes 1572872 | tf_op jit(solution)/shard_map/ppermute | solution.py:28
  106.5 45.6 %copy-start.5 = (bf16[2048,128]{1,0:T(8,128)(2,1)}, bf16[2048,128]{1,0:T(8,128)(2,1)S(1)}, u32[]{:S(2)}) copy-start(bf16[2048,128]{1,0:T(8,128)(2,1)S(1)} %collective-permute-done.3) | copy-start | bytes 1572868
  106.5 16.7 %collective-permute-start.6 = (bf16[4,512,128]{2,1,0:T(8,128)(2,1)S(1)}, bf16[4,512,128]{2,1,0:T(8,128)(2,1)S(1)}, u32[]{:S(2)}, u32[]{:S(2)}) collective-permute-start(bf16[4,512,128]{2,1,0:T(8,128)(2,1)S(1)} %bitcast.30), channel_id=1, source_target_pairs={{0,1},{1,2},{2,3},{3,4},{4,5},{5,6},{6,7},{7,8},{8,9},{9,10},{10,1... | collective-permute-start | bytes 1572872 | tf_op jit(solution)/shard_map/ppermute | solution.py:28
  109.8 20.9 %collective-permute-start.9 = (bf16[4,512,128]{2,1,0:T(8,128)(2,1)S(1)}, bf16[4,512,128]{2,1,0:T(8,128)(2,1)S(1)}, u32[]{:S(2)}, u32[]{:S(2)}) collective-permute-start(bf16[4,512,128]{2,1,0:T(8,128)(2,1)S(1)} %bitcast.31), channel_id=1, source_target_pairs={{0,31},{1,0},{2,1},{3,2},{4,3},{5,4},{6,5},{7,6},{8,7},{9,8},{10,9... | collective-permute-start | bytes 1572872 | tf_op jit(solution)/shard_map/ppermute | solution.py:28
  123.3 12.3 %collective-permute-start.7 = (bf16[4,512,128]{2,1,0:T(8,128)(2,1)S(1)}, bf16[4,512,128]{2,1,0:T(8,128)(2,1)S(1)}, u32[]{:S(2)}, u32[]{:S(2)}) collective-permute-start(bf16[4,512,128]{2,1,0:T(8,128)(2,1)S(1)} %collective-permute-done.6.refs_1_), channel_id=1, source_target_pairs={{0,1},{1,2},{2,3},{3,4},{4,5},{5,6},{6,7},{7,8},{8,9},{9,10},{10,1... | collective-permute-start | bytes 1572872 | tf_op jit(solution)/shard_map/ppermute | solution.py:28
  126.4 13.8 %collective-permute-start.11 = (bf16[2048,128]{1,0:T(8,128)(2,1)S(1)}, bf16[2048,128]{1,0:T(8,128)(2,1)S(1)}, u32[]{:S(2)}, u32[]{:S(2)}) collective-permute-start(bf16[2048,128]{1,0:T(8,128)(2,1)S(1)} %get-tuple-element.42), channel_id=1, source_target_pairs={{0,32},{32,0},{64,96},{96,64},{128,160},{160,128},{192,224},{224,1... | collective-permute-start | bytes 1572872 | tf_op jit(solution)/shard_map/ppermute | solution.py:450
  128.3 14.3 %collective-permute-start.12 = (bf16[2048,128]{1,0:T(8,128)(2,1)S(1)}, bf16[2048,128]{1,0:T(8,128)(2,1)S(1)}, u32[]{:S(2)}, u32[]{:S(2)}) collective-permute-start(bf16[2048,128]{1,0:T(8,128)(2,1)S(1)} %collective-permute-done.3), channel_id=1, source_target_pairs={{0,32},{32,0},{64,96},{96,64},{128,160},{160,128},{192,224},{224,1... | collective-permute-start | bytes 1572872 | tf_op jit(solution)/shard_map/ppermute | solution.py:450
  130.7 15.8 %collective-permute-start.10 = (bf16[4,512,128]{2,1,0:T(8,128)(2,1)S(1)}, bf16[4,512,128]{2,1,0:T(8,128)(2,1)}, u32[]{:S(2)}, u32[]{:S(2)}) collective-permute-start(bf16[4,512,128]{2,1,0:T(8,128)(2,1)S(1)} %collective-permute-done.9.refs_2_), channel_id=1, source_target_pairs={{0,31},{1,0},{2,1},{3,2},{4,3},{5,4},{6,5},{7,6},{8,7},{9,8},{10,9... | collective-permute-start | bytes 1572872 | tf_op jit(solution)/shard_map/ppermute | solution.py:28
  135.5 16.6 %collective-permute-start.8 = (bf16[4,512,128]{2,1,0:T(8,128)(2,1)S(1)}, bf16[4,512,128]{2,1,0:T(8,128)(2,1)S(1)}, u32[]{:S(2)}, u32[]{:S(2)}) collective-permute-start(bf16[4,512,128]{2,1,0:T(8,128)(2,1)S(1)} %collective-permute-done.7.refs_3_), channel_id=1, source_target_pairs={{0,1},{1,2},{2,3},{3,4},{4,5},{5,6},{6,7},{7,8},{8,9},{9,10},{10,1... | collective-permute-start | bytes 1572872 | tf_op jit(solution)/shard_map/ppermute | solution.py:28
  138.3 15.9 %collective-permute-start.14 = (bf16[2048,128]{1,0:T(8,128)(2,1)}, bf16[2048,128]{1,0:T(8,128)(2,1)}, u32[]{:S(2)}, u32[]{:S(2)}) collective-permute-start(bf16[2048,128]{1,0:T(8,128)(2,1)} %collective-permute-done.4), channel_id=1, source_target_pairs={{0,32},{32,0},{64,96},{96,64},{128,160},{160,128},{192,224},{224,1... | collective-permute-start | bytes 1572872 | tf_op jit(solution)/shard_map/ppermute | solution.py:450
  140.2 11.9 %copy-start.6 = (bf16[2048,128]{1,0:T(8,128)(2,1)}, bf16[2048,128]{1,0:T(8,128)(2,1)S(1)}, u32[]{:S(2)}) copy-start(bf16[2048,128]{1,0:T(8,128)(2,1)S(1)} %collective-permute-done.11) | copy-start | bytes 1572868
  140.2 14.0 %collective-permute-start.15 = (bf16[2048,128]{1,0:T(8,128)(2,1)}, bf16[2048,128]{1,0:T(8,128)(2,1)}, u32[]{:S(2)}, u32[]{:S(2)}) collective-permute-start(bf16[2048,128]{1,0:T(8,128)(2,1)} %collective-permute-done.5), channel_id=1, source_target_pairs={{0,32},{32,0},{64,96},{96,64},{128,160},{160,128},{192,224},{224,1... | collective-permute-start | bytes 1572872 | tf_op jit(solution)/shard_map/ppermute | solution.py:450
  146.6 16.0 %collective-permute-start.13 = (bf16[4,512,128]{2,1,0:T(8,128)(2,1)}, bf16[4,512,128]{2,1,0:T(8,128)(2,1)S(1)}, u32[]{:S(2)}, u32[]{:S(2)}) collective-permute-start(bf16[4,512,128]{2,1,0:T(8,128)(2,1)} %collective-permute-done.10.refs_4_), channel_id=1, source_target_pairs={{0,31},{1,0},{2,1},{3,2},{4,3},{5,4},{6,5},{7,6},{8,7},{9,8},{10,9... | collective-permute-start | bytes 1572872 | tf_op jit(solution)/shard_map/ppermute | solution.py:28
  152.1 20.3 %collective-permute-start.16 = (bf16[4,512,128]{2,1,0:T(8,128)(2,1)S(1)}, bf16[4,512,128]{2,1,0:T(8,128)(2,1)S(1)}, u32[]{:S(2)}, u32[]{:S(2)}) collective-permute-start(bf16[4,512,128]{2,1,0:T(8,128)(2,1)S(1)} %collective-permute-done.8.refs_0_), channel_id=1, source_target_pairs={{0,1},{1,2},{2,3},{3,4},{4,5},{5,6},{6,7},{7,8},{8,9},{9,10},{10,1... | collective-permute-start | bytes 1572872 | tf_op jit(solution)/shard_map/ppermute | solution.py:28
  (6 other events, 24.8 us)

commit v8 on v5

--- a/solution.py
+++ b/solution.py
@@ -199,7 +199,7 @@
                 for i in range(ROWS):
                     sums[i] = sums[i] + columns[i + a] * tap
         for i in range(ROWS):
-            conv[i * IMG_W + c0 : i * IMG_W + c0 + wide] = sums[i].astype(BF16)
+            conv[i, c0 : c0 + wide] = sums[i].astype(BF16)
 
 
 def attend(place, qx, above, below, far, begun, taps, bias):
@@ -208,7 +208,7 @@
     flops = (POS + 2 * EDGE) * SEQ * POS * HEAD_DIM
     return pl.pallas_call(
         attend_kernel,
-        out_shape=(out, out),
+        out_shape=(out, jax.ShapeDtypeStruct((ROWS, IMG_W, HEAD_DIM), BF16)),
         in_specs=[pl.BlockSpec(memory_space=pltpu.SMEM)] + [vmem] * 9,
         out_specs=(vmem, vmem),
         scratch_shapes=[
@@ -225,14 +225,14 @@
 AUX = 16
 
 
-def fetch(weights, groups, slabs, sems):
+def fetch(weights, groups, targets, sems):
     copies = []
     for n, group in enumerate(groups):
         rows = weights.shape[2]
         copies.append(
             [
                 pltpu.make_async_copy(
-                    weights.at[j, group], slabs.at[n, j * rows : (j + 1) * rows], sems.at[n, j]
+                    weights.at[j, group], targets[n].at[j * rows : (j + 1) * rows], sems.at[n, j]
                 )
                 for j in range(SEQ)
             ]
@@ -246,7 +246,7 @@
     _, _, rows, columns = weights.shape
     return [
         pltpu.VMEM((count, SEQ * rows, columns), BF16),
-        pltpu.SemaphoreType.DMA((count, SEQ)),
+        pltpu.SemaphoreType.DMA((count + 1, SEQ)),
     ]
 
 
@@ -289,7 +289,7 @@
     parts, refs = refs[:count], refs[count:]
     weights, gain, offset, acc, pivot, sum1, sum2, slabs, sems = refs
     groups = [lax.rem(place[0] + away + CLASSES, CLASSES) for away in offsets]
-    copies = fetch(weights, groups, slabs, sems)
+    copies = fetch(weights, groups, [slabs.at[n] for n in range(count)], sems)
     lead = jnp.mean(parts[0][0].astype(F32), axis=1, keepdims=True)
     pivot[...] = jnp.broadcast_to(lead, (POS, HEAD_DIM))
     sum1[...] = jnp.zeros((POS, HEAD_DIM), F32)
@@ -307,15 +307,19 @@
 def more_kernel(offsets, place, *refs):
     count = len(offsets)
     parts, refs = refs[:count], refs[count:]
-    acc, pivot, sum1, sum2, weights, gain, offset, acc_out, sum1_out, sum2_out, slabs, sems = refs
-    groups = [lax.rem(place[0] + away + CLASSES, CLASSES) for away in offsets]
-    copies = fetch(weights, groups, slabs, sems)
+    acc, pivot, sum1, sum2, weights, gain, offset, *refs = refs
+    acc_out, sum1_out, sum2_out, slab_out, slabs, sems = refs
+    groups = [lax.rem(place[0] + away + CLASSES, CLASSES) for away in (*offsets, SEQ)]
+    targets = [slabs.at[n] for n in range(count)] + [slab_out]
+    copies = fetch(weights, groups, targets, sems)
     for n, part in enumerate(parts):
         blocks = [part.at[j] for j in range(SEQ)]
         before = (acc, sum1, sum2) if n == 0 else (acc_out, sum1_out, sum2_out)
         product = product_of(blocks, copies[n], slabs.at[n], gain, offset, groups[n])
         acc_out[...] = before[0][...] + product
         add_stats(blocks, pivot, before[1], before[2], sum1_out, sum2_out)
+    for copy in copies[count]:
+        copy.wait()
 
 
 def stage(kernel, offsets, place, parts, before, weights, gain, offset):
@@ -323,7 +327,8 @@
     hidden = weights.shape[-1]
     stat = jax.ShapeDtypeStruct((POS, HEAD_DIM), F32)
     total = jax.ShapeDtypeStruct((POS + AUX, hidden), F32)
-    out_shape = (total, stat, stat) if before else (total, stat, stat, stat)
+    slab = jax.ShapeDtypeStruct((SEQ * weights.shape[2], hidden), BF16)
+    out_shape = (total, stat, stat, slab) if before else (total, stat, stat, stat)
     return pl.pallas_call(
         functools.partial(kernel, offsets),
         out_shape=out_shape,
@@ -341,12 +346,11 @@
 
 
 def last_kernel(place, *refs):
-    acc, pivot, sum1, sum2, part, weights, gain, offset, bias, out, one, two, slabs, sems = refs
-    group = lax.rem(place[0] + 4, CLASSES)
-    (copies,) = fetch(weights, [group], slabs, sems)
+    acc, pivot, sum1, sum2, part, slab, gain, offset, bias, out, one, two = refs
+    group = lax.rem(place[0] + SEQ, CLASSES)
     blocks = [part.at[j] for j in range(SEQ)]
     add_stats(blocks, pivot, sum1, sum2, one, two)
-    product = acc[...] + product_of(blocks, copies, slabs.at[0], gain, offset, group)
+    product = acc[...] + product_of(blocks, (), slab, gain, offset, group)
     mean1 = jnp.sum(one[...], axis=1, keepdims=True) * (1.0 / C)
     mean2 = jnp.sum(two[...], axis=1, keepdims=True) * (1.0 / C)
     centre = pivot[:, 0:1] + mean1
@@ -358,19 +362,18 @@
     out[...] = (0.5 * project * (1.0 + lax.erf(project * math.sqrt(0.5)))).astype(BF16)
 
 
-def last(place, acc, stats, part, weights, gain, offset, bias):
-    vmem, here = pl.BlockSpec(memory_space=pltpu.VMEM), pl.BlockSpec(memory_space=pltpu.HBM)
-    hidden = weights.shape[-1]
+def last(place, acc, stats, part, slab, gain, offset, bias):
+    vmem = pl.BlockSpec(memory_space=pltpu.VMEM)
     return pl.pallas_call(
         last_kernel,
-        out_shape=jax.ShapeDtypeStruct((POS, hidden), BF16),
-        in_specs=[pl.BlockSpec(memory_space=pltpu.SMEM)] + [vmem] * 5 + [here] + [vmem] * 3,
+        out_shape=jax.ShapeDtypeStruct((POS, bias.shape[1]), BF16),
+        in_specs=[pl.BlockSpec(memory_space=pltpu.SMEM)] + [vmem] * 9,
         out_specs=vmem,
-        scratch_shapes=[pltpu.VMEM((POS, HEAD_DIM), F32)] * 2 + slab_scratch(1, weights),
+        scratch_shapes=[pltpu.VMEM((POS, HEAD_DIM), F32)] * 2,
         compiler_params=pltpu.CompilerParams(vmem_limit_bytes=16 << 20),
-        cost_estimate=pl.CostEstimate(flops=1 << 28, bytes_accessed=7 << 20, transcendentals=1 << 18),
+        cost_estimate=pl.CostEstimate(flops=1 << 28, bytes_accessed=4 << 20, transcendentals=1 << 18),
         name="last",
-    )(place, acc, *stats, part, weights, gain, offset, bias)
+    )(place, acc, *stats, part, slab, gain, offset, bias)
 
 
 def on_device(
@@ -420,10 +423,10 @@
     up, before = lax.optimization_barrier((up, before))
     pairs[2] = (up, down)
     up = shift(up, "col", 1)
-    acc, *sums = stage(more_kernel, (-3, 3), place, pairs[2], before, weights, gain, offset)
+    acc, *sums, slab = stage(more_kernel, (-3, 3), place, pairs[2], before, weights, gain, offset)
     pivot = before[1]
     bias = expand_bias.astype(F32).reshape(1, hidden)
-    out = last(place, acc, (pivot, *sums), up, weights, gain, offset, bias)
+    out = last(place, acc, (pivot, *sums), up, slab, gain, offset, bias)
     return (
         residual.reshape(inputs.shape),
         out.reshape(inputs.shape[:3] + (hidden,)),

time: 169 us -> 168 us (level)
  the two profiles are of different devices: /device:TPU:8 before, /device:TPU:6 now
where the time goes in v8:
time: 168 us; the launch traced here: 167 us
  blocking collectives  53 us (32%)
  starting transfers between devices  45 us (27%)
  waiting for transfers between devices  36 us (21%)
  Pallas kernels  18.8 us (11%)
  between operations  14.3 us (9%)
    all_gather x1, blocking collectives, on_device(): lax.all_gather(convolved, 'col', axis=0, tiled=True, axis_index_groups=st...  53 us
    ppermute x10, starting transfers between devices, shift(): lax.ppermute(array, axis, [(i, (i + by) % peers) for i in range(peers)])  45 us
    ppermute x10, waiting for transfers between devices, shift(): lax.ppermute(array, axis, [(i, (i + by) % peers) for i in range(peers)])  35.9 us
    pallas_call x2, Pallas kernels, stage(): pl.pallas_call(functools.partial(kernel, offsets), out_shape=out_shape, i...  7.11 us
    pallas_call x1, Pallas kernels, attend(): pl.pallas_call(attend_kernel, out_shape=(out, jax.ShapeDtypeStruct((ROWS,...  3.46 us
  transfers between devices with their start and end apart: 11, of which 7 were waited for; matrix products, arithmetic and copies ran while one was open for 0% of the time, Pallas kernels for 9%

profile of v8, /device:TPU:6, one launch (start us, length us, event | category | flops | bytes accessed | tf_op | source)
XLA Modules:
  0.0 167.2 jit_solution(14466420182581018113)
XLA Ops:
  7.2 1.9 %scale.1 = (bf16[1024,128]{1,0:T(8,128)(2,1)S(1)}, bf16[1408,128]{1,0:T(8,128)(2,1)S(1)}, bf16[128,512]{1,0:T(8,128)(2,1)}) custom-call(s32[1]{0:T(128)} %bitcast.5.place, bf16[512,128]{1,0:T(8,128)(2,1)} %bitcast.27, bf16[512,128]{1,0:T(8,128)(2,1)} %bitcast.29, bf16[512,128]{1,0:T(8,128)(2,1)} %bitcast.31, bf16[512,128]{1,0:T(8,128)(2,1)} %bitcast.33, ...), custom_call_target="tpu_custom_call" | custom-call | tf_op jit(solution)/shard_map/scale/pallas_call | solution.py:88
  9.2 1.2 pack.1
  10.3 15.0 %collective-permute-start = (bf16[1408,128]{1,0:T(8,128)(2,1)S(1)}, bf16[1408,128]{1,0:T(8,128)(2,1)S(1)}, u32[]{:S(2)}, u32[]{:S(2)}) collective-permute-start(bf16[1408,128]{1,0:T(8,128)(2,1)S(1)} %get-tuple-element.26), channel_id=1, source_target_pairs={{0,256},{256,512},{512,768},{768,0},{1,257},{257,513},{513,769},{7... | collective-permute-start | bytes 1081352 | tf_op jit(solution)/shard_map/ppermute | solution.py:28
  25.4 1.9 %collective-permute-start.1 = (bf16[1408,128]{1,0:T(8,128)(2,1)S(1)}, bf16[1408,128]{1,0:T(8,128)(2,1)S(1)}, u32[]{:S(2)}, u32[]{:S(2)}) collective-permute-start(bf16[1408,128]{1,0:T(8,128)(2,1)S(1)} %get-tuple-element.27), channel_id=1, source_target_pairs={{0,768},{256,0},{512,256},{768,512},{1,769},{257,1},{513,257},{769... | collective-permute-start | bytes 1081352 | tf_op jit(solution)/shard_map/ppermute | solution.py:28
  27.3 3.4 %collective-permute-start.2 = (bf16[1024,128]{1,0:T(8,128)(2,1)S(1)}, bf16[1024,128]{1,0:T(8,128)(2,1)S(1)}, u32[]{:S(2)}, u32[]{:S(2)}) collective-permute-start(bf16[1024,128]{1,0:T(8,128)(2,1)S(1)} %get-tuple-element.28.kv), channel_id=1, source_target_pairs={{0,512},{256,768},{512,0},{768,256},{1,513},{257,769},{513,1},{769... | collective-permute-start | bytes 786440 | tf_op jit(solution)/shard_map/ppermute | solution.py:28
  30.8 8.0 %collective-permute-done.1.below = bf16[1408,128]{1,0:T(8,128)(2,1)S(1)} collective-permute-done((bf16[1408,128]{1,0:T(8,128)(2,1)S(1)}, bf16[1408,128]{1,0:T(8,128)(2,1)S(1)}, u32[]{:S(2)}, u32[]{:S(2)}) %collective-permute-start.1) | collective-permute-done | bytes 360480 | tf_op jit(solution)/shard_map/ppermute | solution.py:28
  38.7 3.1 %near.1 = (f32[896,128]{1,0:T(8,128)S(1)}, f32[896,128]{1,0:T(8,128)S(1)}, f32[896,128]{1,0:T(8,128)S(1)}) custom-call(bf16[1024,128]{1,0:T(8,128)(2,1)S(1)} %get-tuple-element.28.kv, bf16[1024,128]{1,0:T(8,128)(2,1)S(1)} %get-tuple-element.25.qx, bf16[1408,128]{1,0:T(8,128)(2,1)S(1)} %collective-permute-done.above, ...), custom_call_target="tpu_custom_call" | custom-call | flops 704643072 | bytes 3145728 | tf_op jit(solution)/shard_map/near/pallas_call | solution.py:152
  41.9 3.5 %attend.1 = (bf16[512,128]{1,0:T(8,128)(2,1)}, bf16[8,64,128]{2,1,0:T(8,128)(2,1)S(1)}) custom-call(s32[1]{0:T(128)} %bitcast.place, bf16[1024,128]{1,0:T(8,128)(2,1)S(1)} %get-tuple-element.25.qx, bf16[1408,128]{1,0:T(8,128)(2,1)S(1)} %collective-permute-done.above, bf16[1408,128]{1,0:T(8,128)(2,1)S(1)} %collective-permute-done.1.below, ...), custom_call_target="tpu_custom_call" | custom-call | flops 234881024 | bytes 2097152 | tf_op jit(solution)/shard_map/attend/pallas_call | solution.py:209
  45.3 53.0 %all_gather.6 = bf16[32,64,128]{2,1,0:T(8,128)(2,1)S(1)} all-gather(bf16[8,64,128]{2,1,0:T(8,128)(2,1)S(1)} %get-tuple-element.33), channel_id=1, replica_groups={{0,8,16,24},{1,9,17,25},{2,10,18,26},{3,11,19,27},{4,12,20,28},{5,13,21..., dimensions={0}, use_global_device_ids=true | all-gather | bytes 655360 | tf_op jit(solution)/shard_map/all_gather | solution.py:414
  98.4 4.7 %collective-permute-start.3 = (bf16[4,512,128]{2,1,0:T(8,128)(2,1)S(1)}, bf16[4,512,128]{2,1,0:T(8,128)(2,1)S(1)}, u32[]{:S(2)}, u32[]{:S(2)}) collective-permute-start(bf16[4,512,128]{2,1,0:T(8,128)(2,1)S(1)} %bitcast.20), channel_id=1, source_target_pairs={{0,1},{1,2},{2,3},{3,4},{4,5},{5,6},{6,7},{7,8},{8,9},{9,10},{10,1... | collective-permute-start | bytes 1572872 | tf_op jit(solution)/shard_map/ppermute | solution.py:28
  103.0 2.4 %collective-permute-start.6 = (bf16[4,512,128]{2,1,0:T(8,128)(2,1)S(1)}, bf16[4,512,128]{2,1,0:T(8,128)(2,1)S(1)}, u32[]{:S(2)}, u32[]{:S(2)}) collective-permute-start(bf16[4,512,128]{2,1,0:T(8,128)(2,1)S(1)} %bitcast.21), channel_id=1, source_target_pairs={{0,31},{1,0},{2,1},{3,2},{4,3},{5,4},{6,5},{7,6},{8,7},{9,8},{10,9... | collective-permute-start | bytes 1572872 | tf_op jit(solution)/shard_map/ppermute | solution.py:28
  105.4 7.7 %collective-permute-done.3.refs_1_ = bf16[4,512,128]{2,1,0:T(8,128)(2,1)S(1)} collective-permute-done((bf16[4,512,128]{2,1,0:T(8,128)(2,1)S(1)}, bf16[4,512,128]{2,1,0:T(8,128)(2,1)S(1)}, u32[]{:S(2)}, u32[]{:S(2)}) %collective-permute-start.3) | collective-permute-done | bytes 524320 | tf_op jit(solution)/shard_map/ppermute | solution.py:28
  113.1 4.3 %collective-permute-start.4 = (bf16[4,512,128]{2,1,0:T(8,128)(2,1)S(1)}, bf16[4,512,128]{2,1,0:T(8,128)(2,1)}, u32[]{:S(2)}, u32[]{:S(2)}) collective-permute-start(bf16[4,512,128]{2,1,0:T(8,128)(2,1)S(1)} %collective-permute-done.3.refs_1_), channel_id=1, source_target_pairs={{0,1},{1,2},{2,3},{3,4},{4,5},{5,6},{6,7},{7,8},{8,9},{9,10},{10,1... | collective-permute-start | bytes 1572872 | tf_op jit(solution)/shard_map/ppermute | solution.py:28
  117.6 2.8 %collective-permute-start.7 = (bf16[4,512,128]{2,1,0:T(8,128)(2,1)S(1)}, bf16[4,512,128]{2,1,0:T(8,128)(2,1)S(1)}, u32[]{:S(2)}, u32[]{:S(2)}) collective-permute-start(bf16[4,512,128]{2,1,0:T(8,128)(2,1)S(1)} %collective-permute-done.6.refs_2_), channel_id=1, source_target_pairs={{0,31},{1,0},{2,1},{3,2},{4,3},{5,4},{6,5},{7,6},{8,7},{9,8},{10,9... | collective-permute-start | bytes 1572872 | tf_op jit(solution)/shard_map/ppermute | solution.py:28
  120.4 8.3 %collective-permute-done.4.refs_3_ = bf16[4,512,128]{2,1,0:T(8,128)(2,1)} collective-permute-done((bf16[4,512,128]{2,1,0:T(8,128)(2,1)S(1)}, bf16[4,512,128]{2,1,0:T(8,128)(2,1)}, u32[]{:S(2)}, u32[]{:S(2)}) %collective-permute-start.4) | collective-permute-done | bytes 524320 | tf_op jit(solution)/shard_map/ppermute | solution.py:28
  128.7 4.0 %collective-permute-start.5 = (bf16[4,512,128]{2,1,0:T(8,128)(2,1)}, bf16[4,512,128]{2,1,0:T(8,128)(2,1)S(1)}, u32[]{:S(2)}, u32[]{:S(2)}) collective-permute-start(bf16[4,512,128]{2,1,0:T(8,128)(2,1)} %collective-permute-done.4.refs_3_), channel_id=1, source_target_pairs={{0,1},{1,2},{2,3},{3,4},{4,5},{5,6},{6,7},{7,8},{8,9},{9,10},{10,1... | collective-permute-start | bytes 1572872 | tf_op jit(solution)/shard_map/ppermute | solution.py:28
  132.8 0.6 collective-permute-done.7.refs_4_
  133.3 3.2 %collective-permute-start.8 = (bf16[4,512,128]{2,1,0:T(8,128)(2,1)S(1)}, bf16[4,512,128]{2,1,0:T(8,128)(2,1)S(1)}, u32[]{:S(2)}, u32[]{:S(2)}) collective-permute-start(bf16[4,512,128]{2,1,0:T(8,128)(2,1)S(1)} %collective-permute-done.7.refs_4_), channel_id=1, source_target_pairs={{0,31},{1,0},{2,1},{3,2},{4,3},{5,4},{6,5},{7,6},{8,7},{9,8},{10,9... | collective-permute-start | bytes 1572872 | tf_op jit(solution)/shard_map/ppermute | solution.py:28
  136.6 4.8 %stage.2 = (f32[528,512]{1,0:T(8,128)S(1)}, f32[512,128]{1,0:T(8,128)S(1)}, f32[512,128]{1,0:T(8,128)S(1)}, f32[512,128]{1,0:T(8,128)S(1)}) custom-call(s32[1]{0:T(128)} %bitcast.9.place, bf16[4,512,128]{2,1,0:T(8,128)(2,1)S(1)} %bitcast.22, bf16[4,512,128]{2,1,0:T(8,128)(2,1)S(1)} %collective-permute-done.3.refs_1_, ...), custom_call_target="tpu_custom_call" | custom-call | flops 1342177280 | bytes 5242880 | tf_op jit(solution)/shard_map/stage/pallas_call | solution.py:332
  141.4 4.5 %collective-permute-done.5.refs_0_ = bf16[4,512,128]{2,1,0:T(8,128)(2,1)S(1)} collective-permute-done((bf16[4,512,128]{2,1,0:T(8,128)(2,1)}, bf16[4,512,128]{2,1,0:T(8,128)(2,1)S(1)}, u32[]{:S(2)}, u32[]{:S(2)}) %collective-permute-start.5) | collective-permute-done | bytes 524320 | tf_op jit(solution)/shard_map/ppermute | solution.py:28
  145.9 3.3 %collective-permute-start.9 = (bf16[4,512,128]{2,1,0:T(8,128)(2,1)S(1)}, bf16[4,512,128]{2,1,0:T(8,128)(2,1)S(1)}, u32[]{:S(2)}, u32[]{:S(2)}) collective-permute-start(bf16[4,512,128]{2,1,0:T(8,128)(2,1)S(1)} %collective-permute-done.5.refs_0_), channel_id=1, source_target_pairs={{0,1},{1,2},{2,3},{3,4},{4,5},{5,6},{6,7},{7,8},{8,9},{9,10},{10,1... | collective-permute-start | bytes 1572872 | tf_op jit(solution)/shard_map/ppermute | solution.py:28
  149.3 2.3 %stage.3 = (f32[528,512]{1,0:T(8,128)S(1)}, f32[512,128]{1,0:T(8,128)S(1)}, f32[512,128]{1,0:T(8,128)S(1)}, bf16[512,512]{1,0:T(8,128)(2,1)S(1)}) custom-call(s32[1]{0:T(128)} %bitcast.9.place, bf16[4,512,128]{2,1,0:T(8,128)(2,1)S(1)} %collective-permute-done.5.refs_0_, bf16[4,512,128]{2,1,0:T(8,128)(2,1)S(1)} %collective-permute-done.8.refs_1_, ...), custom_call_target="tpu_custom_call" | custom-call | flops 536870912 | bytes 2097152 | tf_op jit(solution)/shard_map/stage/pallas_call | solution.py:332
  151.6 6.7 %collective-permute-done.9.refs_4_ = bf16[4,512,128]{2,1,0:T(8,128)(2,1)S(1)} collective-permute-done((bf16[4,512,128]{2,1,0:T(8,128)(2,1)S(1)}, bf16[4,512,128]{2,1,0:T(8,128)(2,1)S(1)}, u32[]{:S(2)}, u32[]{:S(2)}) %collective-permute-start.9) | collective-permute-done | bytes 524320 | tf_op jit(solution)/shard_map/ppermute | solution.py:28
  158.3 2.1 %last.1 = bf16[512,512]{1,0:T(8,128)(2,1)} custom-call(s32[1]{0:T(128)} %bitcast.9.place, f32[528,512]{1,0:T(8,128)S(1)} %get-tuple-element.44.refs_0_, f32[512,128]{1,0:T(8,128)S(1)} %get-tuple-element.41.refs_3_.refs_1_, f32[512,128]{1,0:T(8,128)S(1)} %get-tuple-element.45.refs_2_, f32[512,128]{1,0:T(8,128)S(1)} %get-tuple-element.46.refs_3_, ...), custom_call_target="tpu_custom_call" | custom-call | flops 268435456 | bytes 4194304 | tf_op jit(solution)/shard_map/last/pallas_call | solution.py:367
  (22 shorter events, 0.3 us)
Async XLA Ops:
  7.2 23.5 %copy-start.1 = (bf16[7,7,128]{2,1,0:T(8,128)(2,1)S(1)}, bf16[7,7,128]{2,1,0:T(8,128)(2,1)}, u32[]{:S(2)}) copy-start(bf16[7,7,128]{2,1,0:T(8,128)(2,1)} %param.14) | copy-start | bytes 37636
  7.2 23.6 %copy-start.4 = (bf16[128]{0:T(256)(128)(2,1)S(1)}, bf16[128]{0:T(256)(128)(2,1)}, u32[]{:S(2)}) copy-start(bf16[128]{0:T(256)(128)(2,1)} %param.15) | copy-start | bytes 772
  7.2 129.4 %all-gather.2.cloned.1.call-start = ((), (), s32[]{:S(2)}) async-start(), calls=%async_computation | async-start | bytes 4325376 | tf_op jit(solution)/shard_map/all_gather | solution.py:402
  10.3 20.4 %collective-permute-start = (bf16[1408,128]{1,0:T(8,128)(2,1)S(1)}, bf16[1408,128]{1,0:T(8,128)(2,1)S(1)}, u32[]{:S(2)}, u32[]{:S(2)}) collective-permute-start(bf16[1408,128]{1,0:T(8,128)(2,1)S(1)} %get-tuple-element.26), channel_id=1, source_target_pairs={{0,256},{256,512},{512,768},{768,0},{1,257},{257,513},{513,769},{7... | collective-permute-start | bytes 1081352 | tf_op jit(solution)/shard_map/ppermute | solution.py:28
  25.4 13.3 %collective-permute-start.1 = (bf16[1408,128]{1,0:T(8,128)(2,1)S(1)}, bf16[1408,128]{1,0:T(8,128)(2,1)S(1)}, u32[]{:S(2)}, u32[]{:S(2)}) collective-permute-start(bf16[1408,128]{1,0:T(8,128)(2,1)S(1)} %get-tuple-element.27), channel_id=1, source_target_pairs={{0,768},{256,0},{512,256},{768,512},{1,769},{257,1},{513,257},{769... | collective-permute-start | bytes 1081352 | tf_op jit(solution)/shard_map/ppermute | solution.py:28
  27.3 14.5 %collective-permute-start.2 = (bf16[1024,128]{1,0:T(8,128)(2,1)S(1)}, bf16[1024,128]{1,0:T(8,128)(2,1)S(1)}, u32[]{:S(2)}, u32[]{:S(2)}) collective-permute-start(bf16[1024,128]{1,0:T(8,128)(2,1)S(1)} %get-tuple-element.28.kv), channel_id=1, source_target_pairs={{0,512},{256,768},{512,0},{768,256},{1,513},{257,769},{513,1},{769... | collective-permute-start | bytes 786440 | tf_op jit(solution)/shard_map/ppermute | solution.py:28
  41.8 90.9 %copy-start = (bf16[4096]{0:T(1024)(128)(2,1)S(1)}, bf16[4096]{0:T(1024)(128)(2,1)}, u32[]{:S(2)}) copy-start(bf16[4096]{0:T(1024)(128)(2,1)} %param.16) | copy-start | bytes 24580
  41.9 90.9 %copy-start.2 = (bf16[4096]{0:T(1024)(128)(2,1)S(1)}, bf16[4096]{0:T(1024)(128)(2,1)}, u32[]{:S(2)}) copy-start(bf16[4096]{0:T(1024)(128)(2,1)} %param.17) | copy-start | bytes 24580
  98.4 14.8 %collective-permute-start.3 = (bf16[4,512,128]{2,1,0:T(8,128)(2,1)S(1)}, bf16[4,512,128]{2,1,0:T(8,128)(2,1)S(1)}, u32[]{:S(2)}, u32[]{:S(2)}) collective-permute-start(bf16[4,512,128]{2,1,0:T(8,128)(2,1)S(1)} %bitcast.20), channel_id=1, source_target_pairs={{0,1},{1,2},{2,3},{3,4},{4,5},{5,6},{6,7},{7,8},{8,9},{9,10},{10,1... | collective-permute-start | bytes 1572872 | tf_op jit(solution)/shard_map/ppermute | solution.py:28
  103.0 14.6 %collective-permute-start.6 = (bf16[4,512,128]{2,1,0:T(8,128)(2,1)S(1)}, bf16[4,512,128]{2,1,0:T(8,128)(2,1)S(1)}, u32[]{:S(2)}, u32[]{:S(2)}) collective-permute-start(bf16[4,512,128]{2,1,0:T(8,128)(2,1)S(1)} %bitcast.21), channel_id=1, source_target_pairs={{0,31},{1,0},{2,1},{3,2},{4,3},{5,4},{6,5},{7,6},{8,7},{9,8},{10,9... | collective-permute-start | bytes 1572872 | tf_op jit(solution)/shard_map/ppermute | solution.py:28
  113.1 15.6 %collective-permute-start.4 = (bf16[4,512,128]{2,1,0:T(8,128)(2,1)S(1)}, bf16[4,512,128]{2,1,0:T(8,128)(2,1)}, u32[]{:S(2)}, u32[]{:S(2)}) collective-permute-start(bf16[4,512,128]{2,1,0:T(8,128)(2,1)S(1)} %collective-permute-done.3.refs_1_), channel_id=1, source_target_pairs={{0,1},{1,2},{2,3},{3,4},{4,5},{5,6},{6,7},{7,8},{8,9},{9,10},{10,1... | collective-permute-start | bytes 1572872 | tf_op jit(solution)/shard_map/ppermute | solution.py:28
  117.6 15.7 %collective-permute-start.7 = (bf16[4,512,128]{2,1,0:T(8,128)(2,1)S(1)}, bf16[4,512,128]{2,1,0:T(8,128)(2,1)S(1)}, u32[]{:S(2)}, u32[]{:S(2)}) collective-permute-start(bf16[4,512,128]{2,1,0:T(8,128)(2,1)S(1)} %collective-permute-done.6.refs_2_), channel_id=1, source_target_pairs={{0,31},{1,0},{2,1},{3,2},{4,3},{5,4},{6,5},{7,6},{8,7},{9,8},{10,9... | collective-permute-start | bytes 1572872 | tf_op jit(solution)/shard_map/ppermute | solution.py:28
  128.7 17.2 %collective-permute-start.5 = (bf16[4,512,128]{2,1,0:T(8,128)(2,1)}, bf16[4,512,128]{2,1,0:T(8,128)(2,1)S(1)}, u32[]{:S(2)}, u32[]{:S(2)}) collective-permute-start(bf16[4,512,128]{2,1,0:T(8,128)(2,1)} %collective-permute-done.4.refs_3_), channel_id=1, source_target_pairs={{0,1},{1,2},{2,3},{3,4},{4,5},{5,6},{6,7},{7,8},{8,9},{9,10},{10,1... | collective-permute-start | bytes 1572872 | tf_op jit(solution)/shard_map/ppermute | solution.py:28
  133.3 16.0 %collective-permute-start.8 = (bf16[4,512,128]{2,1,0:T(8,128)(2,1)S(1)}, bf16[4,512,128]{2,1,0:T(8,128)(2,1)S(1)}, u32[]{:S(2)}, u32[]{:S(2)}) collective-permute-start(bf16[4,512,128]{2,1,0:T(8,128)(2,1)S(1)} %collective-permute-done.7.refs_4_), channel_id=1, source_target_pairs={{0,31},{1,0},{2,1},{3,2},{4,3},{5,4},{6,5},{7,6},{8,7},{9,8},{10,9... | collective-permute-start | bytes 1572872 | tf_op jit(solution)/shard_map/ppermute | solution.py:28
  136.6 12.7 %copy-start.3 = (bf16[512]{0:T(512)(128)(2,1)S(1)}, bf16[512]{0:T(512)(128)(2,1)}, u32[]{:S(2)}) copy-start(bf16[512]{0:T(512)(128)(2,1)} %param.19) | copy-start | bytes 3076
  145.9 12.3 %collective-permute-start.9 = (bf16[4,512,128]{2,1,0:T(8,128)(2,1)S(1)}, bf16[4,512,128]{2,1,0:T(8,128)(2,1)S(1)}, u32[]{:S(2)}, u32[]{:S(2)}) collective-permute-start(bf16[4,512,128]{2,1,0:T(8,128)(2,1)S(1)} %collective-permute-done.5.refs_0_), channel_id=1, source_target_pairs={{0,1},{1,2},{2,3},{3,4},{4,5},{5,6},{6,7},{7,8},{8,9},{9,10},{10,1... | collective-permute-start | bytes 1572872 | tf_op jit(solution)/shard_map/ppermute | solution.py:28
Sparse Core Ops, SparseCore 0:
  12.9 89.0 all-gather.1

commit v9 on v8

--- a/solution.py
+++ b/solution.py
@@ -135,8 +135,9 @@
     return highest, total, summed
 
 
-def near_kernel(kv, qx, above, below, summed_out, peak_out, total_out, qs):
+def near_kernel(kv, qx, above, below, summed_out, peak_out, total_out, qs, xs):
     spread_rows(above, qx[0:POS], below, qs, 2 * POS)
+    spread_rows(above, qx[POS:], below, xs, 2 * POS + EDGE)
     for t in range(TALL // 2):
         own = slice(t * TILE, (t + 1) * TILE)
         peak, total, summed = weigh(qs[own], (kv, above, below), None)
@@ -151,19 +152,16 @@
     flops = 3 * (POS + 2 * EDGE) * SEQ * POS * HEAD_DIM
     return pl.pallas_call(
         near_kernel,
-        out_shape=(out,) * 3,
+        out_shape=(out,) * 3 + (jax.ShapeDtypeStruct(out.shape, BF16),) * 2,
         in_specs=[vmem] * 4,
-        out_specs=(vmem,) * 3,
-        scratch_shapes=[pltpu.VMEM((POS + 2 * EDGE, HEAD_DIM), BF16)],
+        out_specs=(vmem,) * 5,
         compiler_params=pltpu.CompilerParams(vmem_limit_bytes=16 << 20),
         cost_estimate=pl.CostEstimate(flops=flops, bytes_accessed=3 << 20, transcendentals=2 << 20),
         name="near",
     )(kv, qx, above, below)
 
 
-def attend_kernel(place, qx, above, below, far, summed_in, peak_in, total_in, taps, bias, res, conv, qs, xs, image):
-    spread_rows(above, qx[0:POS], below, qs, 2 * POS)
-    spread_rows(above, qx[POS:], below, xs, 2 * POS + EDGE)
+def attend_kernel(place, far, summed_in, peak_in, total_in, qs, xs, taps, bias, res, conv, image):
     tall = TALL
     blank = jnp.zeros((tall, 8, HEAD_DIM), F32)
     image[:, 0:LEFT, :] = blank
@@ -202,24 +200,22 @@
             conv[i, c0 : c0 + wide] = sums[i].astype(BF16)
 
 
-def attend(place, qx, above, below, far, begun, taps, bias):
+def attend(place, far, begun, taps, bias):
     out = jax.ShapeDtypeStruct((POS, HEAD_DIM), BF16)
     vmem = pl.BlockSpec(memory_space=pltpu.VMEM)
     flops = (POS + 2 * EDGE) * SEQ * POS * HEAD_DIM
     return pl.pallas_call(
         attend_kernel,
         out_shape=(out, jax.ShapeDtypeStruct((ROWS, IMG_W, HEAD_DIM), BF16)),
-        in_specs=[pl.BlockSpec(memory_space=pltpu.SMEM)] + [vmem] * 9,
+        in_specs=[pl.BlockSpec(memory_space=pltpu.SMEM)] + [vmem] * 8,
         out_specs=(vmem, vmem),
         scratch_shapes=[
-            pltpu.VMEM((POS + 2 * EDGE, HEAD_DIM), BF16),
-            pltpu.VMEM((POS + 2 * EDGE, HEAD_DIM), BF16),
             pltpu.VMEM((TALL, IMG_W + 16, HEAD_DIM), F32),
         ],
         compiler_params=pltpu.CompilerParams(vmem_limit_bytes=16 << 20),
         cost_estimate=pl.CostEstimate(flops=flops, bytes_accessed=2 << 20, transcendentals=1 << 19),
         name="attend",
-    )(place, qx, above, below, far, *begun, taps, bias)
+    )(place, far, *begun, taps, bias)
 
 
 AUX = 16
@@ -407,7 +403,7 @@
     bias = depth_bias.astype(F32).reshape(1, HEAD_DIM)
     begun = near(kv, qx, above, below)
     residual, convolved = attend(
-        seq.astype(jnp.int32).reshape(1), qx, above, below, far, begun, taps, bias
+        seq.astype(jnp.int32).reshape(1), far, begun, taps, bias
     )
 
     strides = [[i + CLASSES * j for j in range(SEQ)] for i in range(CLASSES)]

time: 168 us -> 169 us (level)
  waiting for transfers between devices: 36 us -> 38.7 us
    ppermute x10, waiting for transfers between devices: 35.9 us -> 38.7 us  [shift(): lax.ppermute(array, axis, [(i, (i + by) % peers) for i in range(peers)])]
where the time goes in v9:
time: 169 us
  blocking collectives  52.2 us (31%)
  starting transfers between devices  44.4 us (26%)
  waiting for transfers between devices  38.7 us (23%)
  Pallas kernels  18.9 us (11%)
  between operations  14.3 us (8%)
    all_gather x1, blocking collectives, on_device(): lax.all_gather(convolved, 'col', axis=0, tiled=True, axis_index_groups=st...  52.2 us
    ppermute x10, starting transfers between devices, shift(): lax.ppermute(array, axis, [(i, (i + by) % peers) for i in range(peers)])  44.3 us
    ppermute x10, waiting for transfers between devices, shift(): lax.ppermute(array, axis, [(i, (i + by) % peers) for i in range(peers)])  38.7 us
    pallas_call x2, Pallas kernels, stage(): pl.pallas_call(functools.partial(kernel, offsets), out_shape=out_shape, i...  7.11 us
    pallas_call x1, Pallas kernels, attend(): pl.pallas_call(attend_kernel, out_shape=(out, jax.ShapeDtypeStruct((ROWS,...  3.44 us
  transfers between devices with their start and end apart: 11, of which 7 were waited for; matrix products, arithmetic and copies ran while one was open for 0% of the time, Pallas kernels for 9%

profile of v9, /device:TPU:6, one launch (start us, length us, event | category | flops | bytes accessed | tf_op | source)
XLA Modules:
  0.0 168.5 jit_solution(11671428808974576358)
XLA Ops:
  7.2 1.9 %scale.1 = (bf16[1024,128]{1,0:T(8,128)(2,1)S(1)}, bf16[1408,128]{1,0:T(8,128)(2,1)S(1)}, bf16[128,512]{1,0:T(8,128)(2,1)}) custom-call(s32[1]{0:T(128)} %bitcast.1.place, bf16[512,128]{1,0:T(8,128)(2,1)} %bitcast.27, bf16[512,128]{1,0:T(8,128)(2,1)} %bitcast.29, bf16[512,128]{1,0:T(8,128)(2,1)} %bitcast.31, bf16[512,128]{1,0:T(8,128)(2,1)} %bitcast.33, ...), custom_call_target="tpu_custom_call" | custom-call | tf_op jit(solution)/shard_map/scale/pallas_call | solution.py:88
  9.2 1.2 pack.1
  10.3 15.0 %collective-permute-start.1 = (bf16[1408,128]{1,0:T(8,128)(2,1)S(1)}, bf16[1408,128]{1,0:T(8,128)(2,1)S(1)}, u32[]{:S(2)}, u32[]{:S(2)}) collective-permute-start(bf16[1408,128]{1,0:T(8,128)(2,1)S(1)} %get-tuple-element.29), channel_id=1, source_target_pairs={{0,256},{256,512},{512,768},{768,0},{1,257},{257,513},{513,769},{7... | collective-permute-start | bytes 1081352 | tf_op jit(solution)/shard_map/ppermute | solution.py:28
  25.4 1.9 %collective-permute-start.2 = (bf16[1408,128]{1,0:T(8,128)(2,1)S(1)}, bf16[1408,128]{1,0:T(8,128)(2,1)S(1)}, u32[]{:S(2)}, u32[]{:S(2)}) collective-permute-start(bf16[1408,128]{1,0:T(8,128)(2,1)S(1)} %get-tuple-element.30), channel_id=1, source_target_pairs={{0,768},{256,0},{512,256},{768,512},{1,769},{257,1},{513,257},{769... | collective-permute-start | bytes 1081352 | tf_op jit(solution)/shard_map/ppermute | solution.py:28
  27.3 3.4 %collective-permute-start = (bf16[1024,128]{1,0:T(8,128)(2,1)S(1)}, bf16[1024,128]{1,0:T(8,128)(2,1)S(1)}, u32[]{:S(2)}, u32[]{:S(2)}) collective-permute-start(bf16[1024,128]{1,0:T(8,128)(2,1)S(1)} %get-tuple-element.27.kv), channel_id=1, source_target_pairs={{0,512},{256,768},{512,0},{768,256},{1,513},{257,769},{513,1},{769... | collective-permute-start | bytes 786440 | tf_op jit(solution)/shard_map/ppermute | solution.py:28
  30.8 8.0 %collective-permute-done.2.below = bf16[1408,128]{1,0:T(8,128)(2,1)S(1)} collective-permute-done((bf16[1408,128]{1,0:T(8,128)(2,1)S(1)}, bf16[1408,128]{1,0:T(8,128)(2,1)S(1)}, u32[]{:S(2)}, u32[]{:S(2)}) %collective-permute-start.2) | collective-permute-done | bytes 360480 | tf_op jit(solution)/shard_map/ppermute | solution.py:28
  38.7 3.1 %near.1 = (f32[896,128]{1,0:T(8,128)S(1)}, f32[896,128]{1,0:T(8,128)S(1)}, f32[896,128]{1,0:T(8,128)S(1)}, bf16[896,128]{1,0:T(8,128)(2,1)S(1)}, bf16[896,128]{1,0:T(8,128)(2,1)S(1)}) custom-call(bf16[1024,128]{1,0:T(8,128)(2,1)S(1)} %get-tuple-element.27.kv, bf16[1024,128]{1,0:T(8,128)(2,1)S(1)} %get-tuple-element.28.qx, ...), custom_call_target="tpu_custom_call" | custom-call | flops 704643072 | bytes 3145728 | tf_op jit(solution)/shard_map/near/pallas_call | solution.py:153
  41.9 3.4 %attend.1 = (bf16[512,128]{1,0:T(8,128)(2,1)}, bf16[8,64,128]{2,1,0:T(8,128)(2,1)S(1)}) custom-call(s32[1]{0:T(128)} %bitcast.place, bf16[1024,128]{1,0:T(8,128)(2,1)S(1)} %collective-permute-done.far, f32[896,128]{1,0:T(8,128)S(1)} %get-tuple-element.31.summed_in, f32[896,128]{1,0:T(8,128)S(1)} %get-tuple-element.32.peak_in, ...), custom_call_target="tpu_custom_call" | custom-call | flops 234881024 | bytes 2097152 | tf_op jit(solution)/shard_map/attend/pallas_call | solution.py:207
  45.4 52.2 %all_gather.6 = bf16[32,64,128]{2,1,0:T(8,128)(2,1)S(1)} all-gather(bf16[8,64,128]{2,1,0:T(8,128)(2,1)S(1)} %get-tuple-element.37), channel_id=1, replica_groups={{0,8,16,24},{1,9,17,25},{2,10,18,26},{3,11,19,27},{4,12,20,28},{5,13,21..., dimensions={0}, use_global_device_ids=true | all-gather | bytes 655360 | tf_op jit(solution)/shard_map/all_gather | solution.py:410
  97.6 5.2 %collective-permute-start.3 = (bf16[4,512,128]{2,1,0:T(8,128)(2,1)S(1)}, bf16[4,512,128]{2,1,0:T(8,128)(2,1)S(1)}, u32[]{:S(2)}, u32[]{:S(2)}) collective-permute-start(bf16[4,512,128]{2,1,0:T(8,128)(2,1)S(1)} %bitcast.20), channel_id=1, source_target_pairs={{0,1},{1,2},{2,3},{3,4},{4,5},{5,6},{6,7},{7,8},{8,9},{9,10},{10,1... | collective-permute-start | bytes 1572872 | tf_op jit(solution)/shard_map/ppermute | solution.py:28
  102.7 1.9 %collective-permute-start.6 = (bf16[4,512,128]{2,1,0:T(8,128)(2,1)S(1)}, bf16[4,512,128]{2,1,0:T(8,128)(2,1)S(1)}, u32[]{:S(2)}, u32[]{:S(2)}) collective-permute-start(bf16[4,512,128]{2,1,0:T(8,128)(2,1)S(1)} %bitcast.21), channel_id=1, source_target_pairs={{0,31},{1,0},{2,1},{3,2},{4,3},{5,4},{6,5},{7,6},{8,7},{9,8},{10,9... | collective-permute-start | bytes 1572872 | tf_op jit(solution)/shard_map/ppermute | solution.py:28
  104.7 8.0 %collective-permute-done.3.refs_1_ = bf16[4,512,128]{2,1,0:T(8,128)(2,1)S(1)} collective-permute-done((bf16[4,512,128]{2,1,0:T(8,128)(2,1)S(1)}, bf16[4,512,128]{2,1,0:T(8,128)(2,1)S(1)}, u32[]{:S(2)}, u32[]{:S(2)}) %collective-permute-start.3) | collective-permute-done | bytes 524320 | tf_op jit(solution)/shard_map/ppermute | solution.py:28
  112.7 4.4 %collective-permute-start.4 = (bf16[4,512,128]{2,1,0:T(8,128)(2,1)S(1)}, bf16[4,512,128]{2,1,0:T(8,128)(2,1)}, u32[]{:S(2)}, u32[]{:S(2)}) collective-permute-start(bf16[4,512,128]{2,1,0:T(8,128)(2,1)S(1)} %collective-permute-done.3.refs_1_), channel_id=1, source_target_pairs={{0,1},{1,2},{2,3},{3,4},{4,5},{5,6},{6,7},{7,8},{8,9},{9,10},{10,1... | collective-permute-start | bytes 1572872 | tf_op jit(solution)/shard_map/ppermute | solution.py:28
  117.0 0.2 collective-permute-done.6.refs_2_
  117.2 2.5 %collective-permute-start.7 = (bf16[4,512,128]{2,1,0:T(8,128)(2,1)S(1)}, bf16[4,512,128]{2,1,0:T(8,128)(2,1)S(1)}, u32[]{:S(2)}, u32[]{:S(2)}) collective-permute-start(bf16[4,512,128]{2,1,0:T(8,128)(2,1)S(1)} %collective-permute-done.6.refs_2_), channel_id=1, source_target_pairs={{0,31},{1,0},{2,1},{3,2},{4,3},{5,4},{6,5},{7,6},{8,7},{9,8},{10,9... | collective-permute-start | bytes 1572872 | tf_op jit(solution)/shard_map/ppermute | solution.py:28
  119.7 8.9 %collective-permute-done.4.refs_3_ = bf16[4,512,128]{2,1,0:T(8,128)(2,1)} collective-permute-done((bf16[4,512,128]{2,1,0:T(8,128)(2,1)S(1)}, bf16[4,512,128]{2,1,0:T(8,128)(2,1)}, u32[]{:S(2)}, u32[]{:S(2)}) %collective-permute-start.4) | collective-permute-done | bytes 524320 | tf_op jit(solution)/shard_map/ppermute | solution.py:28
  128.6 3.6 %collective-permute-start.5 = (bf16[4,512,128]{2,1,0:T(8,128)(2,1)}, bf16[4,512,128]{2,1,0:T(8,128)(2,1)S(1)}, u32[]{:S(2)}, u32[]{:S(2)}) collective-permute-start(bf16[4,512,128]{2,1,0:T(8,128)(2,1)} %collective-permute-done.4.refs_3_), channel_id=1, source_target_pairs={{0,1},{1,2},{2,3},{3,4},{4,5},{5,6},{6,7},{7,8},{8,9},{9,10},{10,1... | collective-permute-start | bytes 1572872 | tf_op jit(solution)/shard_map/ppermute | solution.py:28
  132.4 4.5 %collective-permute-start.8 = (bf16[4,512,128]{2,1,0:T(8,128)(2,1)S(1)}, bf16[4,512,128]{2,1,0:T(8,128)(2,1)S(1)}, u32[]{:S(2)}, u32[]{:S(2)}) collective-permute-start(bf16[4,512,128]{2,1,0:T(8,128)(2,1)S(1)} %collective-permute-done.7.refs_4_), channel_id=1, source_target_pairs={{0,31},{1,0},{2,1},{3,2},{4,3},{5,4},{6,5},{7,6},{8,7},{9,8},{10,9... | collective-permute-start | bytes 1572872 | tf_op jit(solution)/shard_map/ppermute | solution.py:28
  137.0 4.8 %stage.2 = (f32[528,512]{1,0:T(8,128)S(1)}, f32[512,128]{1,0:T(8,128)S(1)}, f32[512,128]{1,0:T(8,128)S(1)}, f32[512,128]{1,0:T(8,128)S(1)}) custom-call(s32[1]{0:T(128)} %bitcast.9.place, bf16[4,512,128]{2,1,0:T(8,128)(2,1)S(1)} %bitcast.22, bf16[4,512,128]{2,1,0:T(8,128)(2,1)S(1)} %collective-permute-done.3.refs_1_, ...), custom_call_target="tpu_custom_call" | custom-call | flops 1342177280 | bytes 5242880 | tf_op jit(solution)/shard_map/stage/pallas_call | solution.py:328
  141.8 5.5 %collective-permute-done.5.refs_0_ = bf16[4,512,128]{2,1,0:T(8,128)(2,1)S(1)} collective-permute-done((bf16[4,512,128]{2,1,0:T(8,128)(2,1)}, bf16[4,512,128]{2,1,0:T(8,128)(2,1)S(1)}, u32[]{:S(2)}, u32[]{:S(2)}) %collective-permute-start.5) | collective-permute-done | bytes 524320 | tf_op jit(solution)/shard_map/ppermute | solution.py:28
  147.3 1.9 %collective-permute-start.9 = (bf16[4,512,128]{2,1,0:T(8,128)(2,1)S(1)}, bf16[4,512,128]{2,1,0:T(8,128)(2,1)S(1)}, u32[]{:S(2)}, u32[]{:S(2)}) collective-permute-start(bf16[4,512,128]{2,1,0:T(8,128)(2,1)S(1)} %collective-permute-done.5.refs_0_), channel_id=1, source_target_pairs={{0,1},{1,2},{2,3},{3,4},{4,5},{5,6},{6,7},{7,8},{8,9},{9,10},{10,1... | collective-permute-start | bytes 1572872 | tf_op jit(solution)/shard_map/ppermute | solution.py:28
  149.2 2.3 %stage.3 = (f32[528,512]{1,0:T(8,128)S(1)}, f32[512,128]{1,0:T(8,128)S(1)}, f32[512,128]{1,0:T(8,128)S(1)}, bf16[512,512]{1,0:T(8,128)(2,1)S(1)}) custom-call(s32[1]{0:T(128)} %bitcast.9.place, bf16[4,512,128]{2,1,0:T(8,128)(2,1)S(1)} %collective-permute-done.5.refs_0_, bf16[4,512,128]{2,1,0:T(8,128)(2,1)S(1)} %collective-permute-done.8.refs_1_, ...), custom_call_target="tpu_custom_call" | custom-call | flops 536870912 | bytes 2097152 | tf_op jit(solution)/shard_map/stage/pallas_call | solution.py:328
  151.5 8.0 %collective-permute-done.9.refs_4_ = bf16[4,512,128]{2,1,0:T(8,128)(2,1)S(1)} collective-permute-done((bf16[4,512,128]{2,1,0:T(8,128)(2,1)S(1)}, bf16[4,512,128]{2,1,0:T(8,128)(2,1)S(1)}, u32[]{:S(2)}, u32[]{:S(2)}) %collective-permute-start.9) | collective-permute-done | bytes 524320 | tf_op jit(solution)/shard_map/ppermute | solution.py:28
  159.6 2.1 %last.1 = bf16[512,512]{1,0:T(8,128)(2,1)} custom-call(s32[1]{0:T(128)} %bitcast.9.place, f32[528,512]{1,0:T(8,128)S(1)} %get-tuple-element.48.refs_0_, f32[512,128]{1,0:T(8,128)S(1)} %get-tuple-element.45.refs_3_.refs_1_, f32[512,128]{1,0:T(8,128)S(1)} %get-tuple-element.49.refs_2_, f32[512,128]{1,0:T(8,128)S(1)} %get-tuple-element.50.refs_3_, ...), custom_call_target="tpu_custom_call" | custom-call | flops 268435456 | bytes 4194304 | tf_op jit(solution)/shard_map/last/pallas_call | solution.py:363
  (22 shorter events, 0.2 us)
Async XLA Ops:
  7.2 23.5 %copy-start.1 = (bf16[7,7,128]{2,1,0:T(8,128)(2,1)S(1)}, bf16[7,7,128]{2,1,0:T(8,128)(2,1)}, u32[]{:S(2)}) copy-start(bf16[7,7,128]{2,1,0:T(8,128)(2,1)} %param.14) | copy-start | bytes 37636
  7.2 23.6 %copy-start.4 = (bf16[128]{0:T(256)(128)(2,1)S(1)}, bf16[128]{0:T(256)(128)(2,1)}, u32[]{:S(2)}) copy-start(bf16[128]{0:T(256)(128)(2,1)} %param.15) | copy-start | bytes 772
  7.2 129.8 %all-gather.2.cloned.1.call-start = ((), (), s32[]{:S(2)}) async-start(), calls=%async_computation | async-start | bytes 4325376 | tf_op jit(solution)/shard_map/all_gather | solution.py:398
  10.3 20.4 %collective-permute-start.1 = (bf16[1408,128]{1,0:T(8,128)(2,1)S(1)}, bf16[1408,128]{1,0:T(8,128)(2,1)S(1)}, u32[]{:S(2)}, u32[]{:S(2)}) collective-permute-start(bf16[1408,128]{1,0:T(8,128)(2,1)S(1)} %get-tuple-element.29), channel_id=1, source_target_pairs={{0,256},{256,512},{512,768},{768,0},{1,257},{257,513},{513,769},{7... | collective-permute-start | bytes 1081352 | tf_op jit(solution)/shard_map/ppermute | solution.py:28
  25.4 13.3 %collective-permute-start.2 = (bf16[1408,128]{1,0:T(8,128)(2,1)S(1)}, bf16[1408,128]{1,0:T(8,128)(2,1)S(1)}, u32[]{:S(2)}, u32[]{:S(2)}) collective-permute-start(bf16[1408,128]{1,0:T(8,128)(2,1)S(1)} %get-tuple-element.30), channel_id=1, source_target_pairs={{0,768},{256,0},{512,256},{768,512},{1,769},{257,1},{513,257},{769... | collective-permute-start | bytes 1081352 | tf_op jit(solution)/shard_map/ppermute | solution.py:28
  27.3 14.6 %collective-permute-start = (bf16[1024,128]{1,0:T(8,128)(2,1)S(1)}, bf16[1024,128]{1,0:T(8,128)(2,1)S(1)}, u32[]{:S(2)}, u32[]{:S(2)}) collective-permute-start(bf16[1024,128]{1,0:T(8,128)(2,1)S(1)} %get-tuple-element.27.kv), channel_id=1, source_target_pairs={{0,512},{256,768},{512,0},{768,256},{1,513},{257,769},{513,1},{769... | collective-permute-start | bytes 786440 | tf_op jit(solution)/shard_map/ppermute | solution.py:28
  41.9 90.4 %copy-start = (bf16[4096]{0:T(1024)(128)(2,1)S(1)}, bf16[4096]{0:T(1024)(128)(2,1)}, u32[]{:S(2)}) copy-start(bf16[4096]{0:T(1024)(128)(2,1)} %param.16) | copy-start | bytes 24580
  41.9 90.4 %copy-start.2 = (bf16[4096]{0:T(1024)(128)(2,1)S(1)}, bf16[4096]{0:T(1024)(128)(2,1)}, u32[]{:S(2)}) copy-start(bf16[4096]{0:T(1024)(128)(2,1)} %param.17) | copy-start | bytes 24580
  97.6 15.1 %collective-permute-start.3 = (bf16[4,512,128]{2,1,0:T(8,128)(2,1)S(1)}, bf16[4,512,128]{2,1,0:T(8,128)(2,1)S(1)}, u32[]{:S(2)}, u32[]{:S(2)}) collective-permute-start(bf16[4,512,128]{2,1,0:T(8,128)(2,1)S(1)} %bitcast.20), channel_id=1, source_target_pairs={{0,1},{1,2},{2,3},{3,4},{4,5},{5,6},{6,7},{7,8},{8,9},{9,10},{10,1... | collective-permute-start | bytes 1572872 | tf_op jit(solution)/shard_map/ppermute | solution.py:28
  102.7 14.5 %collective-permute-start.6 = (bf16[4,512,128]{2,1,0:T(8,128)(2,1)S(1)}, bf16[4,512,128]{2,1,0:T(8,128)(2,1)S(1)}, u32[]{:S(2)}, u32[]{:S(2)}) collective-permute-start(bf16[4,512,128]{2,1,0:T(8,128)(2,1)S(1)} %bitcast.21), channel_id=1, source_target_pairs={{0,31},{1,0},{2,1},{3,2},{4,3},{5,4},{6,5},{7,6},{8,7},{9,8},{10,9... | collective-permute-start | bytes 1572872 | tf_op jit(solution)/shard_map/ppermute | solution.py:28
  112.7 16.0 %collective-permute-start.4 = (bf16[4,512,128]{2,1,0:T(8,128)(2,1)S(1)}, bf16[4,512,128]{2,1,0:T(8,128)(2,1)}, u32[]{:S(2)}, u32[]{:S(2)}) collective-permute-start(bf16[4,512,128]{2,1,0:T(8,128)(2,1)S(1)} %collective-permute-done.3.refs_1_), channel_id=1, source_target_pairs={{0,1},{1,2},{2,3},{3,4},{4,5},{5,6},{6,7},{7,8},{8,9},{9,10},{10,1... | collective-permute-start | bytes 1572872 | tf_op jit(solution)/shard_map/ppermute | solution.py:28
  117.2 15.2 %collective-permute-start.7 = (bf16[4,512,128]{2,1,0:T(8,128)(2,1)S(1)}, bf16[4,512,128]{2,1,0:T(8,128)(2,1)S(1)}, u32[]{:S(2)}, u32[]{:S(2)}) collective-permute-start(bf16[4,512,128]{2,1,0:T(8,128)(2,1)S(1)} %collective-permute-done.6.refs_2_), channel_id=1, source_target_pairs={{0,31},{1,0},{2,1},{3,2},{4,3},{5,4},{6,5},{7,6},{8,7},{9,8},{10,9... | collective-permute-start | bytes 1572872 | tf_op jit(solution)/shard_map/ppermute | solution.py:28
  128.6 18.7 %collective-permute-start.5 = (bf16[4,512,128]{2,1,0:T(8,128)(2,1)}, bf16[4,512,128]{2,1,0:T(8,128)(2,1)S(1)}, u32[]{:S(2)}, u32[]{:S(2)}) collective-permute-start(bf16[4,512,128]{2,1,0:T(8,128)(2,1)} %collective-permute-done.4.refs_3_), channel_id=1, source_target_pairs={{0,1},{1,2},{2,3},{3,4},{4,5},{5,6},{6,7},{7,8},{8,9},{9,10},{10,1... | collective-permute-start | bytes 1572872 | tf_op jit(solution)/shard_map/ppermute | solution.py:28
  132.4 16.8 %collective-permute-start.8 = (bf16[4,512,128]{2,1,0:T(8,128)(2,1)S(1)}, bf16[4,512,128]{2,1,0:T(8,128)(2,1)S(1)}, u32[]{:S(2)}, u32[]{:S(2)}) collective-permute-start(bf16[4,512,128]{2,1,0:T(8,128)(2,1)S(1)} %collective-permute-done.7.refs_4_), channel_id=1, source_target_pairs={{0,31},{1,0},{2,1},{3,2},{4,3},{5,4},{6,5},{7,6},{8,7},{9,8},{10,9... | collective-permute-start | bytes 1572872 | tf_op jit(solution)/shard_map/ppermute | solution.py:28
  137.0 12.3 %copy-start.3 = (bf16[512]{0:T(512)(128)(2,1)S(1)}, bf16[512]{0:T(512)(128)(2,1)}, u32[]{:S(2)}) copy-start(bf16[512]{0:T(512)(128)(2,1)} %param.19) | copy-start | bytes 3076
  147.3 12.3 %collective-permute-start.9 = (bf16[4,512,128]{2,1,0:T(8,128)(2,1)S(1)}, bf16[4,512,128]{2,1,0:T(8,128)(2,1)S(1)}, u32[]{:S(2)}, u32[]{:S(2)}) collective-permute-start(bf16[4,512,128]{2,1,0:T(8,128)(2,1)S(1)} %collective-permute-done.5.refs_0_), channel_id=1, source_target_pairs={{0,1},{1,2},{2,3},{3,4},{4,5},{5,6},{6,7},{7,8},{8,9},{9,10},{10,1... | collective-permute-start | bytes 1572872 | tf_op jit(solution)/shard_map/ppermute | solution.py:28
Sparse Core Ops, SparseCore 0:
  12.9 89.0 all-gather.1
